TPU v7x, 128 devices: a whole 4x4x4 slice. The times are simulated.
128 devices in a mesh: lat: 16 (over x, z_lo, core), lon: 8 (over z_hi, y).
Axes of the slice: x: 4, y: 4, z: 4 (z_hi: 2, z_lo: 2; z = z_hi * 2 + z_lo), core: 2. Of those that a mesh axis runs over, the one named last changes fastest.
Arguments:
- x_tiles: bfloat16 [8, 64, 77, 256], P('lon', 'lat'), may hold values from -6 to 6
- tile_pos: int32 [8, 64], P('lon', 'lat'), may hold values from 0 to 511, as said below
- valid_rows: int32 [8, 64], P('lon', 'lat'), may hold values from 1 to 16
- stem_w: bfloat16 [77, 200], replicated, may hold values from -0.625 to 0.625
- dw_kernel: float32 [200, 49], replicated, may hold values from -0.875 to 0.875
- norm_gain: float32 [200], replicated, may hold values from 0.1 to 1.9
- w_in: bfloat16 [200, 800], replicated, may hold values from -0.4375 to 0.4375
- w_out: bfloat16 [800, 200], replicated, may hold values from -0.21875 to 0.21875
- cotangent: bfloat16 [8, 64, 200, 256], P('lon', 'lat'), may hold values from -3072 to 3072
Outputs:
- out_tiles: bfloat16 [8, 64, 200, 256], P('lon', 'lat')
- grad_w_in: float32 [200, 800], replicated
- grad_w_out: float32 [800, 200], replicated
- grad_kernel: float32 [200, 49], replicated
- grad_gain: float32 [200], replicated
Inputs may be any that keep to these rules, and one draw needn't show every extreme that they name: `tile_pos`: in each sector the places are distinct; in the order of place, the r-th active tile of a sector is held by lat index r % 16. At most 2 tiles of one device lie in one band block of 32 tiles, and this is reached; some band block is fully active in every sector.
All inputs are finite; a program needn't handle non-finite values.
Results may differ from a plain program's by a relative error of at most 0.0075.
Values may be sent and summed in bfloat16 or wider, within the bound.
No kernel may reach another device: no remote copies, remote signals or barrier semaphores. Data moves between devices by JAX's collectives and lax.ppermute only.
A program may use at most 128 MiB of HBM per device.

v0:
```python
import jax
import jax.numpy as jnp
import numpy as np
from jax import lax
from jax.experimental import pallas as pl
from jax.experimental.pallas import tpu as pltpu
from jax.sharding import PartitionSpec as P

C = 200
CIN = 77
HID = 800
KW = 7
TS = 16
TT = 256
A_DEV = 4
COLS = 8
TILE_ROWS = 64
HALF = 128
KPAD = 80
PIECE = 48
SHELL = 4 * PIECE
EDGE = A_DEV * PIECE
PAY = A_DEV * SHELL + 2 * EDGE
GROUP = 8
PITCH = 24
PROWS = TS + KW - 1
HB = 7
CHUNKS = 64
F32 = jnp.float32
BF16 = jnp.bfloat16
TN = (((0,), (0,)), ((), ()))
NT = (((1,), (1,)), ((), ()))
DIRS = [(dr, dc) for dr in (-1, 0, 1) for dc in (-1, 0, 1) if (dr, dc) != (0, 0)]


def shell_cells():
    m = np.arange(PIECE)
    left = (m // 3) * TS + m % 3
    pieces = np.concatenate([m, 13 * TS + m, left, left + 13, np.full(256 - SHELL, -1)])
    return pieces.reshape(1, 256).astype(np.int32)


def shell_kernel(pos_ref, rows_ref, x_ref, map_ref, shell_ref, east_ref, west_ref, kept_ref, flat, cut, buf):
    for k in range(CIN):
        for h in range(2):
            flat[h, A_DEV * k : A_DEV * k + A_DEV, :] = x_ref[k, :, h * HALF : (h + 1) * HALF].astype(F32)
    row = lax.broadcasted_iota(jnp.int32, (A_DEV * CIN, 1), 0) % A_DEV
    limit = jnp.full((A_DEV * CIN, 1), rows_ref[0, 0], jnp.int32)
    for a in range(1, A_DEV):
        limit = jnp.where(row == a, rows_ref[0, a], limit)
    cell_row = lax.broadcasted_iota(jnp.int32, (1, TT), 1) // TS
    for h in range(2):
        flat[h] = jnp.where(cell_row[:, h * HALF : (h + 1) * HALF] < limit, flat[h], 0.0)
    cell_id = lax.broadcasted_iota(jnp.int32, (TT, 256), 0)
    pick = (cell_id == map_ref[...]).astype(F32).astype(BF16)
    pieces = jnp.dot(flat[0].astype(BF16), pick[0:HALF], preferred_element_type=F32)
    pieces = pieces + jnp.dot(flat[1].astype(BF16), pick[HALF:TT], preferred_element_type=F32)
    cut[0] = pieces[:, 0:HALF]
    cut[1] = pieces[:, HALF:256]
    fill = lax.broadcasted_iota(jnp.int32, (3, 1), 0)
    buf[:, 768:1536] = jnp.zeros((KPAD, 768), F32)
    kept_ref[...] = jnp.zeros_like(kept_ref)
    for a in range(A_DEV):
        for h in range(2):
            kept_ref[a, 0:CIN, h * HALF : (h + 1) * HALF] = flat[h, pl.ds(a, CIN, stride=A_DEV), :].astype(BF16)
        v0 = cut[0, pl.ds(a, CIN, stride=A_DEV), :]
        v1 = cut[1, pl.ds(a, CIN, stride=A_DEV), :]
        place = pos_ref[0, a]
        tail = jnp.where(fill == 0, place // 16, jnp.where(fill == 1, place % 16, 0)).astype(F32)
        at = a * SHELL
        buf[0:CIN, at : at + HALF] = v0
        buf[0:CIN, at + HALF : at + SHELL] = v1[:, 0 : SHELL - HALF]
        buf[CIN:KPAD, at : at + SHELL] = jnp.broadcast_to(tail, (3, SHELL))
        east = 768 + a * PIECE
        west = 1152 + EDGE + a * PIECE
        buf[0:CIN, east : east + PIECE] = v1[:, 16:64]
        buf[CIN:KPAD, east : east + PIECE] = jnp.broadcast_to(tail, (3, PIECE))
        buf[0:CIN, west : west + 32] = v0[:, 96:HALF]
        buf[0:CIN, west + 32 : west + PIECE] = v1[:, 0:16]
        buf[CIN:KPAD, west : west + PIECE] = jnp.broadcast_to(tail, (3, PIECE))
    shell_ref[...] = buf[:, 0:768].astype(BF16)
    east_ref[...] = buf[:, 768:1152].astype(BF16)
    west_ref[...] = buf[:, 1152:1536].astype(BF16)


def gelu_parts(v):
    k = 0.7978845608028654
    sq = v * v
    u = 0.5 * jnp.tanh(v * (k + (k * 0.044715) * sq)) + 0.5
    value = v * u
    slope = u + (value - value * u) * (2.0 * k + (6.0 * k * 0.044715) * sq)
    return value, slope


def main_kernel(
    pos_ref, rows_ref, core_ref, ga_ref, gb_ref, x_ref, sw_ref, dw_ref, gain_ref, wi_ref, wo_ref, cot_ref,
    out_ref, own_ref, send_ref,
    swp, dwt, gnp, wide, wit, wot, pm, tv, sm, ts, sem, lp, st, pt, cv, un, iv, ft, mg, hs, gps, gf, gc, si, so,
):
    swp[...] = jnp.zeros_like(swp)
    swp[0:CIN, 0:C] = sw_ref[...]
    dwt[1] = jnp.zeros((56, HALF), F32)
    dwt[0, 0 : KW * KW, :] = dw_ref[:, 0:HALF]
    dwt[1, 0 : KW * KW, 0 : C - HALF] = dw_ref[:, HALF:C]
    gnp[...] = jnp.zeros_like(gnp)
    gnp[:, 0:C] = gain_ref[...]
    gain0 = gnp[:, 0:HALF]
    gain1 = gnp[:, HALF:256]

    for g in range(GROUP):
        for j, ref in enumerate((ga_ref, gb_ref)):
            tail = ref[g, 64:KPAD, :].astype(F32)
            pm[2 * g + j : 2 * g + j + 1, :] = tail[13:14, :] * 16.0 + tail[14:15, :]
    lane = lax.broadcasted_iota(jnp.int32, (16, PAY), 1)
    slot = lax.broadcasted_iota(jnp.int32, (16, PAY), 0)
    kind = jnp.where(lane < 768, 0, jnp.where(lane < 768 + EDGE, 1, 2))
    first = jnp.where(lane < 768, lane % SHELL, (lane - 768) % PIECE) == 0
    label = jnp.where(first, pm[...] + 1000.0 * kind.astype(F32), -1.0)
    code = (slot * PAY + lane + 1).astype(F32)
    for a in range(A_DEV):
        q = pos_ref[0, a]
        row, col = q // COLS, q % COLS
        for n, (dr, dc) in enumerate(DIRS):
            nrow, ncol = row + dr, col + dc
            inside = (nrow >= 0) & (nrow < TILE_ROWS)
            side = jnp.where(ncol < 0, 1000, jnp.where(ncol >= COLS, 2000, 0))
            want = jnp.where(inside, nrow * COLS + (ncol + COLS) % COLS + side, -7)
            hit = jnp.where(label == want.astype(F32), code, 0.0)
            acc = jnp.sum(hit, axis=0, keepdims=True)
            folded = acc[:, 0:HALF]
            for i in range(1, PAY // HALF):
                folded = folded + acc[:, i * HALF : (i + 1) * HALF]
            tv[a * 8 + n : a * 8 + n + 1, :] = folded
    total = jnp.sum(tv[...], axis=1, keepdims=True)
    sm[...] = jnp.broadcast_to(total, (32, HALF)).astype(jnp.int32)
    tcopy = pltpu.make_async_copy(sm, ts, sem)
    tcopy.start()

    for a in range(A_DEV):
        rows = lax.dot_general(x_ref[a], swp[...], TN, preferred_element_type=F32)
        rows = rows.astype(BF16).astype(F32)
        for h in range(2):
            for y in range(TS):
                at = (a * PROWS + 3 + y) * PITCH + 3
                pt[h, at : at + TS, :] = rows[y * TS : (y + 1) * TS, h * HALF : (h + 1) * HALF]
    cell_row = lax.broadcasted_iota(jnp.int32, (1, TT), 1) // TS
    mg[...] = jnp.zeros_like(mg)
    for a in range(A_DEV):
        keep = cell_row < rows_ref[0, a]
        mg[0:C, a * TT : (a + 1) * TT] = jnp.where(keep, cot_ref[a].astype(F32), 0.0).astype(BF16)
    wide[C:256, :] = jnp.zeros((256 - C, HB * HALF), F32)
    wide[:, 768:896] = jnp.zeros((256, HALF), F32)
    for src, dst in ((wi_ref, wit), (wo_ref, wot)):
        wide[0:C, 0:HID] = src[...].astype(F32)
        for b in range(HB):
            dst[b * HALF : (b + 1) * HALF, :] = wide[:, b * HALF : (b + 1) * HALF].T.astype(BF16)
    tcopy.wait()

    gap = lax.broadcasted_iota(jnp.int32, (PIECE, 256), 1) - lax.broadcasted_iota(jnp.int32, (PIECE, 256), 0)
    for a in range(A_DEV):
        col = pos_ref[0, a] % COLS
        for n, (dr, dc) in enumerate(DIRS):
            got = ts[a * 8 + n, 0]
            if dc == 0:
                offset = 48 if dr < 0 else 0
            elif dc < 0:
                offset = jnp.where(col == 0, 0, 144)
            else:
                offset = jnp.where(col == COLS - 1, 0, 96)
            spot = jnp.maximum(got - 1, 0)
            source = spot // PAY
            at = spot - source * PAY + offset
            block = jnp.minimum(at // HALF, PAY // HALF - 2)
            shift = jnp.where(got == 0, -1000, at - block * HALF)
            cells = pl.ds(pl.multiple_of(block * HALF, HALF), 256)
            near = ga_ref[source // 2, :, cells]
            far = gb_ref[source // 2, :, cells]
            window = jnp.where(source % 2 == 0, near, far)
            pick = (gap == shift).astype(F32).astype(BF16)
            piece = lax.dot_general(pick, window, NT, preferred_element_type=F32)
            spot = (a * 8 + n) * PIECE
            lp[spot : spot + PIECE, 0:KPAD] = piece.astype(BF16)
    for a in range(A_DEV):
        span = slice(a * 8 * PIECE, (a + 1) * 8 * PIECE)
        rows = jnp.dot(lp[span, 0:KPAD], swp[...], preferred_element_type=F32)
        rows = rows.astype(BF16).astype(F32)
        st[0, span, :] = rows[:, 0:HALF]
        st[1, span, :] = rows[:, HALF:256]
    for a in range(A_DEV):
        base = {where: (a * 8 + n) * PIECE for n, where in enumerate(DIRS)}
        for h in range(2):
            for i in range(3):
                at = (a * PROWS + i) * PITCH
                low = at + 19 * PITCH
                up, down = base[-1, 0] + i * TS, base[1, 0] + i * TS
                pt[h, at + 3 : at + 3 + TS, :] = st[h, up : up + TS, :]
                pt[h, low + 3 : low + 3 + TS, :] = st[h, down : down + TS, :]
                for dc, xx in ((-1, 0), (1, 19)):
                    up, down = base[-1, dc] + 39 + 3 * i, base[1, dc] + 3 * i
                    pt[h, at + xx : at + xx + 3, :] = st[h, up : up + 3, :]
                    pt[h, low + xx : low + xx + 3, :] = st[h, down : down + 3, :]
            for y in range(TS):
                at = (a * PROWS + 3 + y) * PITCH
                for dc, xx in ((-1, 0), (1, 19)):
                    side = base[0, dc] + 3 * y
                    pt[h, at + xx : at + xx + 3, :] = st[h, side : side + 3, :]

    def conv_step(step, carry):
        h = step // (2 * A_DEV)
        part = step % (2 * A_DEV)
        at = pl.multiple_of((part // 2) * (PROWS * PITCH) + (part % 2) * (8 * PITCH), 8)
        acc = [jnp.zeros((TS, HALF), F32) for _ in range(8)]
        for r in range(KW):
            for k in range(KW):
                w = jnp.broadcast_to(dwt[h, r * KW + k : r * KW + k + 1, :], (TS, HALF))
                for y in range(8):
                    acc[y] = acc[y] + w * pt[h, pl.ds(at + (y + r) * PITCH + k, TS), :]
        for y in range(8):
            cv[h, pl.ds(pl.multiple_of(part * HALF, 8) + y * TS, TS), :] = acc[y]
        return carry

    lax.fori_loop(0, 4 * A_DEV, conv_step, 0)

    live = lax.broadcasted_iota(jnp.int32, (1, HALF), 1) < C - HALF
    for a in range(A_DEV):
        span = slice(a * TT, (a + 1) * TT)
        c0 = cv[0, span, :]
        c1 = cv[1, span, :]
        mean = jnp.sum(c0 + c1, axis=1, keepdims=True) * (1.0 / C)
        c0 = c0 - mean
        c1 = jnp.where(live, c1 - mean, 0.0)
        inv = lax.rsqrt(jnp.sum(c0 * c0 + c1 * c1, axis=1, keepdims=True) * (1.0 / C) + 1e-6)
        u0 = c0 * inv
        u1 = c1 * inv
        cv[0, span, :] = u0
        cv[1, span, :] = u1
        iv[span, :] = jnp.broadcast_to(inv, (TT, HALF))
        ft[0:HALF, span] = (u0 * gain0).T.astype(BF16)
        ft[HALF:256, span] = (u1 * gain1).T.astype(BF16)

    for b in range(HID // 80):
        span = slice(b * 80, (b + 1) * 80)
        preact = jnp.dot(wit[span, :], ft[...], preferred_element_type=F32)
        grad_hidden = jnp.dot(wot[span, :], mg[...], preferred_element_type=F32)
        value, slope = gelu_parts(preact)
        hs[span, :] = value.astype(BF16)
        gps[span, :] = (grad_hidden * slope).astype(BF16)
    gf[C:256, :] = jnp.zeros((256 - C, TT), F32)
    sums = [jnp.zeros((1, HALF), F32), jnp.zeros((1, HALF), F32)]
    for a in range(A_DEV):
        span = slice(a * TT, (a + 1) * TT)
        gf[0:C, :] = jnp.dot(wi_ref[...], gps[:, span], preferred_element_type=F32)
        g0 = gf[0:HALF, :].T.astype(BF16).astype(F32)
        g1 = gf[HALF:256, :].T.astype(BF16).astype(F32)
        u0 = cv[0, span, :]
        u1 = cv[1, span, :]
        inv = iv[span, :]
        sums[0] = sums[0] + jnp.sum(g0 * u0, axis=0, keepdims=True)
        sums[1] = sums[1] + jnp.sum(g1 * u1, axis=0, keepdims=True)
        d0 = g0 * gain0
        d1 = g1 * gain1
        m1 = jnp.sum(d0 + d1, axis=1, keepdims=True) * (1.0 / C)
        m2 = jnp.sum(d0 * u0 + d1 * u1, axis=1, keepdims=True) * (1.0 / C)
        gc[0, span, :] = inv * (d0 - m1 - u0 * m2)
        gc[1, span, :] = jnp.where(live, inv * (d1 - m1 - u1 * m2), 0.0)
        stem = lax.dot_general(swp[...], x_ref[a], TN, preferred_element_type=F32)[0:C, :].astype(BF16).astype(F32)
        branch = jnp.dot(wo_ref[...], hs[:, span], preferred_element_type=F32)
        keep = cell_row < rows_ref[0, a]
        out_ref[a] = jnp.where(keep, branch + stem, 0.0).astype(BF16)
    si[:, 768:896] = jnp.zeros((C, HALF), F32)
    so[:, 768:896] = jnp.zeros((C, HALF), F32)
    si[:, 0:HID] = lax.dot_general(ft[0:C, :], gps[...], NT, preferred_element_type=F32)
    so[:, 0:HID] = lax.dot_general(mg[0:C, :], hs[...], NT, preferred_element_type=F32)

    un[0, 48:56, :] = jnp.zeros((8, HALF), F32)
    un[1, 48:56, :] = jnp.zeros((8, HALF), F32)

    def tap_step(step, carry):
        h = step % 2
        r = step // 2
        down = pl.multiple_of(r * PITCH, 8)
        acc = [jnp.zeros((TS, HALF), F32) for _ in range(KW)]
        for a in range(A_DEV):
            for y in range(TS):
                g = gc[h, a * TT + y * TS : a * TT + (y + 1) * TS, :]
                for k in range(KW):
                    acc[k] = acc[k] + g * pt[h, pl.ds(down + (a * PROWS + y) * PITCH + k, TS), :]
        for k in range(KW):
            un[h, pl.ds(r * KW + k, 1), :] = jnp.sum(acc[k], axis=0, keepdims=True)
        return carry

    lax.fori_loop(0, 2 * KW, tap_step, 0)
    un[0, 49:50, :] = sums[0]
    un[1, 49:50, :] = sums[1]

    is_low = core_ref[0, 0] == 0
    blank = jnp.zeros((8, HALF), F32)
    count = ((rows_ref[0, 0] + rows_ref[0, 1] + rows_ref[0, 2] + rows_ref[0, 3]) * TS).astype(F32)

    def blocks(t):
        if t < 25 * HB:
            r, b = t // HB, t % HB
            return si[8 * r : 8 * r + 8, b * HALF : (b + 1) * HALF], so[8 * r : 8 * r + 8, b * HALF : (b + 1) * HALF]
        t = t - 25 * HB
        if t < 14:
            return un[t // HB, 8 * (t % HB) : 8 * (t % HB) + 8, :], blank
        if t == 14:
            return jnp.where(lax.broadcasted_iota(jnp.int32, (8, HALF), 1) == core_ref[0, 1], count, blank), blank
        return blank, blank

    for chunk in range(CHUNKS):
        pairs = [blocks(3 * chunk + i) for i in range(3)]
        for i, (low, high) in enumerate(pairs):
            own_ref[chunk, 8 * i : 8 * i + 8, :] = jnp.where(is_low, low, high)
        sent = jnp.concatenate([jnp.where(is_low, high, low) for low, high in pairs], axis=0)
        send_ref[chunk] = sent.astype(BF16)


def final_kernel(core_ref, own_ref, other_ref, win_ref, wout_ref, ker_ref, gain_ref, ks):
    is_low = core_ref[0, 0] == 0

    def pair(chunk):
        own = own_ref[chunk].astype(F32)
        other = other_ref[chunk].astype(F32)
        return jnp.where(is_low, own, other), jnp.where(is_low, other, own)

    scale = 1.0 / jnp.sum(pair(CHUNKS - 1)[0][0:1, :], axis=1, keepdims=True)
    for chunk in range(CHUNKS - 1):
        low, high = pair(chunk)
        for i in range(3):
            t = 3 * chunk + i
            block = low[8 * i : 8 * i + 8, :] * scale
            if t < 25 * HB:
                r, b = t // HB, t % HB
                wide = HALF if b < HB - 1 else HID - (HB - 1) * HALF
                win_ref[8 * r : 8 * r + 8, b * HALF : b * HALF + wide] = block[:, 0:wide]
                turned = high[8 * i : 8 * i + 8, :] * scale
                wout_ref[8 * r : 8 * r + 8, b * HALF : b * HALF + wide] = turned[:, 0:wide]
            else:
                t = t - 25 * HB
                ks[8 * (t % HB) : 8 * (t % HB) + 8, (t // HB) * HALF : (t // HB + 1) * HALF] = block
    ker_ref[...] = ks[0 : KW * KW, 0:C]
    gain_ref[...] = ks[49:50, 0:C]


def on_chip(value):
    return pltpu.with_memory_space_constraint(value, pltpu.VMEM)


def body(x_tiles, tile_pos, valid_rows, stem_w, dw_kernel, norm_gain, w_in, w_out, cotangent):
    smem = pl.BlockSpec(memory_space=pltpu.SMEM)
    vmem = pl.BlockSpec(memory_space=pltpu.VMEM)
    lat_id = lax.axis_index("lat")
    core_id = jnp.stack([lat_id & 1, lat_id * lax.axis_size("lon") + lax.axis_index("lon")]).reshape(1, 2)
    shell, east, west, inputs = pl.pallas_call(
        shell_kernel,
        out_shape=(
            jax.ShapeDtypeStruct((KPAD, 768), BF16),
            jax.ShapeDtypeStruct((KPAD, 384), BF16),
            jax.ShapeDtypeStruct((KPAD, 384), BF16),
            jax.ShapeDtypeStruct((A_DEV, KPAD, TT), BF16),
        ),
        in_specs=[smem, smem, vmem, vmem],
        out_specs=(vmem, vmem, vmem, vmem),
        scratch_shapes=[
            pltpu.VMEM((2, A_DEV * CIN, HALF), F32),
            pltpu.VMEM((2, A_DEV * CIN, HALF), F32),
            pltpu.VMEM((KPAD, 1536), F32),
        ],
        name="shell",
    )(tile_pos, valid_rows, x_tiles[0].transpose(1, 0, 2), jnp.asarray(shell_cells()))
    lon = lax.axis_size("lon")
    lat = lax.axis_size("lat")
    from_west = lax.ppermute(east, "lon", [(i, (i + 1) % lon) for i in range(lon)])
    from_east = lax.ppermute(west, "lon", [((i + 1) % lon, i) for i in range(lon)])
    payload = jnp.concatenate([shell, from_west + from_east], axis=1)
    same_core = [[i for i in range(c, lat, 2)] for c in range(2)]
    siblings = [(i, i ^ 1) for i in range(lat)]
    mine = lax.all_to_all(
        jnp.broadcast_to(payload[None], (GROUP, KPAD, PAY)), "lat", 0, 0, axis_index_groups=same_core, tiled=True
    )
    theirs = lax.ppermute(mine, "lat", siblings)

    cells = A_DEV * TT
    out_tiles, own, send = pl.pallas_call(
        main_kernel,
        out_shape=(
            jax.ShapeDtypeStruct((A_DEV, C, TT), BF16),
            jax.ShapeDtypeStruct((CHUNKS, 24, HALF), F32),
            jax.ShapeDtypeStruct((CHUNKS, 24, HALF), BF16),
        ),
        in_specs=[smem] * 3 + [vmem] * 9,
        out_specs=(vmem, vmem, vmem),
        scratch_shapes=[
            pltpu.VMEM((KPAD, 256), BF16),
            pltpu.VMEM((2, 56, HALF), F32),
            pltpu.VMEM((1, 256), F32),
            pltpu.VMEM((256, HB * HALF), F32),
            pltpu.VMEM((HB * HALF, 256), BF16),
            pltpu.VMEM((HB * HALF, 256), BF16),
            pltpu.VMEM((16, PAY), F32),
            pltpu.VMEM((32, HALF), F32),
            pltpu.VMEM((32, HALF), jnp.int32),
            pltpu.SMEM((32, HALF), jnp.int32),
            pltpu.SemaphoreType.DMA,
            pltpu.VMEM((32 * PIECE, HALF), BF16),
            pltpu.VMEM((2, 32 * PIECE, HALF), F32),
            pltpu.VMEM((2, A_DEV * PROWS * PITCH, HALF), F32),
            pltpu.VMEM((2, cells, HALF), F32),
            pltpu.VMEM((2, 56, HALF), F32),
            pltpu.VMEM((cells, HALF), F32),
            pltpu.VMEM((256, cells), BF16),
            pltpu.VMEM((256, cells), BF16),
            pltpu.VMEM((HID, cells), BF16),
            pltpu.VMEM((HID, cells), BF16),
            pltpu.VMEM((256, TT), F32),
            pltpu.VMEM((2, cells, HALF), F32),
            pltpu.VMEM((C, HB * HALF), F32),
            pltpu.VMEM((C, HB * HALF), F32),
        ],
        name="block",
    )(tile_pos, valid_rows, core_id, on_chip(mine), on_chip(theirs), inputs, stem_w, dw_kernel.T, norm_gain.reshape(1, C), w_in, w_out.T, cotangent[0])

    arrived = lax.ppermute(send, "lat", siblings)
    chip_sum = (own + arrived.astype(F32)).astype(BF16)
    every = [[i * lon + j for i in range(c, lat, 2) for j in range(lon)] for c in range(2)]
    part = lax.all_to_all(chip_sum, ("lat", "lon"), 0, 0, axis_index_groups=every, tiled=True)
    part = jnp.sum(part.astype(F32), axis=0)
    whole = part.astype(BF16)
    spread = jnp.broadcast_to(whole[None], (CHUNKS, 24, HALF))
    spread = lax.all_to_all(spread, ("lat", "lon"), 0, 0, axis_index_groups=every, tiled=True)
    other = lax.ppermute(spread, "lat", siblings)
    win, wout, ker, gain = pl.pallas_call(
        final_kernel,
        out_shape=(
            jax.ShapeDtypeStruct((C, HID), F32),
            jax.ShapeDtypeStruct((C, HID), F32),
            jax.ShapeDtypeStruct((KW * KW, C), F32),
            jax.ShapeDtypeStruct((1, C), F32),
        ),
        in_specs=[smem, vmem, vmem],
        out_specs=(vmem, vmem, vmem, vmem),
        scratch_shapes=[pltpu.VMEM((56, 256), F32)],
        name="finish",
    )(core_id, on_chip(spread), on_chip(other))
    return out_tiles[None], win, wout.T, ker.T, gain.reshape(C)


def solution(mesh):
    tiles = P("lon", "lat", None, None)
    in_specs = (tiles, P("lon", "lat"), P("lon", "lat"), P(), P(), P(), P(), P(), tiles)
    out_specs = (tiles, P(), P(), P(), P())
    return jax.shard_map(body, mesh=mesh, in_specs=in_specs, out_specs=out_specs, check_vma=False)
```

profile of v0, /device:TPU:1, one launch (start us, length us, event | category | flops | bytes accessed | tf_op | source)
XLA Modules:
  0.0 105.2 jit_solution(1260726542587083704)
XLA Ops:
  0.6 2.2 %shell.1 = (bf16[80,768]{1,0:T(8,128)(2,1)}, bf16[80,384]{1,0:T(8,128)(2,1)}, bf16[80,384]{1,0:T(8,128)(2,1)}, bf16[4,80,256]{2,1,0:T(8,128)(2,1)}) custom-call(s32[1,4]{1,0:T(1,128)} %pos_ref.3, s32[1,4]{1,0:T(1,128)} %rows_ref.3, bf16[77,4,256]{2,1,0:T(4,128)(2,1)} %bitcast.17, s32[1,256]{1,0:T(1,128)} %constant.18.clone.map_ref), custom_call_target="tpu_custom_call" | custom-call | tf_op jit(solution)/shard_map/shell/pallas_call | solution.py:355
  2.8 2.1 %collective-permute-start = (bf16[80,384]{1,0:T(8,128)(2,1)}, bf16[80,384]{1,0:T(8,128)(2,1)S(1)}, u32[]{:S(2)}, u32[]{:S(2)}) collective-permute-start(bf16[80,384]{1,0:T(8,128)(2,1)} %get-tuple-element.17), channel_id=1, source_target_pairs={{0,1},{1,2},{2,3},{3,4},{4,5},{5,6},{6,7},{7,0},{8,9},{9,10},{10,1... | collective-permute-start | bytes 184328 | tf_op jit(solution)/shard_map/ppermute | solution.py:374
  4.9 4.8 %collective-permute-start.1 = (bf16[80,384]{1,0:T(8,128)(2,1)}, bf16[80,384]{1,0:T(8,128)(2,1)S(1)}, u32[]{:S(2)}, u32[]{:S(2)}) collective-permute-start(bf16[80,384]{1,0:T(8,128)(2,1)} %get-tuple-element.18), channel_id=1, source_target_pairs={{1,0},{2,1},{3,2},{4,3},{5,4},{6,5},{7,6},{0,7},{9,8},{10,9},{11,1... | collective-permute-start | bytes 184328 | tf_op jit(solution)/shard_map/ppermute | solution.py:375
  9.7 1.8 %collective-permute-done = bf16[80,384]{1,0:T(8,128)(2,1)S(1)} collective-permute-done((bf16[80,384]{1,0:T(8,128)(2,1)}, bf16[80,384]{1,0:T(8,128)(2,1)S(1)}, u32[]{:S(2)}, u32[]{:S(2)}) %collective-permute-start) | collective-permute-done | bytes 61472 | tf_op jit(solution)/shard_map/ppermute | solution.py:374
  11.5 0.0 collective-permute-done.1
  11.5 0.9 pad_maximum_fusion
  12.4 0.1 broadcast_in_dim.6
  12.5 22.0 %all_to_all.15.ga_ref = bf16[8,80,1152]{2,1,0:T(8,128)(2,1)S(1)} all-to-all(bf16[8,80,1152]{2,1,0:T(8,128)(2,1)S(1)} %broadcast_in_dim.6), channel_id=1, replica_groups={{0,16,32,48,64,80,96,112},{8,24,40,56,72,88,104,120},{1,17,33,49,65,81,..., dimensions={0} | all-to-all | bytes 2949120 | tf_op jit(solution)/shard_map/all_to_all | solution.py:379
  34.5 3.3 %collective-permute-start.2 = (bf16[8,80,1152]{2,1,0:T(8,128)(2,1)S(1)}, bf16[8,80,1152]{2,1,0:T(8,128)(2,1)S(1)}, u32[]{:S(2)}, u32[]{:S(2)}) collective-permute-start(bf16[8,80,1152]{2,1,0:T(8,128)(2,1)S(1)} %all_to_all.15.ga_ref), channel_id=1, source_target_pairs={{0,8},{8,0},{16,24},{24,16},{32,40},{40,32},{48,56},{56,48},{64,72... | collective-permute-start | bytes 4423688 | tf_op jit(solution)/shard_map/ppermute | solution.py:382
  37.8 0.6 add_bitcast_fusion.core_ref
  38.4 2.3 %collective-permute-done.2.gb_ref = bf16[8,80,1152]{2,1,0:T(8,128)(2,1)S(1)} collective-permute-done((bf16[8,80,1152]{2,1,0:T(8,128)(2,1)S(1)}, bf16[8,80,1152]{2,1,0:T(8,128)(2,1)S(1)}, u32[]{:S(2)}, u32[]{:S(2)}) %collective-permute-start.2) | collective-permute-done | bytes 1474592 | tf_op jit(solution)/shard_map/ppermute | solution.py:382
  40.7 20.6 %block.1 = (bf16[4,200,256]{2,1,0:T(8,128)(2,1)}, f32[64,24,128]{2,1,0:T(8,128)}, bf16[64,24,128]{2,1,0:T(8,128)(2,1)}) custom-call(s32[1,4]{1,0:T(1,128)} %pos_ref.3, s32[1,4]{1,0:T(1,128)} %rows_ref.3, s32[1,2]{1,0:T(1,128)} %add_bitcast_fusion.core_ref, bf16[8,80,1152]{2,1,0:T(8,128)(2,1)S(1)} %all_to_all.15.ga_ref, ...), custom_call_target="tpu_custom_call" | custom-call | tf_op jit(solution)/shard_map/block/pallas_call | solution.py:385
  61.3 0.5 collective-permute-start.3
  61.7 1.6 %collective-permute-done.3 = bf16[64,24,128]{2,1,0:T(8,128)(2,1)S(1)} collective-permute-done((bf16[64,24,128]{2,1,0:T(8,128)(2,1)}, bf16[64,24,128]{2,1,0:T(8,128)(2,1)S(1)}, u32[]{:S(2)}, u32[]{:S(2)}) %collective-permute-start.3) | collective-permute-done | bytes 393248 | tf_op jit(solution)/shard_map/ppermute | solution.py:424
  63.3 1.2 %add_convert_fusion = bf16[64,24,128]{2,1,0:T(8,128)(2,1)S(1)} fusion(f32[64,24,128]{2,1,0:T(8,128)} %get-tuple-element.21, bf16[64,24,128]{2,1,0:T(8,128)(2,1)S(1)} %collective-permute-done.3), kind=kLoop, calls=%fused_computation | loop fusion | flops 589824 | bytes 1572864 | tf_op jit(solution)/shard_map/convert_element_type | solution.py:425
  64.5 19.5 %all_to_all.16 = bf16[64,24,128]{2,1,0:T(8,128)(2,1)S(1)} all-to-all(bf16[64,24,128]{2,1,0:T(8,128)(2,1)S(1)} %add_convert_fusion), channel_id=1, replica_groups={{0,1,2,3,4,5,6,7,16,17,18,19,20,21,22,23,32,33,34,35,36,37,38,39,48,49,..., dimensions={0} | all-to-all | bytes 786432 | tf_op jit(solution)/shard_map/all_to_all | solution.py:427
  84.0 0.1 reduce_sum.12
  84.1 0.1 broadcast_in_dim.8
  84.2 14.5 %all_to_all.17.own_ref = bf16[64,24,128]{2,1,0:T(8,128)(2,1)S(1)} all-to-all(bf16[64,24,128]{2,1,0:T(8,128)(2,1)S(1)} %broadcast_in_dim.8), channel_id=1, replica_groups={{0,1,2,3,4,5,6,7,16,17,18,19,20,21,22,23,32,33,34,35,36,37,38,39,48,49,..., dimensions={0} | all-to-all | bytes 786432 | tf_op jit(solution)/shard_map/all_to_all | solution.py:431
  98.7 3.2 %collective-permute-start.4 = (bf16[64,24,128]{2,1,0:T(8,128)(2,1)S(1)}, bf16[64,24,128]{2,1,0:T(8,128)(2,1)S(1)}, u32[]{:S(2)}, u32[]{:S(2)}) collective-permute-start(bf16[64,24,128]{2,1,0:T(8,128)(2,1)S(1)} %all_to_all.17.own_ref), channel_id=1, source_target_pairs={{0,8},{8,0},{16,24},{24,16},{32,40},{40,32},{48,56},{56,48},{64,72... | collective-permute-start | bytes 1179656 | tf_op jit(solution)/shard_map/ppermute | solution.py:432
  101.9 1.3 %collective-permute-done.4.other_ref = bf16[64,24,128]{2,1,0:T(8,128)(2,1)S(1)} collective-permute-done((bf16[64,24,128]{2,1,0:T(8,128)(2,1)S(1)}, bf16[64,24,128]{2,1,0:T(8,128)(2,1)S(1)}, u32[]{:S(2)}, u32[]{:S(2)}) %collective-permute-start.4) | collective-permute-done | bytes 393248 | tf_op jit(solution)/shard_map/ppermute | solution.py:432
  103.3 1.9 %finish.1 = (f32[200,800]{1,0:T(8,128)}, f32[200,800]{1,0:T(8,128)}, f32[49,200]{1,0:T(8,128)}, f32[1,200]{1,0:T(1,128)}) custom-call(s32[1,2]{1,0:T(1,128)} %add_bitcast_fusion.core_ref, bf16[64,24,128]{2,1,0:T(8,128)(2,1)S(1)} %all_to_all.17.own_ref, bf16[64,24,128]{2,1,0:T(8,128)(2,1)S(1)} %collective-permute-done.4.other_ref), custom_call_target="tpu_custom_call" | custom-call | tf_op jit(solution)/shard_map/finish/pallas_call | solution.py:433
  (1 shorter events, 0.0 us)
Async XLA Ops:
  2.8 8.7 %collective-permute-start = (bf16[80,384]{1,0:T(8,128)(2,1)}, bf16[80,384]{1,0:T(8,128)(2,1)S(1)}, u32[]{:S(2)}, u32[]{:S(2)}) collective-permute-start(bf16[80,384]{1,0:T(8,128)(2,1)} %get-tuple-element.17), channel_id=1, source_target_pairs={{0,1},{1,2},{2,3},{3,4},{4,5},{5,6},{6,7},{7,0},{8,9},{9,10},{10,1... | collective-permute-start | bytes 184328 | tf_op jit(solution)/shard_map/ppermute | solution.py:374
  4.9 6.6 %collective-permute-start.1 = (bf16[80,384]{1,0:T(8,128)(2,1)}, bf16[80,384]{1,0:T(8,128)(2,1)S(1)}, u32[]{:S(2)}, u32[]{:S(2)}) collective-permute-start(bf16[80,384]{1,0:T(8,128)(2,1)} %get-tuple-element.18), channel_id=1, source_target_pairs={{1,0},{2,1},{3,2},{4,3},{5,4},{6,5},{7,6},{0,7},{9,8},{10,9},{11,1... | collective-permute-start | bytes 184328 | tf_op jit(solution)/shard_map/ppermute | solution.py:375
  34.5 6.2 %collective-permute-start.2 = (bf16[8,80,1152]{2,1,0:T(8,128)(2,1)S(1)}, bf16[8,80,1152]{2,1,0:T(8,128)(2,1)S(1)}, u32[]{:S(2)}, u32[]{:S(2)}) collective-permute-start(bf16[8,80,1152]{2,1,0:T(8,128)(2,1)S(1)} %all_to_all.15.ga_ref), channel_id=1, source_target_pairs={{0,8},{8,0},{16,24},{24,16},{32,40},{40,32},{48,56},{56,48},{64,72... | collective-permute-start | bytes 4423688 | tf_op jit(solution)/shard_map/ppermute | solution.py:382
  61.3 2.0 %collective-permute-start.3 = (bf16[64,24,128]{2,1,0:T(8,128)(2,1)}, bf16[64,24,128]{2,1,0:T(8,128)(2,1)S(1)}, u32[]{:S(2)}, u32[]{:S(2)}) collective-permute-start(bf16[64,24,128]{2,1,0:T(8,128)(2,1)} %get-tuple-element.22), channel_id=1, source_target_pairs={{0,8},{8,0},{16,24},{24,16},{32,40},{40,32},{48,56},{56,48},{64,72... | collective-permute-start | bytes 1179656 | tf_op jit(solution)/shard_map/ppermute | solution.py:424
  98.7 4.6 %collective-permute-start.4 = (bf16[64,24,128]{2,1,0:T(8,128)(2,1)S(1)}, bf16[64,24,128]{2,1,0:T(8,128)(2,1)S(1)}, u32[]{:S(2)}, u32[]{:S(2)}) collective-permute-start(bf16[64,24,128]{2,1,0:T(8,128)(2,1)S(1)} %all_to_all.17.own_ref), channel_id=1, source_target_pairs={{0,8},{8,0},{16,24},{24,16},{32,40},{40,32},{48,56},{56,48},{64,72... | collective-permute-start | bytes 1179656 | tf_op jit(solution)/shard_map/ppermute | solution.py:432
where the time goes:
time: 106 us; the launch traced here: 105 us
  blocking collectives  56 us (53%)
  Pallas kernels  24.6 us (23%)
  starting transfers between devices  13.9 us (13%)
  waiting for transfers between devices  6.98 us (7%)
  other arithmetic  2.81 us (3%)
    all_to_all x1, blocking collectives, body(): lax.all_to_all(jnp.broadcast_to(payload[None], (GROUP, KPAD, PAY)), 'lat'...  22 us
    pallas_call x1, Pallas kernels, body(): pl.pallas_call(main_kernel, out_shape=(jax.ShapeDtypeStruct((A_DEV, C, TT...  20.6 us
    all_to_all x1, blocking collectives, body(): lax.all_to_all(chip_sum, ('lat', 'lon'), 0, 0, axis_index_groups=every, t...  19.5 us
    all_to_all x1, blocking collectives, body(): lax.all_to_all(spread, ('lat', 'lon'), 0, 0, axis_index_groups=every, til...  14.5 us
    ppermute x1, starting transfers between devices, body(): lax.ppermute(west, 'lon', [((i + 1) % lon, i) for i in range(lon)])  4.82 us
    ppermute x1, starting transfers between devices, body(): theirs = lax.ppermute(mine, 'lat', siblings)  3.27 us
    ppermute x1, starting transfers between devices, body(): other = lax.ppermute(spread, 'lat', siblings)  3.25 us
    ppermute x1, waiting for transfers between devices, body(): theirs = lax.ppermute(mine, 'lat', siblings)  2.32 us
  transfers between devices with their start and end apart: 5, of which 4 were waited for; matrix products, arithmetic and copies ran while one was open for 1% of the time, Pallas kernels for 0%

commit v1 on v0

--- a/solution.py
+++ b/solution.py
@@ -93,7 +93,7 @@
 
 
 def main_kernel(
-    pos_ref, rows_ref, core_ref, ga_ref, gb_ref, x_ref, sw_ref, dw_ref, gain_ref, wi_ref, wo_ref, cot_ref,
+    pos_ref, rows_ref, ga_ref, gb_ref, x_ref, sw_ref, dw_ref, gain_ref, wi_ref, wo_ref, cot_ref,
     out_ref, own_ref, send_ref,
     swp, dwt, gnp, wide, wit, wot, pm, tv, sm, ts, sem, lp, st, pt, cv, un, iv, ft, mg, hs, gps, gf, gc, si, so,
 ):
@@ -279,12 +279,16 @@
         h = step % 2
         r = step // 2
         down = pl.multiple_of(r * PITCH, 8)
-        acc = [jnp.zeros((TS, HALF), F32) for _ in range(KW)]
-        for a in range(A_DEV):
+        def tile_step(a, acc):
+            acc = list(acc)
+            at = pl.multiple_of(a * (PROWS * PITCH) + down, 8)
             for y in range(TS):
-                g = gc[h, a * TT + y * TS : a * TT + (y + 1) * TS, :]
+                g = gc[h, pl.ds(pl.multiple_of(a * TT, 8) + y * TS, TS), :]
                 for k in range(KW):
-                    acc[k] = acc[k] + g * pt[h, pl.ds(down + (a * PROWS + y) * PITCH + k, TS), :]
+                    acc[k] = acc[k] + g * pt[h, pl.ds(at + y * PITCH + k, TS), :]
+            return tuple(acc)
+
+        acc = lax.fori_loop(0, A_DEV, tile_step, tuple(jnp.zeros((TS, HALF), F32) for _ in range(KW)))
         for k in range(KW):
             un[h, pl.ds(r * KW + k, 1), :] = jnp.sum(acc[k], axis=0, keepdims=True)
         return carry
@@ -293,7 +297,9 @@
     un[0, 49:50, :] = sums[0]
     un[1, 49:50, :] = sums[1]
 
-    is_low = core_ref[0, 0] == 0
+    lat_id = lax.axis_index("lat")
+    is_low = lat_id % 2 == 0
+    device = lat_id * lax.axis_size("lon") + lax.axis_index("lon")
     blank = jnp.zeros((8, HALF), F32)
     count = ((rows_ref[0, 0] + rows_ref[0, 1] + rows_ref[0, 2] + rows_ref[0, 3]) * TS).astype(F32)
 
@@ -305,7 +311,7 @@
         if t < 14:
             return un[t // HB, 8 * (t % HB) : 8 * (t % HB) + 8, :], blank
         if t == 14:
-            return jnp.where(lax.broadcasted_iota(jnp.int32, (8, HALF), 1) == core_ref[0, 1], count, blank), blank
+            return jnp.where(lax.broadcasted_iota(jnp.int32, (8, HALF), 1) == device, count, blank), blank
         return blank, blank
 
     for chunk in range(CHUNKS):
@@ -316,8 +322,8 @@
         send_ref[chunk] = sent.astype(BF16)
 
 
-def final_kernel(core_ref, own_ref, other_ref, win_ref, wout_ref, ker_ref, gain_ref, ks):
-    is_low = core_ref[0, 0] == 0
+def final_kernel(own_ref, other_ref, win_ref, wout_ref, ker_ref, gain_ref, ks):
+    is_low = lax.axis_index("lat") % 2 == 0
 
     def pair(chunk):
         own = own_ref[chunk].astype(F32)
@@ -350,15 +356,13 @@
 def body(x_tiles, tile_pos, valid_rows, stem_w, dw_kernel, norm_gain, w_in, w_out, cotangent):
     smem = pl.BlockSpec(memory_space=pltpu.SMEM)
     vmem = pl.BlockSpec(memory_space=pltpu.VMEM)
-    lat_id = lax.axis_index("lat")
-    core_id = jnp.stack([lat_id & 1, lat_id * lax.axis_size("lon") + lax.axis_index("lon")]).reshape(1, 2)
     shell, east, west, inputs = pl.pallas_call(
         shell_kernel,
         out_shape=(
-            jax.ShapeDtypeStruct((KPAD, 768), BF16),
-            jax.ShapeDtypeStruct((KPAD, 384), BF16),
-            jax.ShapeDtypeStruct((KPAD, 384), BF16),
-            jax.ShapeDtypeStruct((A_DEV, KPAD, TT), BF16),
+            pltpu.VMEM((KPAD, 768), BF16),
+            pltpu.VMEM((KPAD, 384), BF16),
+            pltpu.VMEM((KPAD, 384), BF16),
+            pltpu.VMEM((A_DEV, KPAD, TT), BF16),
         ),
         in_specs=[smem, smem, vmem, vmem],
         out_specs=(vmem, vmem, vmem, vmem),
@@ -367,6 +371,7 @@
             pltpu.VMEM((2, A_DEV * CIN, HALF), F32),
             pltpu.VMEM((KPAD, 1536), F32),
         ],
+        compiler_params=pltpu.CompilerParams(vmem_limit_bytes=8 << 20),
         name="shell",
     )(tile_pos, valid_rows, x_tiles[0].transpose(1, 0, 2), jnp.asarray(shell_cells()))
     lon = lax.axis_size("lon")
@@ -386,10 +391,10 @@
         main_kernel,
         out_shape=(
             jax.ShapeDtypeStruct((A_DEV, C, TT), BF16),
-            jax.ShapeDtypeStruct((CHUNKS, 24, HALF), F32),
-            jax.ShapeDtypeStruct((CHUNKS, 24, HALF), BF16),
+            pltpu.VMEM((CHUNKS, 24, HALF), F32),
+            pltpu.VMEM((CHUNKS, 24, HALF), BF16),
         ),
-        in_specs=[smem] * 3 + [vmem] * 9,
+        in_specs=[smem] * 2 + [vmem] * 9,
         out_specs=(vmem, vmem, vmem),
         scratch_shapes=[
             pltpu.VMEM((KPAD, 256), BF16),
@@ -418,8 +423,9 @@
             pltpu.VMEM((C, HB * HALF), F32),
             pltpu.VMEM((C, HB * HALF), F32),
         ],
+        compiler_params=pltpu.CompilerParams(vmem_limit_bytes=32 << 20),
         name="block",
-    )(tile_pos, valid_rows, core_id, on_chip(mine), on_chip(theirs), inputs, stem_w, dw_kernel.T, norm_gain.reshape(1, C), w_in, w_out.T, cotangent[0])
+    )(tile_pos, valid_rows, on_chip(mine), on_chip(theirs), inputs, stem_w, dw_kernel.T, norm_gain.reshape(1, C), w_in, w_out.T, cotangent[0])
 
     arrived = lax.ppermute(send, "lat", siblings)
     chip_sum = (own + arrived.astype(F32)).astype(BF16)
@@ -438,11 +444,12 @@
             jax.ShapeDtypeStruct((KW * KW, C), F32),
             jax.ShapeDtypeStruct((1, C), F32),
         ),
-        in_specs=[smem, vmem, vmem],
+        in_specs=[vmem, vmem],
         out_specs=(vmem, vmem, vmem, vmem),
         scratch_shapes=[pltpu.VMEM((56, 256), F32)],
+        compiler_params=pltpu.CompilerParams(vmem_limit_bytes=8 << 20),
         name="finish",
-    )(core_id, on_chip(spread), on_chip(other))
+    )(on_chip(spread), on_chip(other))
     return out_tiles[None], win, wout.T, ker.T, gain.reshape(C)
 
 

time: 106 us -> 101 us (0.953)
  Pallas kernels: 24.6 us -> 19.7 us
  local copies, waits for them, and re-layouts: 0.16 us -> 3.11 us
  other arithmetic: 2.81 us -> 0.22 us
    pallas_call x1, Pallas kernels: 20.6 us -> 17.4 us  [body(): pl.pallas_call(main_kernel, out_shape=(jax.ShapeDtypeStruct((A_DEV, C, TT...]
    unnamed x0 -> x24, local copies, waits for them, and re-layouts: none -> 2.95 us
    convert_element_type x1, other arithmetic: 1.21 us -> 0.1 us  [body(): chip_sum = (own + arrived.astype(F32)).astype(BF16)]
    pallas_call x1, Pallas kernels: 2.15 us -> 1.09 us  [body(): pl.pallas_call(shell_kernel, out_shape=(pltpu.VMEM((KPAD, 768), BF16), pl...]
  transfers between devices with their start and end apart: 5 -> 5, of which waited for: 4 -> 4; matrix products, arithmetic and copies ran while one was open for 1% -> 0% of each run, Pallas kernels for 0% -> 0%
where the time goes in v1:
time: 101 us
  blocking collectives  56.2 us (56%)
  Pallas kernels  19.7 us (20%)
  starting transfers between devices  14 us (14%)
  waiting for transfers between devices  7.13 us (7%)
  local copies, waits for them, and re-layouts  3.11 us (3%)
    all_to_all x1, blocking collectives, body(): lax.all_to_all(jnp.broadcast_to(payload[None], (GROUP, KPAD, PAY)), 'lat'...  22.1 us
    all_to_all x1, blocking collectives, body(): lax.all_to_all(chip_sum, ('lat', 'lon'), 0, 0, axis_index_groups=every, t...  19.5 us
    pallas_call x1, Pallas kernels, body(): pl.pallas_call(main_kernel, out_shape=(jax.ShapeDtypeStruct((A_DEV, C, TT...  17.4 us
    all_to_all x1, blocking collectives, body(): lax.all_to_all(spread, ('lat', 'lon'), 0, 0, axis_index_groups=every, til...  14.5 us
    ppermute x1, starting transfers between devices, body(): lax.ppermute(west, 'lon', [((i + 1) % lon, i) for i in range(lon)])  4.83 us
    ppermute x1, starting transfers between devices, body(): theirs = lax.ppermute(mine, 'lat', siblings)  3.28 us
    ppermute x1, starting transfers between devices, body(): other = lax.ppermute(spread, 'lat', siblings)  3.25 us
    unnamed x24, local copies, waits for them, and re-layouts  2.95 us
  transfers between devices with their start and end apart: 5, of which 4 were waited for; matrix products, arithmetic and copies ran while one was open for 0% of the time, Pallas kernels for 0%

profile of v1, /device:TPU:1, one launch (start us, length us, event | category | flops | bytes accessed | tf_op | source)
XLA Modules:
  0.0 101.1 jit_solution(3287695166350446349)
XLA Ops:
  0.6 0.0 copy-start.3
  0.6 0.9 copy-done.3
  1.5 0.0 copy-start.6
  1.5 0.7 copy-done.6
  2.2 0.0 copy-start.8
  2.2 0.7 copy-done.8
  2.9 0.0 copy-start.11
  2.9 0.7 copy-done.11
  3.5 1.1 %shell.1 = (bf16[80,768]{1,0:T(8,128)(2,1)S(1)}, bf16[80,384]{1,0:T(8,128)(2,1)S(1)}, bf16[80,384]{1,0:T(8,128)(2,1)S(1)}, bf16[4,80,256]{2,1,0:T(8,128)(2,1)S(1)}) custom-call(s32[1,4]{1,0:T(1,128)S(1)} %copy-done.6, s32[1,4]{1,0:T(1,128)S(1)} %copy-done.8, bf16[77,4,256]{2,1,0:T(4,128)(2,1)S(1)} %bitcast.13, s32[1,256]{1,0:T(1,128)S(1)} %copy-done.11), custom_call_target="tpu_custom_call" | custom-call | tf_op jit(solution)/shard_map/shell/pallas_call | solution.py:359
  4.6 2.2 %collective-permute-start = (bf16[80,384]{1,0:T(8,128)(2,1)S(1)}, bf16[80,384]{1,0:T(8,128)(2,1)S(1)}, u32[]{:S(2)}, u32[]{:S(2)}) collective-permute-start(bf16[80,384]{1,0:T(8,128)(2,1)S(1)} %get-tuple-element.17), channel_id=1, source_target_pairs={{0,1},{1,2},{2,3},{3,4},{4,5},{5,6},{6,7},{7,0},{8,9},{9,10},{10,1... | collective-permute-start | bytes 184328 | tf_op jit(solution)/shard_map/ppermute | solution.py:379
  6.8 4.8 %collective-permute-start.1 = (bf16[80,384]{1,0:T(8,128)(2,1)S(1)}, bf16[80,384]{1,0:T(8,128)(2,1)S(1)}, u32[]{:S(2)}, u32[]{:S(2)}) collective-permute-start(bf16[80,384]{1,0:T(8,128)(2,1)S(1)} %get-tuple-element.18), channel_id=1, source_target_pairs={{1,0},{2,1},{3,2},{4,3},{5,4},{6,5},{7,6},{0,7},{9,8},{10,9},{11,1... | collective-permute-start | bytes 184328 | tf_op jit(solution)/shard_map/ppermute | solution.py:380
  11.6 1.5 %collective-permute-done = bf16[80,384]{1,0:T(8,128)(2,1)S(1)} collective-permute-done((bf16[80,384]{1,0:T(8,128)(2,1)S(1)}, bf16[80,384]{1,0:T(8,128)(2,1)S(1)}, u32[]{:S(2)}, u32[]{:S(2)}) %collective-permute-start) | collective-permute-done | bytes 61472 | tf_op jit(solution)/shard_map/ppermute | solution.py:379
  13.2 0.0 collective-permute-done.1
  13.2 0.1 broadcast_in_dim.6
  13.3 0.0 copy-start
  13.4 0.0 copy-start.1
  13.4 0.0 copy-start.2
  13.4 0.0 copy-start.4
  13.4 0.0 copy-start.5
  13.4 0.0 copy-start.7
  13.4 0.0 copy-start.9
  13.4 0.0 copy-start.10
  13.4 22.1 %all_to_all.15.ga_ref = bf16[8,80,1152]{2,1,0:T(8,128)(2,1)S(1)} all-to-all(bf16[8,80,1152]{2,1,0:T(8,128)(2,1)S(1)} %broadcast_in_dim.6), channel_id=1, replica_groups={{0,16,32,48,64,80,96,112},{8,24,40,56,72,88,104,120},{1,17,33,49,65,81,..., dimensions={0} | all-to-all | bytes 2949120 | tf_op jit(solution)/shard_map/all_to_all | solution.py:384
  35.6 3.3 %collective-permute-start.2 = (bf16[8,80,1152]{2,1,0:T(8,128)(2,1)S(1)}, bf16[8,80,1152]{2,1,0:T(8,128)(2,1)S(1)}, u32[]{:S(2)}, u32[]{:S(2)}) collective-permute-start(bf16[8,80,1152]{2,1,0:T(8,128)(2,1)S(1)} %all_to_all.15.ga_ref), channel_id=1, source_target_pairs={{0,8},{8,0},{16,24},{24,16},{32,40},{40,32},{48,56},{56,48},{64,72... | collective-permute-start | bytes 4423688 | tf_op jit(solution)/shard_map/ppermute | solution.py:387
  38.8 2.9 %collective-permute-done.2.gb_ref = bf16[8,80,1152]{2,1,0:T(8,128)(2,1)S(1)} collective-permute-done((bf16[8,80,1152]{2,1,0:T(8,128)(2,1)S(1)}, bf16[8,80,1152]{2,1,0:T(8,128)(2,1)S(1)}, u32[]{:S(2)}, u32[]{:S(2)}) %collective-permute-start.2) | collective-permute-done | bytes 1474592 | tf_op jit(solution)/shard_map/ppermute | solution.py:387
  41.7 0.0 copy-done
  41.7 0.0 copy-done.1
  41.7 0.0 copy-done.2
  41.7 0.0 copy-done.4
  41.8 0.0 copy-done.5
  41.8 0.0 copy-done.7
  41.8 0.0 copy-done.9
  41.8 0.0 copy-done.10
  41.8 17.4 %block.1 = (bf16[4,200,256]{2,1,0:T(8,128)(2,1)}, f32[64,24,128]{2,1,0:T(8,128)S(1)}, bf16[64,24,128]{2,1,0:T(8,128)(2,1)S(1)}) custom-call(s32[1,4]{1,0:T(1,128)S(1)} %copy-done.7, s32[1,4]{1,0:T(1,128)S(1)} %copy-done.9, bf16[8,80,1152]{2,1,0:T(8,128)(2,1)S(1)} %all_to_all.15.ga_ref, bf16[8,80,1152]{2,1,0:T(8,128)(2,1)S(1)} %collective-permute-done.2.gb_ref, ...), custom_call_target="tpu_custom_call" | custom-call | tf_op jit(solution)/shard_map/block/pallas_call | solution.py:390
  59.2 0.5 collective-permute-start.3
  59.7 1.3 %collective-permute-done.3 = bf16[64,24,128]{2,1,0:T(8,128)(2,1)S(1)} collective-permute-done((bf16[64,24,128]{2,1,0:T(8,128)(2,1)S(1)}, bf16[64,24,128]{2,1,0:T(8,128)(2,1)S(1)}, u32[]{:S(2)}, u32[]{:S(2)}) %collective-permute-start.3) | collective-permute-done | bytes 393248 | tf_op jit(solution)/shard_map/ppermute | solution.py:430
  61.0 0.1 add_convert_fusion
  61.1 19.5 %all_to_all.16 = bf16[64,24,128]{2,1,0:T(8,128)(2,1)S(1)} all-to-all(bf16[64,24,128]{2,1,0:T(8,128)(2,1)S(1)} %add_convert_fusion), channel_id=1, replica_groups={{0,1,2,3,4,5,6,7,16,17,18,19,20,21,22,23,32,33,34,35,36,37,38,39,48,49,..., dimensions={0} | all-to-all | bytes 786432 | tf_op jit(solution)/shard_map/all_to_all | solution.py:433
  80.7 0.1 reduce_sum.12
  80.7 0.1 broadcast_in_dim.8
  80.8 14.5 %all_to_all.17.own_ref = bf16[64,24,128]{2,1,0:T(8,128)(2,1)S(1)} all-to-all(bf16[64,24,128]{2,1,0:T(8,128)(2,1)S(1)} %broadcast_in_dim.8), channel_id=1, replica_groups={{0,1,2,3,4,5,6,7,16,17,18,19,20,21,22,23,32,33,34,35,36,37,38,39,48,49,..., dimensions={0} | all-to-all | bytes 786432 | tf_op jit(solution)/shard_map/all_to_all | solution.py:437
  95.3 3.2 %collective-permute-start.4 = (bf16[64,24,128]{2,1,0:T(8,128)(2,1)S(1)}, bf16[64,24,128]{2,1,0:T(8,128)(2,1)S(1)}, u32[]{:S(2)}, u32[]{:S(2)}) collective-permute-start(bf16[64,24,128]{2,1,0:T(8,128)(2,1)S(1)} %all_to_all.17.own_ref), channel_id=1, source_target_pairs={{0,8},{8,0},{16,24},{24,16},{32,40},{40,32},{48,56},{56,48},{64,72... | collective-permute-start | bytes 1179656 | tf_op jit(solution)/shard_map/ppermute | solution.py:438
  98.5 1.3 %collective-permute-done.4.other_ref = bf16[64,24,128]{2,1,0:T(8,128)(2,1)S(1)} collective-permute-done((bf16[64,24,128]{2,1,0:T(8,128)(2,1)S(1)}, bf16[64,24,128]{2,1,0:T(8,128)(2,1)S(1)}, u32[]{:S(2)}, u32[]{:S(2)}) %collective-permute-start.4) | collective-permute-done | bytes 393248 | tf_op jit(solution)/shard_map/ppermute | solution.py:438
  99.9 1.3 %finish.1 = (f32[200,800]{1,0:T(8,128)}, f32[200,800]{1,0:T(8,128)}, f32[49,200]{1,0:T(8,128)}, f32[1,200]{1,0:T(1,128)}) custom-call(bf16[64,24,128]{2,1,0:T(8,128)(2,1)S(1)} %all_to_all.17.own_ref, bf16[64,24,128]{2,1,0:T(8,128)(2,1)S(1)} %collective-permute-done.4.other_ref), custom_call_target="tpu_custom_call" | custom-call | tf_op jit(solution)/shard_map/finish/pallas_call | solution.py:439
  (2 shorter events, 0.0 us)
Async XLA Ops:
  0.6 0.9 copy-start.3
  1.5 0.7 copy-start.6
  2.2 0.7 copy-start.8
  2.9 0.7 copy-start.11
  4.6 8.5 %collective-permute-start = (bf16[80,384]{1,0:T(8,128)(2,1)S(1)}, bf16[80,384]{1,0:T(8,128)(2,1)S(1)}, u32[]{:S(2)}, u32[]{:S(2)}) collective-permute-start(bf16[80,384]{1,0:T(8,128)(2,1)S(1)} %get-tuple-element.17), channel_id=1, source_target_pairs={{0,1},{1,2},{2,3},{3,4},{4,5},{5,6},{6,7},{7,0},{8,9},{9,10},{10,1... | collective-permute-start | bytes 184328 | tf_op jit(solution)/shard_map/ppermute | solution.py:379
  6.8 6.4 %collective-permute-start.1 = (bf16[80,384]{1,0:T(8,128)(2,1)S(1)}, bf16[80,384]{1,0:T(8,128)(2,1)S(1)}, u32[]{:S(2)}, u32[]{:S(2)}) collective-permute-start(bf16[80,384]{1,0:T(8,128)(2,1)S(1)} %get-tuple-element.18), channel_id=1, source_target_pairs={{1,0},{2,1},{3,2},{4,3},{5,4},{6,5},{7,6},{0,7},{9,8},{10,9},{11,1... | collective-permute-start | bytes 184328 | tf_op jit(solution)/shard_map/ppermute | solution.py:380
  13.3 28.4 %copy-start = (bf16[1,4,200,256]{3,2,1,0:T(8,128)(2,1)S(1)}, bf16[1,4,200,256]{3,2,1,0:T(8,128)(2,1)}, u32[]{:S(2)}) copy-start(bf16[1,4,200,256]{3,2,1,0:T(8,128)(2,1)} %param.18) | copy-start | bytes 1228804
  13.4 28.4 %copy-start.1 = (bf16[200,800]{1,0:T(8,128)(2,1)S(1)}, bf16[200,800]{1,0:T(8,128)(2,1)}, u32[]{:S(2)}) copy-start(bf16[200,800]{1,0:T(8,128)(2,1)} %wi_ref.1) | copy-start | bytes 960004
  13.4 28.4 %copy-start.2 = (bf16[800,200]{0,1:T(8,128)(2,1)S(1)}, bf16[800,200]{0,1:T(8,128)(2,1)}, u32[]{:S(2)}) copy-start(bf16[800,200]{0,1:T(8,128)(2,1)} %param.17) | copy-start | bytes 960004
  13.4 28.4 %copy-start.4 = (f32[200,49]{0,1:T(8,128)S(1)}, f32[200,49]{0,1:T(8,128)}, u32[]{:S(2)}) copy-start(f32[200,49]{0,1:T(8,128)} %param.14) | copy-start | bytes 117604
  13.4 28.4 %copy-start.5 = (bf16[77,200]{1,0:T(8,128)(2,1)S(1)}, bf16[77,200]{1,0:T(8,128)(2,1)}, u32[]{:S(2)}) copy-start(bf16[77,200]{1,0:T(8,128)(2,1)} %sw_ref.1) | copy-start | bytes 92404
  13.4 28.4 %copy-start.7 = (s32[1,4]{1,0:T(1,128)S(1)}, s32[1,4]{1,0:T(1,128)}, u32[]{:S(2)}) copy-start(s32[1,4]{1,0:T(1,128)} %pos_ref.3) | copy-start | bytes 52
  13.4 28.4 %copy-start.9 = (s32[1,4]{1,0:T(1,128)S(1)}, s32[1,4]{1,0:T(1,128)}, u32[]{:S(2)}) copy-start(s32[1,4]{1,0:T(1,128)} %rows_ref.3) | copy-start | bytes 52
  13.4 28.4 %copy-start.10 = (f32[200]{0:T(256)S(1)}, f32[200]{0:T(256)}, u32[]{:S(2)}) copy-start(f32[200]{0:T(256)} %param.15) | copy-start | bytes 2404
  35.6 6.2 %collective-permute-start.2 = (bf16[8,80,1152]{2,1,0:T(8,128)(2,1)S(1)}, bf16[8,80,1152]{2,1,0:T(8,128)(2,1)S(1)}, u32[]{:S(2)}, u32[]{:S(2)}) collective-permute-start(bf16[8,80,1152]{2,1,0:T(8,128)(2,1)S(1)} %all_to_all.15.ga_ref), channel_id=1, source_target_pairs={{0,8},{8,0},{16,24},{24,16},{32,40},{40,32},{48,56},{56,48},{64,72... | collective-permute-start | bytes 4423688 | tf_op jit(solution)/shard_map/ppermute | solution.py:387
  59.2 1.8 %collective-permute-start.3 = (bf16[64,24,128]{2,1,0:T(8,128)(2,1)S(1)}, bf16[64,24,128]{2,1,0:T(8,128)(2,1)S(1)}, u32[]{:S(2)}, u32[]{:S(2)}) collective-permute-start(bf16[64,24,128]{2,1,0:T(8,128)(2,1)S(1)} %get-tuple-element.22), channel_id=1, source_target_pairs={{0,8},{8,0},{16,24},{24,16},{32,40},{40,32},{48,56},{56,48},{64,72... | collective-permute-start | bytes 1179656 | tf_op jit(solution)/shard_map/ppermute | solution.py:430
  95.3 4.6 %collective-permute-start.4 = (bf16[64,24,128]{2,1,0:T(8,128)(2,1)S(1)}, bf16[64,24,128]{2,1,0:T(8,128)(2,1)S(1)}, u32[]{:S(2)}, u32[]{:S(2)}) collective-permute-start(bf16[64,24,128]{2,1,0:T(8,128)(2,1)S(1)} %all_to_all.17.own_ref), channel_id=1, source_target_pairs={{0,8},{8,0},{16,24},{24,16},{32,40},{40,32},{48,56},{56,48},{64,72... | collective-permute-start | bytes 1179656 | tf_op jit(solution)/shard_map/ppermute | solution.py:438

commit v2 on v1

--- a/solution.py
+++ b/solution.py
@@ -18,9 +18,9 @@
 HALF = 128
 KPAD = 80
 PIECE = 48
-SHELL = 4 * PIECE
-EDGE = A_DEV * PIECE
-PAY = A_DEV * SHELL + 2 * EDGE
+SHELL = 160
+PAY = A_DEV * SHELL
+STRIP = 72
 GROUP = 8
 PITCH = 24
 PROWS = TS + KW - 1
@@ -34,13 +34,26 @@
 
 
 def shell_cells():
-    m = np.arange(PIECE)
-    left = (m // 3) * TS + m % 3
-    pieces = np.concatenate([m, 13 * TS + m, left, left + 13, np.full(256 - SHELL, -1)])
-    return pieces.reshape(1, 256).astype(np.int32)
-
-
-def shell_kernel(pos_ref, rows_ref, x_ref, map_ref, shell_ref, east_ref, west_ref, kept_ref, flat, cut, buf):
+    m = np.arange(60)
+    ends = (3 + m // 6) * TS + np.where(m % 6 < 3, m % 6, m % 6 + 10)
+    cells = np.concatenate([np.arange(PIECE), 13 * TS + np.arange(PIECE), ends, np.full(100, -1)])
+    return cells.reshape(1, 256).astype(np.int32)
+
+
+def strip_sources():
+    lane_of = {int(c): i for i, c in enumerate(shell_cells()[0]) if c >= 0}
+    table = np.full((STRIP, HALF), -100000, np.int32)
+    for j in range(3 * PROWS):
+        row, c = j // 3 - 3, j % 3
+        part = 0 if row < 0 else (1 if row < TS else 2)
+        for side in range(2):
+            table[j, 3 * side + part] = lane_of[(row % TS) * TS + (13 + c if side == 0 else c)]
+    table[:PIECE, 6] = lane_of[13 * TS] + np.arange(PIECE)
+    table[:PIECE, 7] = np.arange(PIECE)
+    return table
+
+
+def shell_kernel(pos_ref, rows_ref, x_ref, map_ref, shell_ref, kept_ref, flat, cut, buf):
     for k in range(CIN):
         for h in range(2):
             flat[h, A_DEV * k : A_DEV * k + A_DEV, :] = x_ref[k, :, h * HALF : (h + 1) * HALF].astype(F32)
@@ -58,29 +71,89 @@
     cut[0] = pieces[:, 0:HALF]
     cut[1] = pieces[:, HALF:256]
     fill = lax.broadcasted_iota(jnp.int32, (3, 1), 0)
-    buf[:, 768:1536] = jnp.zeros((KPAD, 768), F32)
     kept_ref[...] = jnp.zeros_like(kept_ref)
     for a in range(A_DEV):
         for h in range(2):
             kept_ref[a, 0:CIN, h * HALF : (h + 1) * HALF] = flat[h, pl.ds(a, CIN, stride=A_DEV), :].astype(BF16)
-        v0 = cut[0, pl.ds(a, CIN, stride=A_DEV), :]
-        v1 = cut[1, pl.ds(a, CIN, stride=A_DEV), :]
         place = pos_ref[0, a]
         tail = jnp.where(fill == 0, place // 16, jnp.where(fill == 1, place % 16, 0)).astype(F32)
         at = a * SHELL
-        buf[0:CIN, at : at + HALF] = v0
-        buf[0:CIN, at + HALF : at + SHELL] = v1[:, 0 : SHELL - HALF]
+        buf[0:CIN, at : at + HALF] = cut[0, pl.ds(a, CIN, stride=A_DEV), :]
+        buf[0:CIN, at + HALF : at + SHELL] = cut[1, pl.ds(a, CIN, stride=A_DEV), :][:, 0 : SHELL - HALF]
         buf[CIN:KPAD, at : at + SHELL] = jnp.broadcast_to(tail, (3, SHELL))
-        east = 768 + a * PIECE
-        west = 1152 + EDGE + a * PIECE
-        buf[0:CIN, east : east + PIECE] = v1[:, 16:64]
-        buf[CIN:KPAD, east : east + PIECE] = jnp.broadcast_to(tail, (3, PIECE))
-        buf[0:CIN, west : west + 32] = v0[:, 96:HALF]
-        buf[0:CIN, west + 32 : west + PIECE] = v1[:, 0:16]
-        buf[CIN:KPAD, west : west + PIECE] = jnp.broadcast_to(tail, (3, PIECE))
-    shell_ref[...] = buf[:, 0:768].astype(BF16)
-    east_ref[...] = buf[:, 768:1152].astype(BF16)
-    west_ref[...] = buf[:, 1152:1536].astype(BF16)
+    shell_ref[...] = buf[...].astype(BF16)
+
+
+def pick_kernel(
+    pos_ref, east_ref, west_ref, ga_ref, gb_ref, src_ref,
+    side_ref, band_ref, to_east_ref, to_west_ref,
+    pm, tv, sm, ts, sem, gaps,
+):
+    for g in range(GROUP):
+        for j, ref in enumerate((ga_ref, gb_ref)):
+            tail = ref[g, 64:KPAD, :].astype(F32)
+            pm[2 * g + j : 2 * g + j + 1, :] = tail[13:14, :] * 16.0 + tail[14:15, :]
+    lane = lax.broadcasted_iota(jnp.int32, (16, PAY), 1)
+    slot = lax.broadcasted_iota(jnp.int32, (16, PAY), 0)
+    label = jnp.where(lane % SHELL == 0, pm[...], -1.0)
+    code = (slot * 1024 + lane + 1).astype(F32)
+    tv[...] = jnp.zeros_like(tv)
+
+    def ask(entry, want):
+        hit = jnp.where(label == want.astype(F32), code, 0.0)
+        acc = jnp.sum(hit, axis=0, keepdims=True)
+        folded = acc[:, 0:HALF]
+        for i in range(1, PAY // HALF):
+            folded = folded + acc[:, i * HALF : (i + 1) * HALF]
+        tv[entry : entry + 1, :] = folded
+
+    for a in range(A_DEV):
+        q = pos_ref[0, a]
+        row, col = q // COLS, q % COLS
+        for n, (dr, dc) in enumerate(DIRS):
+            nrow, ncol = row + dr, col + dc
+            inside = (nrow >= 0) & (nrow < TILE_ROWS) & (ncol >= 0) & (ncol < COLS)
+            ask(a * 8 + n, jnp.where(inside, nrow * COLS + ncol, -7))
+        for first, ref, edge in ((32, east_ref, 0), (48, west_ref, COLS - 1)):
+            q = ref[0, a]
+            row, col = q // COLS, q % COLS
+            for dr in (-1, 0, 1):
+                inside = (row + dr >= 0) & (row + dr < TILE_ROWS) & (col == edge)
+                ask(first + a * 4 + dr + 1, jnp.where(inside, (row + dr) * COLS + COLS - 1 - edge, -7))
+    total = jnp.sum(tv[...], axis=1, keepdims=True)
+    sm[...] = jnp.broadcast_to(total, (64, HALF)).astype(jnp.int32)
+    tcopy = pltpu.make_async_copy(sm, ts, sem)
+    tcopy.start()
+    column = lax.broadcasted_iota(jnp.int32, (STRIP, 3 * HALF), 1)
+    for n in range(8):
+        gaps[n] = column - src_ref[:, n : n + 1]
+    tcopy.wait()
+
+    def take(entry, n, size):
+        got = ts[entry, 0]
+        spot = jnp.maximum(got - 1, 0)
+        source = spot // 1024
+        at = spot % 1024
+        block = jnp.minimum(at // HALF, PAY // HALF - 3)
+        shift = jnp.where(got == 0, -5000, at - block * HALF)
+        cells = pl.ds(pl.multiple_of(block * HALF, HALF), 3 * HALF)
+        near = ga_ref[source // 2, :, cells]
+        far = gb_ref[source // 2, :, cells]
+        window = jnp.where(source % 2 == 0, near, far)
+        pick = (gaps[n, 0:size, :] == shift).astype(F32).astype(BF16)
+        return lax.dot_general(pick, window, NT, preferred_element_type=F32)
+
+    order = {where: n for n, where in enumerate(DIRS)}
+    for a in range(A_DEV):
+        rows = slice(a * STRIP, (a + 1) * STRIP)
+        for side, dc in enumerate((-1, 1)):
+            parts = [take(a * 8 + order[dr, dc], 3 * side + dr + 1, STRIP) for dr in (-1, 0, 1)]
+            side_ref[side, rows, :] = (parts[0] + parts[1] + parts[2]).astype(BF16)
+        band_ref[2 * a] = take(a * 8 + order[-1, 0], 6, PIECE).astype(BF16)
+        band_ref[2 * a + 1] = take(a * 8 + order[1, 0], 7, PIECE).astype(BF16)
+        for side, first, ref in ((0, 32, to_east_ref), (1, 48, to_west_ref)):
+            parts = [take(first + a * 4 + dr + 1, 3 * side + dr + 1, STRIP) for dr in (-1, 0, 1)]
+            ref[rows, :] = (parts[0] + parts[1] + parts[2]).astype(BF16)
 
 
 def gelu_parts(v):
@@ -93,9 +166,9 @@
 
 
 def main_kernel(
-    pos_ref, rows_ref, ga_ref, gb_ref, x_ref, sw_ref, dw_ref, gain_ref, wi_ref, wo_ref, cot_ref,
+    rows_ref, side_ref, band_ref, west_ref, east_ref, x_ref, sw_ref, dw_ref, gain_ref, wi_ref, wo_ref, cot_ref,
     out_ref, own_ref, send_ref,
-    swp, dwt, gnp, wide, wit, wot, pm, tv, sm, ts, sem, lp, st, pt, cv, un, iv, ft, mg, hs, gps, gf, gc, si, so,
+    swp, dwt, gnp, wide, wit, wot, pt, cv, un, iv, ft, mg, hs, gps, gf, gc, si, so,
 ):
     swp[...] = jnp.zeros_like(swp)
     swp[0:CIN, 0:C] = sw_ref[...]
@@ -107,35 +180,6 @@
     gain0 = gnp[:, 0:HALF]
     gain1 = gnp[:, HALF:256]
 
-    for g in range(GROUP):
-        for j, ref in enumerate((ga_ref, gb_ref)):
-            tail = ref[g, 64:KPAD, :].astype(F32)
-            pm[2 * g + j : 2 * g + j + 1, :] = tail[13:14, :] * 16.0 + tail[14:15, :]
-    lane = lax.broadcasted_iota(jnp.int32, (16, PAY), 1)
-    slot = lax.broadcasted_iota(jnp.int32, (16, PAY), 0)
-    kind = jnp.where(lane < 768, 0, jnp.where(lane < 768 + EDGE, 1, 2))
-    first = jnp.where(lane < 768, lane % SHELL, (lane - 768) % PIECE) == 0
-    label = jnp.where(first, pm[...] + 1000.0 * kind.astype(F32), -1.0)
-    code = (slot * PAY + lane + 1).astype(F32)
-    for a in range(A_DEV):
-        q = pos_ref[0, a]
-        row, col = q // COLS, q % COLS
-        for n, (dr, dc) in enumerate(DIRS):
-            nrow, ncol = row + dr, col + dc
-            inside = (nrow >= 0) & (nrow < TILE_ROWS)
-            side = jnp.where(ncol < 0, 1000, jnp.where(ncol >= COLS, 2000, 0))
-            want = jnp.where(inside, nrow * COLS + (ncol + COLS) % COLS + side, -7)
-            hit = jnp.where(label == want.astype(F32), code, 0.0)
-            acc = jnp.sum(hit, axis=0, keepdims=True)
-            folded = acc[:, 0:HALF]
-            for i in range(1, PAY // HALF):
-                folded = folded + acc[:, i * HALF : (i + 1) * HALF]
-            tv[a * 8 + n : a * 8 + n + 1, :] = folded
-    total = jnp.sum(tv[...], axis=1, keepdims=True)
-    sm[...] = jnp.broadcast_to(total, (32, HALF)).astype(jnp.int32)
-    tcopy = pltpu.make_async_copy(sm, ts, sem)
-    tcopy.start()
-
     for a in range(A_DEV):
         rows = lax.dot_general(x_ref[a], swp[...], TN, preferred_element_type=F32)
         rows = rows.astype(BF16).astype(F32)
@@ -154,56 +198,23 @@
         wide[0:C, 0:HID] = src[...].astype(F32)
         for b in range(HB):
             dst[b * HALF : (b + 1) * HALF, :] = wide[:, b * HALF : (b + 1) * HALF].T.astype(BF16)
-    tcopy.wait()
-
-    gap = lax.broadcasted_iota(jnp.int32, (PIECE, 256), 1) - lax.broadcasted_iota(jnp.int32, (PIECE, 256), 0)
-    for a in range(A_DEV):
-        col = pos_ref[0, a] % COLS
-        for n, (dr, dc) in enumerate(DIRS):
-            got = ts[a * 8 + n, 0]
-            if dc == 0:
-                offset = 48 if dr < 0 else 0
-            elif dc < 0:
-                offset = jnp.where(col == 0, 0, 144)
-            else:
-                offset = jnp.where(col == COLS - 1, 0, 96)
-            spot = jnp.maximum(got - 1, 0)
-            source = spot // PAY
-            at = spot - source * PAY + offset
-            block = jnp.minimum(at // HALF, PAY // HALF - 2)
-            shift = jnp.where(got == 0, -1000, at - block * HALF)
-            cells = pl.ds(pl.multiple_of(block * HALF, HALF), 256)
-            near = ga_ref[source // 2, :, cells]
-            far = gb_ref[source // 2, :, cells]
-            window = jnp.where(source % 2 == 0, near, far)
-            pick = (gap == shift).astype(F32).astype(BF16)
-            piece = lax.dot_general(pick, window, NT, preferred_element_type=F32)
-            spot = (a * 8 + n) * PIECE
-            lp[spot : spot + PIECE, 0:KPAD] = piece.astype(BF16)
-    for a in range(A_DEV):
-        span = slice(a * 8 * PIECE, (a + 1) * 8 * PIECE)
-        rows = jnp.dot(lp[span, 0:KPAD], swp[...], preferred_element_type=F32)
-        rows = rows.astype(BF16).astype(F32)
-        st[0, span, :] = rows[:, 0:HALF]
-        st[1, span, :] = rows[:, HALF:256]
-    for a in range(A_DEV):
-        base = {where: (a * 8 + n) * PIECE for n, where in enumerate(DIRS)}
+
+    for side, (ref, xx) in enumerate(((west_ref, 0), (east_ref, 19))):
+        cells = (side_ref[side].astype(F32) + ref[...].astype(F32)).astype(BF16)
+        rows = jnp.dot(cells, swp[...], preferred_element_type=F32).astype(BF16).astype(F32)
         for h in range(2):
-            for i in range(3):
-                at = (a * PROWS + i) * PITCH
-                low = at + 19 * PITCH
-                up, down = base[-1, 0] + i * TS, base[1, 0] + i * TS
-                pt[h, at + 3 : at + 3 + TS, :] = st[h, up : up + TS, :]
-                pt[h, low + 3 : low + 3 + TS, :] = st[h, down : down + TS, :]
-                for dc, xx in ((-1, 0), (1, 19)):
-                    up, down = base[-1, dc] + 39 + 3 * i, base[1, dc] + 3 * i
-                    pt[h, at + xx : at + xx + 3, :] = st[h, up : up + 3, :]
-                    pt[h, low + xx : low + xx + 3, :] = st[h, down : down + 3, :]
-            for y in range(TS):
-                at = (a * PROWS + 3 + y) * PITCH
-                for dc, xx in ((-1, 0), (1, 19)):
-                    side = base[0, dc] + 3 * y
-                    pt[h, at + xx : at + xx + 3, :] = st[h, side : side + 3, :]
+            for a in range(A_DEV):
+                for y in range(PROWS):
+                    at = (a * PROWS + y) * PITCH + xx
+                    j = a * STRIP + 3 * y
+                    pt[h, at : at + 3, :] = rows[j : j + 3, h * HALF : (h + 1) * HALF]
+    for a in range(A_DEV):
+        for n in range(2):
+            rows = jnp.dot(band_ref[2 * a + n], swp[...], preferred_element_type=F32).astype(BF16).astype(F32)
+            for h in range(2):
+                for i in range(3):
+                    at = (a * PROWS + 19 * n + i) * PITCH + 3
+                    pt[h, at : at + TS, :] = rows[i * TS : (i + 1) * TS, h * HALF : (h + 1) * HALF]
 
     def conv_step(step, carry):
         h = step // (2 * A_DEV)
@@ -356,35 +367,54 @@
 def body(x_tiles, tile_pos, valid_rows, stem_w, dw_kernel, norm_gain, w_in, w_out, cotangent):
     smem = pl.BlockSpec(memory_space=pltpu.SMEM)
     vmem = pl.BlockSpec(memory_space=pltpu.VMEM)
-    shell, east, west, inputs = pl.pallas_call(
+    lon = lax.axis_size("lon")
+    lat = lax.axis_size("lat")
+    eastward = [(i, (i + 1) % lon) for i in range(lon)]
+    westward = [((i + 1) % lon, i) for i in range(lon)]
+    pos_west = lax.ppermute(tile_pos, "lon", eastward)
+    pos_east = lax.ppermute(tile_pos, "lon", westward)
+    shell, inputs = pl.pallas_call(
         shell_kernel,
-        out_shape=(
-            pltpu.VMEM((KPAD, 768), BF16),
-            pltpu.VMEM((KPAD, 384), BF16),
-            pltpu.VMEM((KPAD, 384), BF16),
-            pltpu.VMEM((A_DEV, KPAD, TT), BF16),
-        ),
+        out_shape=(pltpu.VMEM((KPAD, PAY), BF16), pltpu.VMEM((A_DEV, KPAD, TT), BF16)),
         in_specs=[smem, smem, vmem, vmem],
-        out_specs=(vmem, vmem, vmem, vmem),
+        out_specs=(vmem, vmem),
         scratch_shapes=[
             pltpu.VMEM((2, A_DEV * CIN, HALF), F32),
             pltpu.VMEM((2, A_DEV * CIN, HALF), F32),
-            pltpu.VMEM((KPAD, 1536), F32),
+            pltpu.VMEM((KPAD, PAY), F32),
         ],
-        compiler_params=pltpu.CompilerParams(vmem_limit_bytes=8 << 20),
         name="shell",
     )(tile_pos, valid_rows, x_tiles[0].transpose(1, 0, 2), jnp.asarray(shell_cells()))
-    lon = lax.axis_size("lon")
-    lat = lax.axis_size("lat")
-    from_west = lax.ppermute(east, "lon", [(i, (i + 1) % lon) for i in range(lon)])
-    from_east = lax.ppermute(west, "lon", [((i + 1) % lon, i) for i in range(lon)])
-    payload = jnp.concatenate([shell, from_west + from_east], axis=1)
+    shell, pos_west, pos_east = lax.optimization_barrier((shell, pos_west, pos_east))
     same_core = [[i for i in range(c, lat, 2)] for c in range(2)]
     siblings = [(i, i ^ 1) for i in range(lat)]
     mine = lax.all_to_all(
-        jnp.broadcast_to(payload[None], (GROUP, KPAD, PAY)), "lat", 0, 0, axis_index_groups=same_core, tiled=True
+        jnp.broadcast_to(shell[None], (GROUP, KPAD, PAY)), "lat", 0, 0, axis_index_groups=same_core, tiled=True
     )
     theirs = lax.ppermute(mine, "lat", siblings)
+    side, band, to_east, to_west = pl.pallas_call(
+        pick_kernel,
+        out_shape=(
+            pltpu.VMEM((2, A_DEV * STRIP, KPAD), BF16),
+            pltpu.VMEM((2 * A_DEV, PIECE, KPAD), BF16),
+            pltpu.VMEM((A_DEV * STRIP, KPAD), BF16),
+            pltpu.VMEM((A_DEV * STRIP, KPAD), BF16),
+        ),
+        in_specs=[smem] * 3 + [vmem] * 3,
+        out_specs=(vmem, vmem, vmem, vmem),
+        scratch_shapes=[
+            pltpu.VMEM((16, PAY), F32),
+            pltpu.VMEM((64, HALF), F32),
+            pltpu.VMEM((64, HALF), jnp.int32),
+            pltpu.SMEM((64, HALF), jnp.int32),
+            pltpu.SemaphoreType.DMA,
+            pltpu.VMEM((8, STRIP, 3 * HALF), jnp.int32),
+        ],
+        compiler_params=pltpu.CompilerParams(vmem_limit_bytes=16 << 20),
+        name="pick",
+    )(tile_pos, pos_east, pos_west, on_chip(mine), on_chip(theirs), jnp.asarray(strip_sources()))
+    from_west = lax.ppermute(to_east, "lon", eastward)
+    from_east = lax.ppermute(to_west, "lon", westward)
 
     cells = A_DEV * TT
     out_tiles, own, send = pl.pallas_call(
@@ -394,7 +424,7 @@
             pltpu.VMEM((CHUNKS, 24, HALF), F32),
             pltpu.VMEM((CHUNKS, 24, HALF), BF16),
         ),
-        in_specs=[smem] * 2 + [vmem] * 9,
+        in_specs=[smem] + [vmem] * 11,
         out_specs=(vmem, vmem, vmem),
         scratch_shapes=[
             pltpu.VMEM((KPAD, 256), BF16),
@@ -403,13 +433,6 @@
             pltpu.VMEM((256, HB * HALF), F32),
             pltpu.VMEM((HB * HALF, 256), BF16),
             pltpu.VMEM((HB * HALF, 256), BF16),
-            pltpu.VMEM((16, PAY), F32),
-            pltpu.VMEM((32, HALF), F32),
-            pltpu.VMEM((32, HALF), jnp.int32),
-            pltpu.SMEM((32, HALF), jnp.int32),
-            pltpu.SemaphoreType.DMA,
-            pltpu.VMEM((32 * PIECE, HALF), BF16),
-            pltpu.VMEM((2, 32 * PIECE, HALF), F32),
             pltpu.VMEM((2, A_DEV * PROWS * PITCH, HALF), F32),
             pltpu.VMEM((2, cells, HALF), F32),
             pltpu.VMEM((2, 56, HALF), F32),
@@ -425,7 +448,7 @@
         ],
         compiler_params=pltpu.CompilerParams(vmem_limit_bytes=32 << 20),
         name="block",
-    )(tile_pos, valid_rows, on_chip(mine), on_chip(theirs), inputs, stem_w, dw_kernel.T, norm_gain.reshape(1, C), w_in, w_out.T, cotangent[0])
+    )(valid_rows, side, band, on_chip(from_west), on_chip(from_east), inputs, stem_w, dw_kernel.T, norm_gain.reshape(1, C), w_in, w_out.T, cotangent[0])
 
     arrived = lax.ppermute(send, "lat", siblings)
     chip_sum = (own + arrived.astype(F32)).astype(BF16)

time: 101 us -> 99.6 us (0.986)
  blocking collectives: 56.2 us -> 49.2 us
  starting transfers between devices: 14 us -> 19.7 us
  local copies, waits for them, and re-layouts: 3.11 us -> 0.8 us
  Pallas kernels: 19.7 us -> 21.8 us
    all_to_all x1, blocking collectives: 22.1 us -> 15.7 us  [body(): lax.all_to_all(jnp.broadcast_to(shell[None], (GROUP, KPAD, PAY)), 'lat',...]
    ppermute x2 -> x4, starting transfers between devices: 7.01 us -> 12.5 us  [the longest x1 5.43 us: body(): from_east = lax.ppermute(to_west, 'lon', westward)]
    pallas_call x1 -> x2, Pallas kernels: 1.09 us -> 5.13 us  [the longest x1 3.75 us: body(): pl.pallas_call(pick_kernel, out_shape=(pltpu.VMEM((2, A_DEV * STRIP, KPAD...]
    unnamed x24 -> x18, local copies, waits for them, and re-layouts: 2.95 us -> 0.68 us
    pallas_call x1, Pallas kernels: 17.4 us -> 15.4 us  [body(): pl.pallas_call(main_kernel, out_shape=(jax.ShapeDtypeStruct((A_DEV, C, TT...]
    ppermute x2 -> x4, waiting for transfers between devices: 1.53 us -> 2.2 us  [the longest x1 2.2 us: body(): from_west = lax.ppermute(to_east, 'lon', eastward)]
  transfers between devices with their start and end apart: 5 -> 7, of which waited for: 4 -> 4; matrix products, arithmetic and copies ran while one was open for 0% -> 0% of each run, Pallas kernels for 0% -> 1%
where the time goes in v2:
time: 99.6 us; the launch traced here: 99.3 us
  blocking collectives  49.2 us (49%)
  Pallas kernels  21.8 us (22%)
  starting transfers between devices  19.7 us (20%)
  waiting for transfers between devices  6.86 us (7%)
    all_to_all x1, blocking collectives, body(): lax.all_to_all(chip_sum, ('lat', 'lon'), 0, 0, axis_index_groups=every, t...  19 us
    all_to_all x1, blocking collectives, body(): lax.all_to_all(jnp.broadcast_to(shell[None], (GROUP, KPAD, PAY)), 'lat',...  15.7 us
    pallas_call x1, Pallas kernels, body(): pl.pallas_call(main_kernel, out_shape=(jax.ShapeDtypeStruct((A_DEV, C, TT...  15.4 us
    all_to_all x1, blocking collectives, body(): lax.all_to_all(spread, ('lat', 'lon'), 0, 0, axis_index_groups=every, til...  14.5 us
    ppermute x1, starting transfers between devices, body(): from_east = lax.ppermute(to_west, 'lon', westward)  5.43 us
    ppermute x1, starting transfers between devices, body(): pos_east = lax.ppermute(tile_pos, 'lon', westward)  4.83 us
    pallas_call x1, Pallas kernels, body(): pl.pallas_call(pick_kernel, out_shape=(pltpu.VMEM((2, A_DEV * STRIP, KPAD...  3.75 us
    ppermute x1, starting transfers between devices, body(): other = lax.ppermute(spread, 'lat', siblings)  3.25 us
  transfers between devices with their start and end apart: 7, of which 4 were waited for; matrix products, arithmetic and copies ran while one was open for 0% of the time, Pallas kernels for 1%

profile of v2, /device:TPU:1, one launch (start us, length us, event | category | flops | bytes accessed | tf_op | source)
XLA Modules:
  0.0 99.3 jit_solution(12025373400962789648)
XLA Ops:
  0.6 2.2 %collective-permute-start = (s32[1,4]{1,0:T(1,128)}, s32[1,4]{1,0:T(1,128)S(1)}, u32[]{:S(2)}, u32[]{:S(2)}) collective-permute-start(s32[1,4]{1,0:T(1,128)} %pos_ref.3), channel_id=1, source_target_pairs={{0,1},{1,2},{2,3},{3,4},{4,5},{5,6},{6,7},{7,0},{8,9},{9,10},{10,1... | collective-permute-start | bytes 56 | tf_op jit(solution)/shard_map/ppermute | solution.py:374
  2.8 4.8 %collective-permute-start.1 = (s32[1,4]{1,0:T(1,128)}, s32[1,4]{1,0:T(1,128)S(1)}, u32[]{:S(2)}, u32[]{:S(2)}) collective-permute-start(s32[1,4]{1,0:T(1,128)} %pos_ref.3), channel_id=1, source_target_pairs={{1,0},{2,1},{3,2},{4,3},{5,4},{6,5},{7,6},{0,7},{9,8},{10,9},{11,1... | collective-permute-start | bytes 56 | tf_op jit(solution)/shard_map/ppermute | solution.py:375
  7.6 1.4 %shell.1 = (bf16[80,640]{1,0:T(8,128)(2,1)S(1)}, bf16[4,80,256]{2,1,0:T(8,128)(2,1)S(1)}) custom-call(s32[1,4]{1,0:T(1,128)} %pos_ref.3, s32[1,4]{1,0:T(1,128)} %rows_ref.3, bf16[77,4,256]{2,1,0:T(4,128)(2,1)} %bitcast.15, s32[1,256]{1,0:T(1,128)} %constant.7.clone.map_ref), custom_call_target="tpu_custom_call" | custom-call | tf_op jit(solution)/shard_map/shell/pallas_call | solution.py:376
  9.0 0.0 collective-permute-done.west_ref
  9.0 0.0 collective-permute-done.1.east_ref
  9.1 0.1 broadcast_in_dim.6
  9.1 0.0 copy-start.5
  9.1 0.0 copy-start.6
  9.1 15.7 %all_to_all.15.ga_ref = bf16[8,80,640]{2,1,0:T(8,128)(2,1)S(1)} all-to-all(bf16[8,80,640]{2,1,0:T(8,128)(2,1)S(1)} %broadcast_in_dim.6), channel_id=1, replica_groups={{0,16,32,48,64,80,96,112},{8,24,40,56,72,88,104,120},{1,17,33,49,65,81,..., dimensions={0} | all-to-all | bytes 1638400 | tf_op jit(solution)/shard_map/all_to_all | solution.py:391
  24.9 0.0 copy-start
  24.9 0.0 copy-start.1
  24.9 0.0 copy-start.2
  24.9 0.0 copy-start.3
  24.9 3.0 %collective-permute-start.2 = (bf16[8,80,640]{2,1,0:T(8,128)(2,1)S(1)}, bf16[8,80,640]{2,1,0:T(8,128)(2,1)S(1)}, u32[]{:S(2)}, u32[]{:S(2)}) collective-permute-start(bf16[8,80,640]{2,1,0:T(8,128)(2,1)S(1)} %all_to_all.15.ga_ref), channel_id=1, source_target_pairs={{0,8},{8,0},{16,24},{24,16},{32,40},{40,32},{48,56},{56,48},{64,72... | collective-permute-start | bytes 2457608 | tf_op jit(solution)/shard_map/ppermute | solution.py:394
  27.9 2.0 %collective-permute-done.2.gb_ref = bf16[8,80,640]{2,1,0:T(8,128)(2,1)S(1)} collective-permute-done((bf16[8,80,640]{2,1,0:T(8,128)(2,1)S(1)}, bf16[8,80,640]{2,1,0:T(8,128)(2,1)S(1)}, u32[]{:S(2)}, u32[]{:S(2)}) %collective-permute-start.2) | collective-permute-done | bytes 819232 | tf_op jit(solution)/shard_map/ppermute | solution.py:394
  29.8 0.0 copy-done.5
  29.8 0.0 copy-done.6
  29.8 0.0 copy-start.4
  29.8 3.8 %pick.1 = (bf16[2,288,80]{2,1,0:T(8,128)(2,1)S(1)}, bf16[8,48,80]{2,1,0:T(8,128)(2,1)S(1)}, bf16[288,80]{1,0:T(8,128)(2,1)S(1)}, bf16[288,80]{1,0:T(8,128)(2,1)S(1)}) custom-call(s32[1,4]{1,0:T(1,128)S(1)} %copy-done.6, s32[1,4]{1,0:T(1,128)S(1)} %collective-permute-done.1.east_ref, s32[1,4]{1,0:T(1,128)S(1)} %collective-permute-done.west_ref, ...), custom_call_target="tpu_custom_call" | custom-call | tf_op jit(solution)/shard_map/pick/pallas_call | solution.py:395
  33.6 0.1 collective-permute-start.3
  33.7 5.4 %collective-permute-start.4 = (bf16[288,80]{1,0:T(8,128)(2,1)S(1)}, bf16[288,80]{1,0:T(8,128)(2,1)S(1)}, u32[]{:S(2)}, u32[]{:S(2)}) collective-permute-start(bf16[288,80]{1,0:T(8,128)(2,1)S(1)} %get-tuple-element.28), channel_id=1, source_target_pairs={{1,0},{2,1},{3,2},{4,3},{5,4},{6,5},{7,6},{0,7},{9,8},{10,9},{11,1... | collective-permute-start | bytes 138248 | tf_op jit(solution)/shard_map/ppermute | solution.py:417
  39.1 2.2 %collective-permute-done.3.west_ref = bf16[288,80]{1,0:T(8,128)(2,1)S(1)} collective-permute-done((bf16[288,80]{1,0:T(8,128)(2,1)S(1)}, bf16[288,80]{1,0:T(8,128)(2,1)S(1)}, u32[]{:S(2)}, u32[]{:S(2)}) %collective-permute-start.3) | collective-permute-done | bytes 46112 | tf_op jit(solution)/shard_map/ppermute | solution.py:416
  41.3 0.0 collective-permute-done.4.east_ref
  41.3 0.0 copy-start.7
  41.3 0.0 copy-start.8
  41.3 0.0 copy-done
  41.3 0.0 copy-done.1
  41.3 0.0 copy-done.2
  41.3 0.0 copy-done.3
  41.3 0.0 copy-done.4
  41.4 0.6 copy-done.7
  42.0 0.0 copy-done.8
  42.0 15.4 %block.1 = (bf16[4,200,256]{2,1,0:T(8,128)(2,1)}, f32[64,24,128]{2,1,0:T(8,128)S(1)}, bf16[64,24,128]{2,1,0:T(8,128)(2,1)S(1)}) custom-call(s32[1,4]{1,0:T(1,128)S(1)} %copy-done.7, bf16[2,288,80]{2,1,0:T(8,128)(2,1)S(1)} %get-tuple-element.25.side_ref, bf16[8,48,80]{2,1,0:T(8,128)(2,1)S(1)} %get-tuple-element.26.band_ref, ...), custom_call_target="tpu_custom_call" | custom-call | tf_op jit(solution)/shard_map/block/pallas_call | solution.py:420
  57.4 0.9 collective-permute-start.5
  58.3 1.3 %collective-permute-done.5 = bf16[64,24,128]{2,1,0:T(8,128)(2,1)S(1)} collective-permute-done((bf16[64,24,128]{2,1,0:T(8,128)(2,1)S(1)}, bf16[64,24,128]{2,1,0:T(8,128)(2,1)S(1)}, u32[]{:S(2)}, u32[]{:S(2)}) %collective-permute-start.5) | collective-permute-done | bytes 393248 | tf_op jit(solution)/shard_map/ppermute | solution.py:453
  59.7 0.1 add_convert_fusion
  59.8 19.0 %all_to_all.16 = bf16[64,24,128]{2,1,0:T(8,128)(2,1)S(1)} all-to-all(bf16[64,24,128]{2,1,0:T(8,128)(2,1)S(1)} %add_convert_fusion), channel_id=1, replica_groups={{0,1,2,3,4,5,6,7,16,17,18,19,20,21,22,23,32,33,34,35,36,37,38,39,48,49,..., dimensions={0} | all-to-all | bytes 786432 | tf_op jit(solution)/shard_map/all_to_all | solution.py:456
  78.8 0.1 reduce_sum.12
  78.9 0.1 broadcast_in_dim.8
  78.9 14.5 %all_to_all.17.own_ref = bf16[64,24,128]{2,1,0:T(8,128)(2,1)S(1)} all-to-all(bf16[64,24,128]{2,1,0:T(8,128)(2,1)S(1)} %broadcast_in_dim.8), channel_id=1, replica_groups={{0,1,2,3,4,5,6,7,16,17,18,19,20,21,22,23,32,33,34,35,36,37,38,39,48,49,..., dimensions={0} | all-to-all | bytes 786432 | tf_op jit(solution)/shard_map/all_to_all | solution.py:460
  93.4 3.2 %collective-permute-start.6 = (bf16[64,24,128]{2,1,0:T(8,128)(2,1)S(1)}, bf16[64,24,128]{2,1,0:T(8,128)(2,1)S(1)}, u32[]{:S(2)}, u32[]{:S(2)}) collective-permute-start(bf16[64,24,128]{2,1,0:T(8,128)(2,1)S(1)} %all_to_all.17.own_ref), channel_id=1, source_target_pairs={{0,8},{8,0},{16,24},{24,16},{32,40},{40,32},{48,56},{56,48},{64,72... | collective-permute-start | bytes 1179656 | tf_op jit(solution)/shard_map/ppermute | solution.py:461
  96.7 1.3 %collective-permute-done.6.other_ref = bf16[64,24,128]{2,1,0:T(8,128)(2,1)S(1)} collective-permute-done((bf16[64,24,128]{2,1,0:T(8,128)(2,1)S(1)}, bf16[64,24,128]{2,1,0:T(8,128)(2,1)S(1)}, u32[]{:S(2)}, u32[]{:S(2)}) %collective-permute-start.6) | collective-permute-done | bytes 393248 | tf_op jit(solution)/shard_map/ppermute | solution.py:461
  98.0 1.3 %finish.1 = (f32[200,800]{1,0:T(8,128)}, f32[200,800]{1,0:T(8,128)}, f32[49,200]{1,0:T(8,128)}, f32[1,200]{1,0:T(1,128)}) custom-call(bf16[64,24,128]{2,1,0:T(8,128)(2,1)S(1)} %all_to_all.17.own_ref, bf16[64,24,128]{2,1,0:T(8,128)(2,1)S(1)} %collective-permute-done.6.other_ref), custom_call_target="tpu_custom_call" | custom-call | tf_op jit(solution)/shard_map/finish/pallas_call | solution.py:462
Async XLA Ops:
  0.6 8.4 %collective-permute-start = (s32[1,4]{1,0:T(1,128)}, s32[1,4]{1,0:T(1,128)S(1)}, u32[]{:S(2)}, u32[]{:S(2)}) collective-permute-start(s32[1,4]{1,0:T(1,128)} %pos_ref.3), channel_id=1, source_target_pairs={{0,1},{1,2},{2,3},{3,4},{4,5},{5,6},{6,7},{7,0},{8,9},{9,10},{10,1... | collective-permute-start | bytes 56 | tf_op jit(solution)/shard_map/ppermute | solution.py:374
  2.8 6.2 %collective-permute-start.1 = (s32[1,4]{1,0:T(1,128)}, s32[1,4]{1,0:T(1,128)S(1)}, u32[]{:S(2)}, u32[]{:S(2)}) collective-permute-start(s32[1,4]{1,0:T(1,128)} %pos_ref.3), channel_id=1, source_target_pairs={{1,0},{2,1},{3,2},{4,3},{5,4},{6,5},{7,6},{0,7},{9,8},{10,9},{11,1... | collective-permute-start | bytes 56 | tf_op jit(solution)/shard_map/ppermute | solution.py:375
  9.1 20.7 %copy-start.5 = (s32[72,128]{1,0:T(8,128)S(1)}, s32[72,128]{1,0:T(8,128)}, u32[]{:S(2)}) copy-start(s32[72,128]{1,0:T(8,128)} %constant.8.clone.src_ref) | copy-start | bytes 110596
  9.1 20.7 %copy-start.6 = (s32[1,4]{1,0:T(1,128)S(1)}, s32[1,4]{1,0:T(1,128)}, u32[]{:S(2)}) copy-start(s32[1,4]{1,0:T(1,128)} %pos_ref.3) | copy-start | bytes 52
  24.9 16.4 %copy-start = (bf16[1,4,200,256]{3,2,1,0:T(8,128)(2,1)S(1)}, bf16[1,4,200,256]{3,2,1,0:T(8,128)(2,1)}, u32[]{:S(2)}) copy-start(bf16[1,4,200,256]{3,2,1,0:T(8,128)(2,1)} %param.19) | copy-start | bytes 1228804
  24.9 16.4 %copy-start.1 = (bf16[200,800]{1,0:T(8,128)(2,1)S(1)}, bf16[200,800]{1,0:T(8,128)(2,1)}, u32[]{:S(2)}) copy-start(bf16[200,800]{1,0:T(8,128)(2,1)} %wi_ref.1) | copy-start | bytes 960004
  24.9 16.4 %copy-start.2 = (bf16[800,200]{0,1:T(8,128)(2,1)S(1)}, bf16[800,200]{0,1:T(8,128)(2,1)}, u32[]{:S(2)}) copy-start(bf16[800,200]{0,1:T(8,128)(2,1)} %param.18) | copy-start | bytes 960004
  24.9 16.5 %copy-start.3 = (f32[200,49]{0,1:T(8,128)S(1)}, f32[200,49]{0,1:T(8,128)}, u32[]{:S(2)}) copy-start(f32[200,49]{0,1:T(8,128)} %param.15) | copy-start | bytes 117604
  24.9 4.9 %collective-permute-start.2 = (bf16[8,80,640]{2,1,0:T(8,128)(2,1)S(1)}, bf16[8,80,640]{2,1,0:T(8,128)(2,1)S(1)}, u32[]{:S(2)}, u32[]{:S(2)}) collective-permute-start(bf16[8,80,640]{2,1,0:T(8,128)(2,1)S(1)} %all_to_all.15.ga_ref), channel_id=1, source_target_pairs={{0,8},{8,0},{16,24},{24,16},{32,40},{40,32},{48,56},{56,48},{64,72... | collective-permute-start | bytes 2457608 | tf_op jit(solution)/shard_map/ppermute | solution.py:394
  29.8 11.5 %copy-start.4 = (bf16[77,200]{1,0:T(8,128)(2,1)S(1)}, bf16[77,200]{1,0:T(8,128)(2,1)}, u32[]{:S(2)}) copy-start(bf16[77,200]{1,0:T(8,128)(2,1)} %sw_ref.1) | copy-start | bytes 92404
  33.6 7.7 %collective-permute-start.3 = (bf16[288,80]{1,0:T(8,128)(2,1)S(1)}, bf16[288,80]{1,0:T(8,128)(2,1)S(1)}, u32[]{:S(2)}, u32[]{:S(2)}) collective-permute-start(bf16[288,80]{1,0:T(8,128)(2,1)S(1)} %get-tuple-element.27), channel_id=1, source_target_pairs={{0,1},{1,2},{2,3},{3,4},{4,5},{5,6},{6,7},{7,0},{8,9},{9,10},{10,1... | collective-permute-start | bytes 138248 | tf_op jit(solution)/shard_map/ppermute | solution.py:416
  33.7 7.6 %collective-permute-start.4 = (bf16[288,80]{1,0:T(8,128)(2,1)S(1)}, bf16[288,80]{1,0:T(8,128)(2,1)S(1)}, u32[]{:S(2)}, u32[]{:S(2)}) collective-permute-start(bf16[288,80]{1,0:T(8,128)(2,1)S(1)} %get-tuple-element.28), channel_id=1, source_target_pairs={{1,0},{2,1},{3,2},{4,3},{5,4},{6,5},{7,6},{0,7},{9,8},{10,9},{11,1... | collective-permute-start | bytes 138248 | tf_op jit(solution)/shard_map/ppermute | solution.py:417
  41.3 0.7 copy-start.7
  41.3 0.7 copy-start.8
  57.4 2.3 %collective-permute-start.5 = (bf16[64,24,128]{2,1,0:T(8,128)(2,1)S(1)}, bf16[64,24,128]{2,1,0:T(8,128)(2,1)S(1)}, u32[]{:S(2)}, u32[]{:S(2)}) collective-permute-start(bf16[64,24,128]{2,1,0:T(8,128)(2,1)S(1)} %get-tuple-element.32), channel_id=1, source_target_pairs={{0,8},{8,0},{16,24},{24,16},{32,40},{40,32},{48,56},{56,48},{64,72... | collective-permute-start | bytes 1179656 | tf_op jit(solution)/shard_map/ppermute | solution.py:453
  93.4 4.6 %collective-permute-start.6 = (bf16[64,24,128]{2,1,0:T(8,128)(2,1)S(1)}, bf16[64,24,128]{2,1,0:T(8,128)(2,1)S(1)}, u32[]{:S(2)}, u32[]{:S(2)}) collective-permute-start(bf16[64,24,128]{2,1,0:T(8,128)(2,1)S(1)} %all_to_all.17.own_ref), channel_id=1, source_target_pairs={{0,8},{8,0},{16,24},{24,16},{32,40},{40,32},{48,56},{56,48},{64,72... | collective-permute-start | bytes 1179656 | tf_op jit(solution)/shard_map/ppermute | solution.py:461

commit v3 on v2

--- a/solution.py
+++ b/solution.py
@@ -85,8 +85,8 @@
 
 
 def pick_kernel(
-    pos_ref, east_ref, west_ref, ga_ref, gb_ref, src_ref,
-    side_ref, band_ref, to_east_ref, to_west_ref,
+    pos_ref, first_pos_ref, second_pos_ref, ga_ref, gb_ref, src_ref,
+    side_ref, band_ref, first_ref, second_ref,
     pm, tv, sm, ts, sem, gaps,
 ):
     for g in range(GROUP):
@@ -98,6 +98,8 @@
     label = jnp.where(lane % SHELL == 0, pm[...], -1.0)
     code = (slot * 1024 + lane + 1).astype(F32)
     tv[...] = jnp.zeros_like(tv)
+    odd = lax.axis_index("lon") % 2
+    near_edge = odd * (COLS - 1)
 
     def ask(entry, want):
         hit = jnp.where(label == want.astype(F32), code, 0.0)
@@ -114,7 +116,7 @@
             nrow, ncol = row + dr, col + dc
             inside = (nrow >= 0) & (nrow < TILE_ROWS) & (ncol >= 0) & (ncol < COLS)
             ask(a * 8 + n, jnp.where(inside, nrow * COLS + ncol, -7))
-        for first, ref, edge in ((32, east_ref, 0), (48, west_ref, COLS - 1)):
+        for first, ref, edge in ((32, first_pos_ref, near_edge), (48, second_pos_ref, COLS - 1 - near_edge)):
             q = ref[0, a]
             row, col = q // COLS, q % COLS
             for dr in (-1, 0, 1):
@@ -151,7 +153,7 @@
             side_ref[side, rows, :] = (parts[0] + parts[1] + parts[2]).astype(BF16)
         band_ref[2 * a] = take(a * 8 + order[-1, 0], 6, PIECE).astype(BF16)
         band_ref[2 * a + 1] = take(a * 8 + order[1, 0], 7, PIECE).astype(BF16)
-        for side, first, ref in ((0, 32, to_east_ref), (1, 48, to_west_ref)):
+        for side, first, ref in ((odd, 32, first_ref), (1 - odd, 48, second_ref)):
             parts = [take(first + a * 4 + dr + 1, 3 * side + dr + 1, STRIP) for dr in (-1, 0, 1)]
             ref[rows, :] = (parts[0] + parts[1] + parts[2]).astype(BF16)
 
@@ -166,7 +168,7 @@
 
 
 def main_kernel(
-    rows_ref, side_ref, band_ref, west_ref, east_ref, x_ref, sw_ref, dw_ref, gain_ref, wi_ref, wo_ref, cot_ref,
+    rows_ref, side_ref, band_ref, first_ref, second_ref, x_ref, sw_ref, dw_ref, gain_ref, wi_ref, wo_ref, cot_ref,
     out_ref, own_ref, send_ref,
     swp, dwt, gnp, wide, wit, wot, pt, cv, un, iv, ft, mg, hs, gps, gf, gc, si, so,
 ):
@@ -199,8 +201,10 @@
         for b in range(HB):
             dst[b * HALF : (b + 1) * HALF, :] = wide[:, b * HALF : (b + 1) * HALF].T.astype(BF16)
 
-    for side, (ref, xx) in enumerate(((west_ref, 0), (east_ref, 19))):
-        cells = (side_ref[side].astype(F32) + ref[...].astype(F32)).astype(BF16)
+    odd = lax.axis_index("lon") % 2 == 1
+    for side, (even_ref, odd_ref, xx) in enumerate(((second_ref, first_ref, 0), (first_ref, second_ref, 19))):
+        arrived = jnp.where(odd, odd_ref[...].astype(F32), even_ref[...].astype(F32))
+        cells = (side_ref[side].astype(F32) + arrived).astype(BF16)
         rows = jnp.dot(cells, swp[...], preferred_element_type=F32).astype(BF16).astype(F32)
         for h in range(2):
             for a in range(A_DEV):
@@ -364,15 +368,19 @@
     return pltpu.with_memory_space_constraint(value, pltpu.VMEM)
 
 
+def in_hbm(value):
+    return pltpu.with_memory_space_constraint(value, pltpu.HBM)
+
+
 def body(x_tiles, tile_pos, valid_rows, stem_w, dw_kernel, norm_gain, w_in, w_out, cotangent):
     smem = pl.BlockSpec(memory_space=pltpu.SMEM)
     vmem = pl.BlockSpec(memory_space=pltpu.VMEM)
     lon = lax.axis_size("lon")
     lat = lax.axis_size("lat")
-    eastward = [(i, (i + 1) % lon) for i in range(lon)]
-    westward = [((i + 1) % lon, i) for i in range(lon)]
-    pos_west = lax.ppermute(tile_pos, "lon", eastward)
-    pos_east = lax.ppermute(tile_pos, "lon", westward)
+    first_pair = [(i, i ^ 1) for i in range(lon)]
+    second_pair = [(i, (i + 1 if i % 2 else i - 1) % lon) for i in range(lon)]
+    pos_second = lax.ppermute(tile_pos, "lon", second_pair)
+    pos_first = lax.ppermute(tile_pos, "lon", first_pair)
     shell, inputs = pl.pallas_call(
         shell_kernel,
         out_shape=(pltpu.VMEM((KPAD, PAY), BF16), pltpu.VMEM((A_DEV, KPAD, TT), BF16)),
@@ -385,14 +393,14 @@
         ],
         name="shell",
     )(tile_pos, valid_rows, x_tiles[0].transpose(1, 0, 2), jnp.asarray(shell_cells()))
-    shell, pos_west, pos_east = lax.optimization_barrier((shell, pos_west, pos_east))
+    shell, pos_first, pos_second = lax.optimization_barrier((shell, pos_first, pos_second))
     same_core = [[i for i in range(c, lat, 2)] for c in range(2)]
     siblings = [(i, i ^ 1) for i in range(lat)]
     mine = lax.all_to_all(
         jnp.broadcast_to(shell[None], (GROUP, KPAD, PAY)), "lat", 0, 0, axis_index_groups=same_core, tiled=True
     )
     theirs = lax.ppermute(mine, "lat", siblings)
-    side, band, to_east, to_west = pl.pallas_call(
+    side, band, to_first, to_second = pl.pallas_call(
         pick_kernel,
         out_shape=(
             pltpu.VMEM((2, A_DEV * STRIP, KPAD), BF16),
@@ -412,9 +420,9 @@
         ],
         compiler_params=pltpu.CompilerParams(vmem_limit_bytes=16 << 20),
         name="pick",
-    )(tile_pos, pos_east, pos_west, on_chip(mine), on_chip(theirs), jnp.asarray(strip_sources()))
-    from_west = lax.ppermute(to_east, "lon", eastward)
-    from_east = lax.ppermute(to_west, "lon", westward)
+    )(tile_pos, pos_first, pos_second, on_chip(mine), on_chip(theirs), jnp.asarray(strip_sources()))
+    from_second = lax.ppermute(to_second, "lon", second_pair)
+    from_first = lax.ppermute(to_first, "lon", first_pair)
 
     cells = A_DEV * TT
     out_tiles, own, send = pl.pallas_call(
@@ -448,7 +456,7 @@
         ],
         compiler_params=pltpu.CompilerParams(vmem_limit_bytes=32 << 20),
         name="block",
-    )(valid_rows, side, band, on_chip(from_west), on_chip(from_east), inputs, stem_w, dw_kernel.T, norm_gain.reshape(1, C), w_in, w_out.T, cotangent[0])
+    )(in_hbm(valid_rows), side, band, on_chip(from_first), on_chip(from_second), inputs, stem_w, dw_kernel.T, norm_gain.reshape(1, C), w_in, w_out.T, cotangent[0])
 
     arrived = lax.ppermute(send, "lat", siblings)
     chip_sum = (own + arrived.astype(F32)).astype(BF16)

time: 99.6 us -> 99.8 us (level)
  starting transfers between devices: 19.7 us -> 20.8 us
where the time goes in v3:
time: 99.8 us; the launch traced here: 99.5 us
  blocking collectives  48.6 us (49%)
  Pallas kernels  21.9 us (22%)
  starting transfers between devices  20.8 us (21%)
  waiting for transfers between devices  6.51 us (7%)
    all_to_all x1, blocking collectives, body(): lax.all_to_all(chip_sum, ('lat', 'lon'), 0, 0, axis_index_groups=every, t...  18.4 us
    all_to_all x1, blocking collectives, body(): lax.all_to_all(jnp.broadcast_to(shell[None], (GROUP, KPAD, PAY)), 'lat',...  15.7 us
    pallas_call x1, Pallas kernels, body(): pl.pallas_call(main_kernel, out_shape=(jax.ShapeDtypeStruct((A_DEV, C, TT...  15.5 us
    all_to_all x1, blocking collectives, body(): lax.all_to_all(spread, ('lat', 'lon'), 0, 0, axis_index_groups=every, til...  14.5 us
    ppermute x1, starting transfers between devices, body(): pos_second = lax.ppermute(tile_pos, 'lon', second_pair)  5.21 us
    ppermute x1, starting transfers between devices, body(): from_second = lax.ppermute(to_second, 'lon', second_pair)  5.05 us
    pallas_call x1, Pallas kernels, body(): pl.pallas_call(pick_kernel, out_shape=(pltpu.VMEM((2, A_DEV * STRIP, KPAD...  3.75 us
    ppermute x1, starting transfers between devices, body(): theirs = lax.ppermute(mine, 'lat', siblings)  3.45 us
  transfers between devices with their start and end apart: 7, of which 4 were waited for; matrix products, arithmetic and copies ran while one was open for 0% of the time, Pallas kernels for 1%

profile of v3, /device:TPU:1, one launch (start us, length us, event | category | flops | bytes accessed | tf_op | source)
XLA Modules:
  0.0 99.5 jit_solution(15484385823935126705)
XLA Ops:
  0.6 2.2 %collective-permute-start = (s32[1,4]{1,0:T(1,128)}, s32[1,4]{1,0:T(1,128)S(1)}, u32[]{:S(2)}, u32[]{:S(2)}) collective-permute-start(s32[1,4]{1,0:T(1,128)} %pos_ref.3), channel_id=1, source_target_pairs={{0,1},{1,0},{2,3},{3,2},{4,5},{5,4},{6,7},{7,6},{8,9},{9,8},{10,11... | collective-permute-start | bytes 56 | tf_op jit(solution)/shard_map/ppermute | solution.py:383
  2.8 5.2 %collective-permute-start.1 = (s32[1,4]{1,0:T(1,128)}, s32[1,4]{1,0:T(1,128)S(1)}, u32[]{:S(2)}, u32[]{:S(2)}) collective-permute-start(s32[1,4]{1,0:T(1,128)} %pos_ref.3), channel_id=1, source_target_pairs={{0,7},{1,2},{2,1},{3,4},{4,3},{5,6},{6,5},{7,0},{8,15},{9,10},{10,... | collective-permute-start | bytes 56 | tf_op jit(solution)/shard_map/ppermute | solution.py:382
  8.0 1.4 %shell.1 = (bf16[80,640]{1,0:T(8,128)(2,1)S(1)}, bf16[4,80,256]{2,1,0:T(8,128)(2,1)S(1)}) custom-call(s32[1,4]{1,0:T(1,128)} %pos_ref.3, s32[1,4]{1,0:T(1,128)} %rows_ref.3, bf16[77,4,256]{2,1,0:T(4,128)(2,1)} %bitcast.15, s32[1,256]{1,0:T(1,128)} %constant.7.clone.map_ref), custom_call_target="tpu_custom_call" | custom-call | tf_op jit(solution)/shard_map/shell/pallas_call | solution.py:384
  9.4 0.0 collective-permute-done.first_pos_ref
  9.4 0.0 collective-permute-done.1.second_pos_ref
  9.4 0.1 broadcast_in_dim.6
  9.5 0.0 copy-start.5
  9.5 0.0 copy-start.6
  9.5 15.7 %all_to_all.15.ga_ref = bf16[8,80,640]{2,1,0:T(8,128)(2,1)S(1)} all-to-all(bf16[8,80,640]{2,1,0:T(8,128)(2,1)S(1)} %broadcast_in_dim.6), channel_id=1, replica_groups={{0,16,32,48,64,80,96,112},{8,24,40,56,72,88,104,120},{1,17,33,49,65,81,..., dimensions={0} | all-to-all | bytes 1638400 | tf_op jit(solution)/shard_map/all_to_all | solution.py:399
  25.2 0.0 copy-start
  25.2 0.0 copy-start.1
  25.2 0.0 copy-start.2
  25.2 0.0 copy-start.3
  25.3 3.5 %collective-permute-start.2 = (bf16[8,80,640]{2,1,0:T(8,128)(2,1)S(1)}, bf16[8,80,640]{2,1,0:T(8,128)(2,1)S(1)}, u32[]{:S(2)}, u32[]{:S(2)}) collective-permute-start(bf16[8,80,640]{2,1,0:T(8,128)(2,1)S(1)} %all_to_all.15.ga_ref), channel_id=1, source_target_pairs={{0,8},{8,0},{16,24},{24,16},{32,40},{40,32},{48,56},{56,48},{64,72... | collective-permute-start | bytes 2457608 | tf_op jit(solution)/shard_map/ppermute | solution.py:402
  28.7 2.0 %collective-permute-done.2.gb_ref = bf16[8,80,640]{2,1,0:T(8,128)(2,1)S(1)} collective-permute-done((bf16[8,80,640]{2,1,0:T(8,128)(2,1)S(1)}, bf16[8,80,640]{2,1,0:T(8,128)(2,1)S(1)}, u32[]{:S(2)}, u32[]{:S(2)}) %collective-permute-start.2) | collective-permute-done | bytes 819232 | tf_op jit(solution)/shard_map/ppermute | solution.py:402
  30.7 0.0 copy-done.5
  30.7 0.0 copy-done.6
  30.7 0.0 copy-start.4
  30.7 3.8 %pick.1 = (bf16[2,288,80]{2,1,0:T(8,128)(2,1)S(1)}, bf16[8,48,80]{2,1,0:T(8,128)(2,1)S(1)}, bf16[288,80]{1,0:T(8,128)(2,1)S(1)}, bf16[288,80]{1,0:T(8,128)(2,1)S(1)}) custom-call(s32[1,4]{1,0:T(1,128)S(1)} %copy-done.6, s32[1,4]{1,0:T(1,128)S(1)} %collective-permute-done.first_pos_ref, s32[1,4]{1,0:T(1,128)S(1)} %collective-permute-done.1.second_pos_ref, ...), custom_call_target="tpu_custom_call" | custom-call | tf_op jit(solution)/shard_map/pick/pallas_call | solution.py:403
  34.4 0.1 collective-permute-start.3
  34.5 5.1 %collective-permute-start.4 = (bf16[288,80]{1,0:T(8,128)(2,1)S(1)}, bf16[288,80]{1,0:T(8,128)(2,1)S(1)}, u32[]{:S(2)}, u32[]{:S(2)}) collective-permute-start(bf16[288,80]{1,0:T(8,128)(2,1)S(1)} %get-tuple-element.28), channel_id=1, source_target_pairs={{0,7},{1,2},{2,1},{3,4},{4,3},{5,6},{6,5},{7,0},{8,15},{9,10},{10,... | collective-permute-start | bytes 138248 | tf_op jit(solution)/shard_map/ppermute | solution.py:424
  39.6 0.0 collective-permute-done.3.first_ref
  39.6 1.8 %collective-permute-done.4.second_ref = bf16[288,80]{1,0:T(8,128)(2,1)S(1)} collective-permute-done((bf16[288,80]{1,0:T(8,128)(2,1)S(1)}, bf16[288,80]{1,0:T(8,128)(2,1)S(1)}, u32[]{:S(2)}, u32[]{:S(2)}) %collective-permute-start.4) | collective-permute-done | bytes 46112 | tf_op jit(solution)/shard_map/ppermute | solution.py:424
  41.4 0.0 copy-start.7
  41.4 0.0 copy-done
  41.4 0.0 copy-done.1
  41.4 0.0 copy-done.2
  41.4 0.0 copy-done.3
  41.4 0.0 copy-done.4
  41.5 0.6 copy-done.7
  42.1 15.5 %block.1 = (bf16[4,200,256]{2,1,0:T(8,128)(2,1)}, f32[64,24,128]{2,1,0:T(8,128)S(1)}, bf16[64,24,128]{2,1,0:T(8,128)(2,1)S(1)}) custom-call(s32[1,4]{1,0:T(1,128)} %rows_ref.3, bf16[2,288,80]{2,1,0:T(8,128)(2,1)S(1)} %get-tuple-element.25.side_ref, bf16[8,48,80]{2,1,0:T(8,128)(2,1)S(1)} %get-tuple-element.26.band_ref, ...), custom_call_target="tpu_custom_call" | custom-call | tf_op jit(solution)/shard_map/block/pallas_call | solution.py:428
  57.6 1.5 %collective-permute-start.5 = (bf16[64,24,128]{2,1,0:T(8,128)(2,1)S(1)}, bf16[64,24,128]{2,1,0:T(8,128)(2,1)S(1)}, u32[]{:S(2)}, u32[]{:S(2)}) collective-permute-start(bf16[64,24,128]{2,1,0:T(8,128)(2,1)S(1)} %get-tuple-element.32), channel_id=1, source_target_pairs={{0,8},{8,0},{16,24},{24,16},{32,40},{40,32},{48,56},{56,48},{64,72... | collective-permute-start | bytes 1179656 | tf_op jit(solution)/shard_map/ppermute | solution.py:461
  59.1 1.3 %collective-permute-done.5 = bf16[64,24,128]{2,1,0:T(8,128)(2,1)S(1)} collective-permute-done((bf16[64,24,128]{2,1,0:T(8,128)(2,1)S(1)}, bf16[64,24,128]{2,1,0:T(8,128)(2,1)S(1)}, u32[]{:S(2)}, u32[]{:S(2)}) %collective-permute-start.5) | collective-permute-done | bytes 393248 | tf_op jit(solution)/shard_map/ppermute | solution.py:461
  60.4 0.1 add_convert_fusion
  60.5 18.4 %all_to_all.16 = bf16[64,24,128]{2,1,0:T(8,128)(2,1)S(1)} all-to-all(bf16[64,24,128]{2,1,0:T(8,128)(2,1)S(1)} %add_convert_fusion), channel_id=1, replica_groups={{0,1,2,3,4,5,6,7,16,17,18,19,20,21,22,23,32,33,34,35,36,37,38,39,48,49,..., dimensions={0} | all-to-all | bytes 786432 | tf_op jit(solution)/shard_map/all_to_all | solution.py:464
  79.0 0.1 reduce_sum.12
  79.1 0.1 broadcast_in_dim.8
  79.1 14.5 %all_to_all.17.own_ref = bf16[64,24,128]{2,1,0:T(8,128)(2,1)S(1)} all-to-all(bf16[64,24,128]{2,1,0:T(8,128)(2,1)S(1)} %broadcast_in_dim.8), channel_id=1, replica_groups={{0,1,2,3,4,5,6,7,16,17,18,19,20,21,22,23,32,33,34,35,36,37,38,39,48,49,..., dimensions={0} | all-to-all | bytes 786432 | tf_op jit(solution)/shard_map/all_to_all | solution.py:468
  93.6 3.2 %collective-permute-start.6 = (bf16[64,24,128]{2,1,0:T(8,128)(2,1)S(1)}, bf16[64,24,128]{2,1,0:T(8,128)(2,1)S(1)}, u32[]{:S(2)}, u32[]{:S(2)}) collective-permute-start(bf16[64,24,128]{2,1,0:T(8,128)(2,1)S(1)} %all_to_all.17.own_ref), channel_id=1, source_target_pairs={{0,8},{8,0},{16,24},{24,16},{32,40},{40,32},{48,56},{56,48},{64,72... | collective-permute-start | bytes 1179656 | tf_op jit(solution)/shard_map/ppermute | solution.py:469
  96.9 1.3 %collective-permute-done.6.other_ref = bf16[64,24,128]{2,1,0:T(8,128)(2,1)S(1)} collective-permute-done((bf16[64,24,128]{2,1,0:T(8,128)(2,1)S(1)}, bf16[64,24,128]{2,1,0:T(8,128)(2,1)S(1)}, u32[]{:S(2)}, u32[]{:S(2)}) %collective-permute-start.6) | collective-permute-done | bytes 393248 | tf_op jit(solution)/shard_map/ppermute | solution.py:469
  98.2 1.3 %finish.1 = (f32[200,800]{1,0:T(8,128)}, f32[200,800]{1,0:T(8,128)}, f32[49,200]{1,0:T(8,128)}, f32[1,200]{1,0:T(1,128)}) custom-call(bf16[64,24,128]{2,1,0:T(8,128)(2,1)S(1)} %all_to_all.17.own_ref, bf16[64,24,128]{2,1,0:T(8,128)(2,1)S(1)} %collective-permute-done.6.other_ref), custom_call_target="tpu_custom_call" | custom-call | tf_op jit(solution)/shard_map/finish/pallas_call | solution.py:470
Async XLA Ops:
  0.6 8.8 %collective-permute-start = (s32[1,4]{1,0:T(1,128)}, s32[1,4]{1,0:T(1,128)S(1)}, u32[]{:S(2)}, u32[]{:S(2)}) collective-permute-start(s32[1,4]{1,0:T(1,128)} %pos_ref.3), channel_id=1, source_target_pairs={{0,1},{1,0},{2,3},{3,2},{4,5},{5,4},{6,7},{7,6},{8,9},{9,8},{10,11... | collective-permute-start | bytes 56 | tf_op jit(solution)/shard_map/ppermute | solution.py:383
  2.8 6.6 %collective-permute-start.1 = (s32[1,4]{1,0:T(1,128)}, s32[1,4]{1,0:T(1,128)S(1)}, u32[]{:S(2)}, u32[]{:S(2)}) collective-permute-start(s32[1,4]{1,0:T(1,128)} %pos_ref.3), channel_id=1, source_target_pairs={{0,7},{1,2},{2,1},{3,4},{4,3},{5,6},{6,5},{7,0},{8,15},{9,10},{10,... | collective-permute-start | bytes 56 | tf_op jit(solution)/shard_map/ppermute | solution.py:382
  9.5 21.2 %copy-start.5 = (s32[72,128]{1,0:T(8,128)S(1)}, s32[72,128]{1,0:T(8,128)}, u32[]{:S(2)}) copy-start(s32[72,128]{1,0:T(8,128)} %constant.8.clone.src_ref) | copy-start | bytes 110596
  9.5 21.1 %copy-start.6 = (s32[1,4]{1,0:T(1,128)S(1)}, s32[1,4]{1,0:T(1,128)}, u32[]{:S(2)}) copy-start(s32[1,4]{1,0:T(1,128)} %pos_ref.3) | copy-start | bytes 52
  25.2 16.2 %copy-start = (bf16[1,4,200,256]{3,2,1,0:T(8,128)(2,1)S(1)}, bf16[1,4,200,256]{3,2,1,0:T(8,128)(2,1)}, u32[]{:S(2)}) copy-start(bf16[1,4,200,256]{3,2,1,0:T(8,128)(2,1)} %param.19) | copy-start | bytes 1228804
  25.2 16.2 %copy-start.1 = (bf16[200,800]{1,0:T(8,128)(2,1)S(1)}, bf16[200,800]{1,0:T(8,128)(2,1)}, u32[]{:S(2)}) copy-start(bf16[200,800]{1,0:T(8,128)(2,1)} %wi_ref.1) | copy-start | bytes 960004
  25.2 16.2 %copy-start.2 = (bf16[800,200]{0,1:T(8,128)(2,1)S(1)}, bf16[800,200]{0,1:T(8,128)(2,1)}, u32[]{:S(2)}) copy-start(bf16[800,200]{0,1:T(8,128)(2,1)} %param.18) | copy-start | bytes 960004
  25.2 16.2 %copy-start.3 = (f32[200,49]{0,1:T(8,128)S(1)}, f32[200,49]{0,1:T(8,128)}, u32[]{:S(2)}) copy-start(f32[200,49]{0,1:T(8,128)} %param.15) | copy-start | bytes 117604
  25.3 5.4 %collective-permute-start.2 = (bf16[8,80,640]{2,1,0:T(8,128)(2,1)S(1)}, bf16[8,80,640]{2,1,0:T(8,128)(2,1)S(1)}, u32[]{:S(2)}, u32[]{:S(2)}) collective-permute-start(bf16[8,80,640]{2,1,0:T(8,128)(2,1)S(1)} %all_to_all.15.ga_ref), channel_id=1, source_target_pairs={{0,8},{8,0},{16,24},{24,16},{32,40},{40,32},{48,56},{56,48},{64,72... | collective-permute-start | bytes 2457608 | tf_op jit(solution)/shard_map/ppermute | solution.py:402
  30.7 10.8 %copy-start.4 = (bf16[77,200]{1,0:T(8,128)(2,1)S(1)}, bf16[77,200]{1,0:T(8,128)(2,1)}, u32[]{:S(2)}) copy-start(bf16[77,200]{1,0:T(8,128)(2,1)} %sw_ref.1) | copy-start | bytes 92404
  34.4 5.1 %collective-permute-start.3 = (bf16[288,80]{1,0:T(8,128)(2,1)S(1)}, bf16[288,80]{1,0:T(8,128)(2,1)S(1)}, u32[]{:S(2)}, u32[]{:S(2)}) collective-permute-start(bf16[288,80]{1,0:T(8,128)(2,1)S(1)} %get-tuple-element.27), channel_id=1, source_target_pairs={{0,1},{1,0},{2,3},{3,2},{4,5},{5,4},{6,7},{7,6},{8,9},{9,8},{10,11... | collective-permute-start | bytes 138248 | tf_op jit(solution)/shard_map/ppermute | solution.py:425
  34.5 6.9 %collective-permute-start.4 = (bf16[288,80]{1,0:T(8,128)(2,1)S(1)}, bf16[288,80]{1,0:T(8,128)(2,1)S(1)}, u32[]{:S(2)}, u32[]{:S(2)}) collective-permute-start(bf16[288,80]{1,0:T(8,128)(2,1)S(1)} %get-tuple-element.28), channel_id=1, source_target_pairs={{0,7},{1,2},{2,1},{3,4},{4,3},{5,6},{6,5},{7,0},{8,15},{9,10},{10,... | collective-permute-start | bytes 138248 | tf_op jit(solution)/shard_map/ppermute | solution.py:424
  41.4 0.7 copy-start.7
  57.6 2.9 %collective-permute-start.5 = (bf16[64,24,128]{2,1,0:T(8,128)(2,1)S(1)}, bf16[64,24,128]{2,1,0:T(8,128)(2,1)S(1)}, u32[]{:S(2)}, u32[]{:S(2)}) collective-permute-start(bf16[64,24,128]{2,1,0:T(8,128)(2,1)S(1)} %get-tuple-element.32), channel_id=1, source_target_pairs={{0,8},{8,0},{16,24},{24,16},{32,40},{40,32},{48,56},{56,48},{64,72... | collective-permute-start | bytes 1179656 | tf_op jit(solution)/shard_map/ppermute | solution.py:461
  93.6 4.6 %collective-permute-start.6 = (bf16[64,24,128]{2,1,0:T(8,128)(2,1)S(1)}, bf16[64,24,128]{2,1,0:T(8,128)(2,1)S(1)}, u32[]{:S(2)}, u32[]{:S(2)}) collective-permute-start(bf16[64,24,128]{2,1,0:T(8,128)(2,1)S(1)} %all_to_all.17.own_ref), channel_id=1, source_target_pairs={{0,8},{8,0},{16,24},{24,16},{32,40},{40,32},{48,56},{56,48},{64,72... | collective-permute-start | bytes 1179656 | tf_op jit(solution)/shard_map/ppermute | solution.py:469

commit v4 on v3

--- a/solution.py
+++ b/solution.py
@@ -85,8 +85,8 @@
 
 
 def pick_kernel(
-    pos_ref, first_pos_ref, second_pos_ref, ga_ref, gb_ref, src_ref,
-    side_ref, band_ref, first_ref, second_ref,
+    pos_ref, far_pos_ref, ga_ref, gb_ref, src_ref,
+    side_ref, band_ref, give_ref,
     pm, tv, sm, ts, sem, gaps,
 ):
     for g in range(GROUP):
@@ -98,7 +98,7 @@
     label = jnp.where(lane % SHELL == 0, pm[...], -1.0)
     code = (slot * 1024 + lane + 1).astype(F32)
     tv[...] = jnp.zeros_like(tv)
-    odd = lax.axis_index("lon") % 2
+    odd = lax.axis_index("lat") % 2
     near_edge = odd * (COLS - 1)
 
     def ask(entry, want):
@@ -116,12 +116,12 @@
             nrow, ncol = row + dr, col + dc
             inside = (nrow >= 0) & (nrow < TILE_ROWS) & (ncol >= 0) & (ncol < COLS)
             ask(a * 8 + n, jnp.where(inside, nrow * COLS + ncol, -7))
-        for first, ref, edge in ((32, first_pos_ref, near_edge), (48, second_pos_ref, COLS - 1 - near_edge)):
-            q = ref[0, a]
+        for first, i in ((32, 0), (48, 1)):
+            q = far_pos_ref[i, a]
             row, col = q // COLS, q % COLS
             for dr in (-1, 0, 1):
-                inside = (row + dr >= 0) & (row + dr < TILE_ROWS) & (col == edge)
-                ask(first + a * 4 + dr + 1, jnp.where(inside, (row + dr) * COLS + COLS - 1 - edge, -7))
+                inside = (row + dr >= 0) & (row + dr < TILE_ROWS) & (col == near_edge)
+                ask(first + a * 4 + dr + 1, jnp.where(inside, (row + dr) * COLS + COLS - 1 - near_edge, -7))
     total = jnp.sum(tv[...], axis=1, keepdims=True)
     sm[...] = jnp.broadcast_to(total, (64, HALF)).astype(jnp.int32)
     tcopy = pltpu.make_async_copy(sm, ts, sem)
@@ -153,9 +153,9 @@
             side_ref[side, rows, :] = (parts[0] + parts[1] + parts[2]).astype(BF16)
         band_ref[2 * a] = take(a * 8 + order[-1, 0], 6, PIECE).astype(BF16)
         band_ref[2 * a + 1] = take(a * 8 + order[1, 0], 7, PIECE).astype(BF16)
-        for side, first, ref in ((odd, 32, first_ref), (1 - odd, 48, second_ref)):
-            parts = [take(first + a * 4 + dr + 1, 3 * side + dr + 1, STRIP) for dr in (-1, 0, 1)]
-            ref[rows, :] = (parts[0] + parts[1] + parts[2]).astype(BF16)
+        for i, first in ((0, 32), (1, 48)):
+            parts = [take(first + a * 4 + dr + 1, 3 * odd + dr + 1, STRIP) for dr in (-1, 0, 1)]
+            give_ref[i, rows, :] = (parts[0] + parts[1] + parts[2]).astype(BF16)
 
 
 def gelu_parts(v):
@@ -168,7 +168,7 @@
 
 
 def main_kernel(
-    rows_ref, side_ref, band_ref, first_ref, second_ref, x_ref, sw_ref, dw_ref, gain_ref, wi_ref, wo_ref, cot_ref,
+    rows_ref, side_ref, band_ref, near_ref, swap_ref, x_ref, sw_ref, dw_ref, gain_ref, wi_ref, wo_ref, cot_ref,
     out_ref, own_ref, send_ref,
     swp, dwt, gnp, wide, wit, wot, pt, cv, un, iv, ft, mg, hs, gps, gf, gc, si, so,
 ):
@@ -201,9 +201,11 @@
         for b in range(HB):
             dst[b * HALF : (b + 1) * HALF, :] = wide[:, b * HALF : (b + 1) * HALF].T.astype(BF16)
 
-    odd = lax.axis_index("lon") % 2 == 1
-    for side, (even_ref, odd_ref, xx) in enumerate(((second_ref, first_ref, 0), (first_ref, second_ref, 19))):
-        arrived = jnp.where(odd, odd_ref[...].astype(F32), even_ref[...].astype(F32))
+    odd = lax.axis_index("lat") % 2 == 1
+    near = near_ref[0].astype(F32)
+    swap = swap_ref[1].astype(F32)
+    for side, (even, other, xx) in enumerate(((near, swap, 0), (swap, near, 19))):
+        arrived = jnp.where(odd, other, even)
         cells = (side_ref[side].astype(F32) + arrived).astype(BF16)
         rows = jnp.dot(cells, swp[...], preferred_element_type=F32).astype(BF16).astype(F32)
         for h in range(2):
@@ -377,10 +379,11 @@
     vmem = pl.BlockSpec(memory_space=pltpu.VMEM)
     lon = lax.axis_size("lon")
     lat = lax.axis_size("lat")
-    first_pair = [(i, i ^ 1) for i in range(lon)]
-    second_pair = [(i, (i + 1 if i % 2 else i - 1) % lon) for i in range(lon)]
-    pos_second = lax.ppermute(tile_pos, "lon", second_pair)
-    pos_first = lax.ppermute(tile_pos, "lon", first_pair)
+    hop = [(i * lon + j, i * lon + (j + (1 if i % 2 == 0 else -1)) % lon) for i in range(lat) for j in range(lon)]
+    back = [(target, source) for source, target in hop]
+    siblings = [(i, i ^ 1) for i in range(lat)]
+    pos_pair = jnp.concatenate([tile_pos, lax.ppermute(tile_pos, "lat", siblings)], axis=0)
+    pos_far = lax.ppermute(pos_pair, ("lat", "lon"), back)
     shell, inputs = pl.pallas_call(
         shell_kernel,
         out_shape=(pltpu.VMEM((KPAD, PAY), BF16), pltpu.VMEM((A_DEV, KPAD, TT), BF16)),
@@ -393,23 +396,21 @@
         ],
         name="shell",
     )(tile_pos, valid_rows, x_tiles[0].transpose(1, 0, 2), jnp.asarray(shell_cells()))
-    shell, pos_first, pos_second = lax.optimization_barrier((shell, pos_first, pos_second))
+    shell, pos_far = lax.optimization_barrier((shell, pos_far))
     same_core = [[i for i in range(c, lat, 2)] for c in range(2)]
-    siblings = [(i, i ^ 1) for i in range(lat)]
     mine = lax.all_to_all(
         jnp.broadcast_to(shell[None], (GROUP, KPAD, PAY)), "lat", 0, 0, axis_index_groups=same_core, tiled=True
     )
     theirs = lax.ppermute(mine, "lat", siblings)
-    side, band, to_first, to_second = pl.pallas_call(
+    side, band, give = pl.pallas_call(
         pick_kernel,
         out_shape=(
             pltpu.VMEM((2, A_DEV * STRIP, KPAD), BF16),
             pltpu.VMEM((2 * A_DEV, PIECE, KPAD), BF16),
-            pltpu.VMEM((A_DEV * STRIP, KPAD), BF16),
-            pltpu.VMEM((A_DEV * STRIP, KPAD), BF16),
+            pltpu.VMEM((2, A_DEV * STRIP, KPAD), BF16),
         ),
-        in_specs=[smem] * 3 + [vmem] * 3,
-        out_specs=(vmem, vmem, vmem, vmem),
+        in_specs=[smem] * 2 + [vmem] * 3,
+        out_specs=(vmem, vmem, vmem),
         scratch_shapes=[
             pltpu.VMEM((16, PAY), F32),
             pltpu.VMEM((64, HALF), F32),
@@ -420,9 +421,9 @@
         ],
         compiler_params=pltpu.CompilerParams(vmem_limit_bytes=16 << 20),
         name="pick",
-    )(tile_pos, pos_first, pos_second, on_chip(mine), on_chip(theirs), jnp.asarray(strip_sources()))
-    from_second = lax.ppermute(to_second, "lon", second_pair)
-    from_first = lax.ppermute(to_first, "lon", first_pair)
+    )(tile_pos, pos_far, on_chip(mine), on_chip(theirs), jnp.asarray(strip_sources()))
+    near = lax.ppermute(give, ("lat", "lon"), hop)
+    swap = lax.ppermute(near, "lat", siblings)
 
     cells = A_DEV * TT
     out_tiles, own, send = pl.pallas_call(
@@ -456,7 +457,7 @@
         ],
         compiler_params=pltpu.CompilerParams(vmem_limit_bytes=32 << 20),
         name="block",
-    )(in_hbm(valid_rows), side, band, on_chip(from_first), on_chip(from_second), inputs, stem_w, dw_kernel.T, norm_gain.reshape(1, C), w_in, w_out.T, cotangent[0])
+    )(in_hbm(valid_rows), side, band, on_chip(near), on_chip(swap), inputs, stem_w, dw_kernel.T, in_hbm(norm_gain.reshape(1, C)), w_in, w_out.T, cotangent[0])
 
     arrived = lax.ppermute(send, "lat", siblings)
     chip_sum = (own + arrived.astype(F32)).astype(BF16)

time: 99.8 us -> 99 us (level)
  waiting for transfers between devices: 6.51 us -> 13.5 us
  starting transfers between devices: 20.8 us -> 15.1 us
  blocking collectives: 48.6 us -> 47.3 us
    ppermute x4, waiting for transfers between devices: 1.85 us -> 8.83 us  [the longest x1 5.72 us: body(): pos_far = lax.ppermute(pos_pair, ('lat', 'lon'), back)]
    all_to_all x1, blocking collectives: 18.4 us -> 15.9 us  [body(): lax.all_to_all(chip_sum, ('lat', 'lon'), 0, 0, axis_index_groups=every, t...]
    ppermute x4, starting transfers between devices: 12.5 us -> 10 us  [the longest x1 3.87 us: body(): swap = lax.ppermute(near, 'lat', siblings)]
    ppermute x1, starting transfers between devices: 3.45 us -> 1.98 us  [body(): theirs = lax.ppermute(mine, 'lat', siblings)]
    ppermute x1, starting transfers between devices: 1.52 us -> 0.37 us  [body(): arrived = lax.ppermute(send, 'lat', siblings)]
    all_to_all x1, blocking collectives: 15.7 us -> 16.8 us  [body(): lax.all_to_all(jnp.broadcast_to(shell[None], (GROUP, KPAD, PAY)), 'lat',...]
  transfers between devices with their start and end apart: 7 -> 7, of which waited for: 4 -> 6; matrix products, arithmetic and copies ran while one was open for 0% -> 0% of each run, Pallas kernels for 1% -> 1%
where the time goes in v4:
time: 99 us; the launch traced here: 98.7 us
  blocking collectives  47.3 us (48%)
  Pallas kernels  21.8 us (22%)
  starting transfers between devices  15.1 us (15%)
  waiting for transfers between devices  13.5 us (14%)
    all_to_all x1, blocking collectives, body(): lax.all_to_all(jnp.broadcast_to(shell[None], (GROUP, KPAD, PAY)), 'lat',...  16.8 us
    all_to_all x1, blocking collectives, body(): lax.all_to_all(chip_sum, ('lat', 'lon'), 0, 0, axis_index_groups=every, t...  15.9 us
    pallas_call x1, Pallas kernels, body(): pl.pallas_call(main_kernel, out_shape=(jax.ShapeDtypeStruct((A_DEV, C, TT...  15.4 us
    all_to_all x1, blocking collectives, body(): lax.all_to_all(spread, ('lat', 'lon'), 0, 0, axis_index_groups=every, til...  14.6 us
    ppermute x1, waiting for transfers between devices, body(): pos_far = lax.ppermute(pos_pair, ('lat', 'lon'), back)  5.72 us
    ppermute x1, starting transfers between devices, body(): swap = lax.ppermute(near, 'lat', siblings)  3.87 us
    pallas_call x1, Pallas kernels, body(): pl.pallas_call(pick_kernel, out_shape=(pltpu.VMEM((2, A_DEV * STRIP, KPAD...  3.8 us
    ppermute x1, starting transfers between devices, body(): near = lax.ppermute(give, ('lat', 'lon'), hop)  3.22 us
  transfers between devices with their start and end apart: 7, of which 6 were waited for; matrix products, arithmetic and copies ran while one was open for 0% of the time, Pallas kernels for 1%

profile of v4, /device:TPU:1, one launch (start us, length us, event | category | flops | bytes accessed | tf_op | source)
XLA Modules:
  0.0 98.7 jit_solution(13941662047885127286)
XLA Ops:
  0.6 1.5 %collective-permute-start = (s32[1,4]{1,0:T(1,128)}, s32[1,4]{1,0:T(1,128)S(1)}, u32[]{:S(2)}, u32[]{:S(2)}) collective-permute-start(s32[1,4]{1,0:T(1,128)} %pos_ref.3), channel_id=1, source_target_pairs={{0,8},{8,0},{16,24},{24,16},{32,40},{40,32},{48,56},{56,48},{64,72... | collective-permute-start | bytes 56 | tf_op jit(solution)/shard_map/ppermute | solution.py:385
  2.1 0.0 copy-start.6
  2.1 1.4 %shell.1 = (bf16[80,640]{1,0:T(8,128)(2,1)S(1)}, bf16[4,80,256]{2,1,0:T(8,128)(2,1)S(1)}) custom-call(s32[1,4]{1,0:T(1,128)} %pos_ref.3, s32[1,4]{1,0:T(1,128)} %rows_ref.3, bf16[77,4,256]{2,1,0:T(4,128)(2,1)} %bitcast.14, s32[1,256]{1,0:T(1,128)} %constant.7.clone.map_ref), custom_call_target="tpu_custom_call" | custom-call | tf_op jit(solution)/shard_map/shell/pallas_call | solution.py:387
  3.5 0.0 collective-permute-done
  3.5 0.0 copy-done.6
  3.5 1.5 %collective-permute-start.1 = (s32[2,4]{1,0:T(2,128)S(1)}, s32[2,4]{1,0:T(2,128)S(1)}, u32[]{:S(2)}, u32[]{:S(2)}) collective-permute-start(s32[2,4]{1,0:T(2,128)S(1)} %pad_add_fusion), channel_id=1, source_target_pairs={{1,0},{2,1},{3,2},{4,3},{5,4},{6,5},{7,6},{0,7},{15,8},{8,9},{9,10... | collective-permute-start | bytes 104 | tf_op jit(solution)/shard_map/ppermute | solution.py:386
  5.0 5.7 %collective-permute-done.1.far_pos_ref = s32[2,4]{1,0:T(2,128)S(1)} collective-permute-done((s32[2,4]{1,0:T(2,128)S(1)}, s32[2,4]{1,0:T(2,128)S(1)}, u32[]{:S(2)}, u32[]{:S(2)}) %collective-permute-start.1) | collective-permute-done | bytes 64 | tf_op jit(solution)/shard_map/ppermute | solution.py:386
  10.7 0.1 broadcast_in_dim.6
  10.8 0.0 copy-start.5
  10.8 16.8 %all_to_all.15.ga_ref = bf16[8,80,640]{2,1,0:T(8,128)(2,1)S(1)} all-to-all(bf16[8,80,640]{2,1,0:T(8,128)(2,1)S(1)} %broadcast_in_dim.6), channel_id=1, replica_groups={{0,16,32,48,64,80,96,112},{8,24,40,56,72,88,104,120},{1,17,33,49,65,81,..., dimensions={0} | all-to-all | bytes 1638400 | tf_op jit(solution)/shard_map/all_to_all | solution.py:401
  27.6 0.0 copy-start
  27.6 0.0 copy-start.1
  27.6 0.0 copy-start.2
  27.6 0.0 copy-start.3
  27.6 2.0 %collective-permute-start.2 = (bf16[8,80,640]{2,1,0:T(8,128)(2,1)S(1)}, bf16[8,80,640]{2,1,0:T(8,128)(2,1)S(1)}, u32[]{:S(2)}, u32[]{:S(2)}) collective-permute-start(bf16[8,80,640]{2,1,0:T(8,128)(2,1)S(1)} %all_to_all.15.ga_ref), channel_id=1, source_target_pairs={{0,8},{8,0},{16,24},{24,16},{32,40},{40,32},{48,56},{56,48},{64,72... | collective-permute-start | bytes 2457608 | tf_op jit(solution)/shard_map/ppermute | solution.py:404
  29.6 2.0 %collective-permute-done.2.gb_ref = bf16[8,80,640]{2,1,0:T(8,128)(2,1)S(1)} collective-permute-done((bf16[8,80,640]{2,1,0:T(8,128)(2,1)S(1)}, bf16[8,80,640]{2,1,0:T(8,128)(2,1)S(1)}, u32[]{:S(2)}, u32[]{:S(2)}) %collective-permute-start.2) | collective-permute-done | bytes 819232 | tf_op jit(solution)/shard_map/ppermute | solution.py:404
  31.5 0.0 copy-done.5
  31.5 0.0 copy-start.4
  31.5 3.8 %pick.1 = (bf16[2,288,80]{2,1,0:T(8,128)(2,1)S(1)}, bf16[8,48,80]{2,1,0:T(8,128)(2,1)S(1)}, bf16[2,288,80]{2,1,0:T(8,128)(2,1)S(1)}) custom-call(s32[1,4]{1,0:T(1,128)S(1)} %copy-done.6, s32[2,4]{1,0:T(2,128)S(1)} %collective-permute-done.1.far_pos_ref, bf16[8,80,640]{2,1,0:T(8,128)(2,1)S(1)} %all_to_all.15.ga_ref, ...), custom_call_target="tpu_custom_call" | custom-call | tf_op jit(solution)/shard_map/pick/pallas_call | solution.py:405
  35.3 3.2 %collective-permute-start.3 = (bf16[2,288,80]{2,1,0:T(8,128)(2,1)S(1)}, bf16[2,288,80]{2,1,0:T(8,128)(2,1)S(1)}, u32[]{:S(2)}, u32[]{:S(2)}) collective-permute-start(bf16[2,288,80]{2,1,0:T(8,128)(2,1)S(1)} %get-tuple-element.24), channel_id=1, source_target_pairs={{0,1},{1,2},{2,3},{3,4},{4,5},{5,6},{6,7},{7,0},{8,15},{9,8},{10,9... | collective-permute-start | bytes 276488 | tf_op jit(solution)/shard_map/ppermute | solution.py:425
  38.6 2.1 %collective-permute-done.3.near_ref = bf16[2,288,80]{2,1,0:T(8,128)(2,1)S(1)} collective-permute-done((bf16[2,288,80]{2,1,0:T(8,128)(2,1)S(1)}, bf16[2,288,80]{2,1,0:T(8,128)(2,1)S(1)}, u32[]{:S(2)}, u32[]{:S(2)}) %collective-permute-start.3) | collective-permute-done | bytes 92192 | tf_op jit(solution)/shard_map/ppermute | solution.py:425
  40.7 3.9 %collective-permute-start.4 = (bf16[2,288,80]{2,1,0:T(8,128)(2,1)S(1)}, bf16[2,288,80]{2,1,0:T(8,128)(2,1)S(1)}, u32[]{:S(2)}, u32[]{:S(2)}) collective-permute-start(bf16[2,288,80]{2,1,0:T(8,128)(2,1)S(1)} %collective-permute-done.3.near_ref), channel_id=1, source_target_pairs={{0,8},{8,0},{16,24},{24,16},{32,40},{40,32},{48,56},{56,48},{64,72... | collective-permute-start | bytes 276488 | tf_op jit(solution)/shard_map/ppermute | solution.py:426
  44.5 1.0 %collective-permute-done.4.swap_ref = bf16[2,288,80]{2,1,0:T(8,128)(2,1)S(1)} collective-permute-done((bf16[2,288,80]{2,1,0:T(8,128)(2,1)S(1)}, bf16[2,288,80]{2,1,0:T(8,128)(2,1)S(1)}, u32[]{:S(2)}, u32[]{:S(2)}) %collective-permute-start.4) | collective-permute-done | bytes 92192 | tf_op jit(solution)/shard_map/ppermute | solution.py:426
  45.5 0.0 copy-done
  45.5 0.0 copy-done.1
  45.5 0.0 copy-done.2
  45.5 0.0 copy-done.3
  45.5 0.0 copy-done.4
  45.6 15.4 %block.1 = (bf16[4,200,256]{2,1,0:T(8,128)(2,1)}, f32[64,24,128]{2,1,0:T(8,128)S(1)}, bf16[64,24,128]{2,1,0:T(8,128)(2,1)S(1)}) custom-call(s32[1,4]{1,0:T(1,128)} %rows_ref.3, bf16[2,288,80]{2,1,0:T(8,128)(2,1)S(1)} %get-tuple-element.22.side_ref, bf16[8,48,80]{2,1,0:T(8,128)(2,1)S(1)} %get-tuple-element.23.band_ref, ...), custom_call_target="tpu_custom_call" | custom-call | tf_op jit(solution)/shard_map/block/pallas_call | solution.py:429
  60.9 0.4 collective-permute-start.5
  61.3 1.4 %collective-permute-done.5 = bf16[64,24,128]{2,1,0:T(8,128)(2,1)S(1)} collective-permute-done((bf16[64,24,128]{2,1,0:T(8,128)(2,1)S(1)}, bf16[64,24,128]{2,1,0:T(8,128)(2,1)S(1)}, u32[]{:S(2)}, u32[]{:S(2)}) %collective-permute-start.5) | collective-permute-done | bytes 393248 | tf_op jit(solution)/shard_map/ppermute | solution.py:462
  62.7 0.1 add_convert_fusion
  62.7 15.9 %all_to_all.16 = bf16[64,24,128]{2,1,0:T(8,128)(2,1)S(1)} all-to-all(bf16[64,24,128]{2,1,0:T(8,128)(2,1)S(1)} %add_convert_fusion), channel_id=1, replica_groups={{0,1,2,3,4,5,6,7,16,17,18,19,20,21,22,23,32,33,34,35,36,37,38,39,48,49,..., dimensions={0} | all-to-all | bytes 786432 | tf_op jit(solution)/shard_map/all_to_all | solution.py:465
  78.6 0.1 reduce_sum.12
  78.7 0.1 broadcast_in_dim.8
  78.8 14.6 %all_to_all.17.own_ref = bf16[64,24,128]{2,1,0:T(8,128)(2,1)S(1)} all-to-all(bf16[64,24,128]{2,1,0:T(8,128)(2,1)S(1)} %broadcast_in_dim.8), channel_id=1, replica_groups={{0,1,2,3,4,5,6,7,16,17,18,19,20,21,22,23,32,33,34,35,36,37,38,39,48,49,..., dimensions={0} | all-to-all | bytes 786432 | tf_op jit(solution)/shard_map/all_to_all | solution.py:469
  93.4 2.7 %collective-permute-start.6 = (bf16[64,24,128]{2,1,0:T(8,128)(2,1)S(1)}, bf16[64,24,128]{2,1,0:T(8,128)(2,1)S(1)}, u32[]{:S(2)}, u32[]{:S(2)}) collective-permute-start(bf16[64,24,128]{2,1,0:T(8,128)(2,1)S(1)} %all_to_all.17.own_ref), channel_id=1, source_target_pairs={{0,8},{8,0},{16,24},{24,16},{32,40},{40,32},{48,56},{56,48},{64,72... | collective-permute-start | bytes 1179656 | tf_op jit(solution)/shard_map/ppermute | solution.py:470
  96.1 1.3 %collective-permute-done.6.other_ref = bf16[64,24,128]{2,1,0:T(8,128)(2,1)S(1)} collective-permute-done((bf16[64,24,128]{2,1,0:T(8,128)(2,1)S(1)}, bf16[64,24,128]{2,1,0:T(8,128)(2,1)S(1)}, u32[]{:S(2)}, u32[]{:S(2)}) %collective-permute-start.6) | collective-permute-done | bytes 393248 | tf_op jit(solution)/shard_map/ppermute | solution.py:470
  97.4 1.3 %finish.1 = (f32[200,800]{1,0:T(8,128)}, f32[200,800]{1,0:T(8,128)}, f32[49,200]{1,0:T(8,128)}, f32[1,200]{1,0:T(1,128)}) custom-call(bf16[64,24,128]{2,1,0:T(8,128)(2,1)S(1)} %all_to_all.17.own_ref, bf16[64,24,128]{2,1,0:T(8,128)(2,1)S(1)} %collective-permute-done.6.other_ref), custom_call_target="tpu_custom_call" | custom-call | tf_op jit(solution)/shard_map/finish/pallas_call | solution.py:471
  (1 shorter events, 0.0 us)
Async XLA Ops:
  0.6 2.9 %collective-permute-start = (s32[1,4]{1,0:T(1,128)}, s32[1,4]{1,0:T(1,128)S(1)}, u32[]{:S(2)}, u32[]{:S(2)}) collective-permute-start(s32[1,4]{1,0:T(1,128)} %pos_ref.3), channel_id=1, source_target_pairs={{0,8},{8,0},{16,24},{24,16},{32,40},{40,32},{48,56},{56,48},{64,72... | collective-permute-start | bytes 56 | tf_op jit(solution)/shard_map/ppermute | solution.py:385
  2.1 1.4 %copy-start.6 = (s32[1,4]{1,0:T(1,128)S(1)}, s32[1,4]{1,0:T(1,128)}, u32[]{:S(2)}) copy-start(s32[1,4]{1,0:T(1,128)} %pos_ref.3) | copy-start | bytes 52
  3.5 7.2 %collective-permute-start.1 = (s32[2,4]{1,0:T(2,128)S(1)}, s32[2,4]{1,0:T(2,128)S(1)}, u32[]{:S(2)}, u32[]{:S(2)}) collective-permute-start(s32[2,4]{1,0:T(2,128)S(1)} %pad_add_fusion), channel_id=1, source_target_pairs={{1,0},{2,1},{3,2},{4,3},{5,4},{6,5},{7,6},{0,7},{15,8},{8,9},{9,10... | collective-permute-start | bytes 104 | tf_op jit(solution)/shard_map/ppermute | solution.py:386
  10.8 20.7 %copy-start.5 = (s32[72,128]{1,0:T(8,128)S(1)}, s32[72,128]{1,0:T(8,128)}, u32[]{:S(2)}) copy-start(s32[72,128]{1,0:T(8,128)} %constant.8.clone.src_ref) | copy-start | bytes 110596
  27.6 18.0 %copy-start = (bf16[1,4,200,256]{3,2,1,0:T(8,128)(2,1)S(1)}, bf16[1,4,200,256]{3,2,1,0:T(8,128)(2,1)}, u32[]{:S(2)}) copy-start(bf16[1,4,200,256]{3,2,1,0:T(8,128)(2,1)} %param.19) | copy-start | bytes 1228804
  27.6 18.0 %copy-start.1 = (bf16[200,800]{1,0:T(8,128)(2,1)S(1)}, bf16[200,800]{1,0:T(8,128)(2,1)}, u32[]{:S(2)}) copy-start(bf16[200,800]{1,0:T(8,128)(2,1)} %wi_ref.1) | copy-start | bytes 960004
  27.6 18.0 %copy-start.2 = (bf16[800,200]{0,1:T(8,128)(2,1)S(1)}, bf16[800,200]{0,1:T(8,128)(2,1)}, u32[]{:S(2)}) copy-start(bf16[800,200]{0,1:T(8,128)(2,1)} %param.18) | copy-start | bytes 960004
  27.6 18.0 %copy-start.3 = (f32[200,49]{0,1:T(8,128)S(1)}, f32[200,49]{0,1:T(8,128)}, u32[]{:S(2)}) copy-start(f32[200,49]{0,1:T(8,128)} %param.15) | copy-start | bytes 117604
  27.6 3.9 %collective-permute-start.2 = (bf16[8,80,640]{2,1,0:T(8,128)(2,1)S(1)}, bf16[8,80,640]{2,1,0:T(8,128)(2,1)S(1)}, u32[]{:S(2)}, u32[]{:S(2)}) collective-permute-start(bf16[8,80,640]{2,1,0:T(8,128)(2,1)S(1)} %all_to_all.15.ga_ref), channel_id=1, source_target_pairs={{0,8},{8,0},{16,24},{24,16},{32,40},{40,32},{48,56},{56,48},{64,72... | collective-permute-start | bytes 2457608 | tf_op jit(solution)/shard_map/ppermute | solution.py:404
  31.5 14.0 %copy-start.4 = (bf16[77,200]{1,0:T(8,128)(2,1)S(1)}, bf16[77,200]{1,0:T(8,128)(2,1)}, u32[]{:S(2)}) copy-start(bf16[77,200]{1,0:T(8,128)(2,1)} %sw_ref.1) | copy-start | bytes 92404
  35.3 5.3 %collective-permute-start.3 = (bf16[2,288,80]{2,1,0:T(8,128)(2,1)S(1)}, bf16[2,288,80]{2,1,0:T(8,128)(2,1)S(1)}, u32[]{:S(2)}, u32[]{:S(2)}) collective-permute-start(bf16[2,288,80]{2,1,0:T(8,128)(2,1)S(1)} %get-tuple-element.24), channel_id=1, source_target_pairs={{0,1},{1,2},{2,3},{3,4},{4,5},{5,6},{6,7},{7,0},{8,15},{9,8},{10,9... | collective-permute-start | bytes 276488 | tf_op jit(solution)/shard_map/ppermute | solution.py:425
  40.7 4.9 %collective-permute-start.4 = (bf16[2,288,80]{2,1,0:T(8,128)(2,1)S(1)}, bf16[2,288,80]{2,1,0:T(8,128)(2,1)S(1)}, u32[]{:S(2)}, u32[]{:S(2)}) collective-permute-start(bf16[2,288,80]{2,1,0:T(8,128)(2,1)S(1)} %collective-permute-done.3.near_ref), channel_id=1, source_target_pairs={{0,8},{8,0},{16,24},{24,16},{32,40},{40,32},{48,56},{56,48},{64,72... | collective-permute-start | bytes 276488 | tf_op jit(solution)/shard_map/ppermute | solution.py:426
  60.9 1.7 %collective-permute-start.5 = (bf16[64,24,128]{2,1,0:T(8,128)(2,1)S(1)}, bf16[64,24,128]{2,1,0:T(8,128)(2,1)S(1)}, u32[]{:S(2)}, u32[]{:S(2)}) collective-permute-start(bf16[64,24,128]{2,1,0:T(8,128)(2,1)S(1)} %get-tuple-element.28), channel_id=1, source_target_pairs={{0,8},{8,0},{16,24},{24,16},{32,40},{40,32},{48,56},{56,48},{64,72... | collective-permute-start | bytes 1179656 | tf_op jit(solution)/shard_map/ppermute | solution.py:462
  93.4 4.0 %collective-permute-start.6 = (bf16[64,24,128]{2,1,0:T(8,128)(2,1)S(1)}, bf16[64,24,128]{2,1,0:T(8,128)(2,1)S(1)}, u32[]{:S(2)}, u32[]{:S(2)}) collective-permute-start(bf16[64,24,128]{2,1,0:T(8,128)(2,1)S(1)} %all_to_all.17.own_ref), channel_id=1, source_target_pairs={{0,8},{8,0},{16,24},{24,16},{32,40},{40,32},{48,56},{56,48},{64,72... | collective-permute-start | bytes 1179656 | tf_op jit(solution)/shard_map/ppermute | solution.py:470

commit v5 on v4

--- a/solution.py
+++ b/solution.py
@@ -126,7 +126,7 @@
     sm[...] = jnp.broadcast_to(total, (64, HALF)).astype(jnp.int32)
     tcopy = pltpu.make_async_copy(sm, ts, sem)
     tcopy.start()
-    column = lax.broadcasted_iota(jnp.int32, (STRIP, 3 * HALF), 1)
+    column = lax.broadcasted_iota(jnp.int32, (STRIP, 256), 1)
     for n in range(8):
         gaps[n] = column - src_ref[:, n : n + 1]
     tcopy.wait()
@@ -136,9 +136,9 @@
         spot = jnp.maximum(got - 1, 0)
         source = spot // 1024
         at = spot % 1024
-        block = jnp.minimum(at // HALF, PAY // HALF - 3)
+        block = at // HALF
         shift = jnp.where(got == 0, -5000, at - block * HALF)
-        cells = pl.ds(pl.multiple_of(block * HALF, HALF), 3 * HALF)
+        cells = pl.ds(pl.multiple_of(block * HALF, HALF), 256)
         near = ga_ref[source // 2, :, cells]
         far = gb_ref[source // 2, :, cells]
         window = jnp.where(source % 2 == 0, near, far)
@@ -417,7 +417,7 @@
             pltpu.VMEM((64, HALF), jnp.int32),
             pltpu.SMEM((64, HALF), jnp.int32),
             pltpu.SemaphoreType.DMA,
-            pltpu.VMEM((8, STRIP, 3 * HALF), jnp.int32),
+            pltpu.VMEM((8, STRIP, 256), jnp.int32),
         ],
         compiler_params=pltpu.CompilerParams(vmem_limit_bytes=16 << 20),
         name="pick",

time: 99 us -> 98.5 us (level)
  no operation moved by 1% of the time
where the time goes in v5:
time: 98.5 us; the launch traced here: 98.2 us
  blocking collectives  47.3 us (48%)
  Pallas kernels  21.3 us (22%)
  starting transfers between devices  15.1 us (15%)
  waiting for transfers between devices  13.5 us (14%)
    all_to_all x1, blocking collectives, body(): lax.all_to_all(jnp.broadcast_to(shell[None], (GROUP, KPAD, PAY)), 'lat',...  16.8 us
    all_to_all x1, blocking collectives, body(): lax.all_to_all(chip_sum, ('lat', 'lon'), 0, 0, axis_index_groups=every, t...  15.9 us
    pallas_call x1, Pallas kernels, body(): pl.pallas_call(main_kernel, out_shape=(jax.ShapeDtypeStruct((A_DEV, C, TT...  15.4 us
    all_to_all x1, blocking collectives, body(): lax.all_to_all(spread, ('lat', 'lon'), 0, 0, axis_index_groups=every, til...  14.6 us
    ppermute x1, waiting for transfers between devices, body(): pos_far = lax.ppermute(pos_pair, ('lat', 'lon'), back)  5.72 us
    ppermute x1, starting transfers between devices, body(): swap = lax.ppermute(near, 'lat', siblings)  3.88 us
    pallas_call x1, Pallas kernels, body(): pl.pallas_call(pick_kernel, out_shape=(pltpu.VMEM((2, A_DEV * STRIP, KPAD...  3.33 us
    ppermute x1, starting transfers between devices, body(): near = lax.ppermute(give, ('lat', 'lon'), hop)  3.22 us
  transfers between devices with their start and end apart: 7, of which 6 were waited for; matrix products, arithmetic and copies ran while one was open for 0% of the time, Pallas kernels for 1%

profile of v5, /device:TPU:1, one launch (start us, length us, event | category | flops | bytes accessed | tf_op | source)
XLA Modules:
  0.0 98.2 jit_solution(17293655670318595012)
XLA Ops:
  0.6 1.5 %collective-permute-start = (s32[1,4]{1,0:T(1,128)}, s32[1,4]{1,0:T(1,128)S(1)}, u32[]{:S(2)}, u32[]{:S(2)}) collective-permute-start(s32[1,4]{1,0:T(1,128)} %pos_ref.3), channel_id=1, source_target_pairs={{0,8},{8,0},{16,24},{24,16},{32,40},{40,32},{48,56},{56,48},{64,72... | collective-permute-start | bytes 56 | tf_op jit(solution)/shard_map/ppermute | solution.py:385
  2.1 0.0 copy-start.6
  2.1 1.4 %shell.1 = (bf16[80,640]{1,0:T(8,128)(2,1)S(1)}, bf16[4,80,256]{2,1,0:T(8,128)(2,1)S(1)}) custom-call(s32[1,4]{1,0:T(1,128)} %pos_ref.3, s32[1,4]{1,0:T(1,128)} %rows_ref.3, bf16[77,4,256]{2,1,0:T(4,128)(2,1)} %bitcast.14, s32[1,256]{1,0:T(1,128)} %constant.7.clone.map_ref), custom_call_target="tpu_custom_call" | custom-call | tf_op jit(solution)/shard_map/shell/pallas_call | solution.py:387
  3.5 0.0 collective-permute-done
  3.5 0.0 copy-done.6
  3.5 1.5 %collective-permute-start.1 = (s32[2,4]{1,0:T(2,128)S(1)}, s32[2,4]{1,0:T(2,128)S(1)}, u32[]{:S(2)}, u32[]{:S(2)}) collective-permute-start(s32[2,4]{1,0:T(2,128)S(1)} %pad_add_fusion), channel_id=1, source_target_pairs={{1,0},{2,1},{3,2},{4,3},{5,4},{6,5},{7,6},{0,7},{15,8},{8,9},{9,10... | collective-permute-start | bytes 104 | tf_op jit(solution)/shard_map/ppermute | solution.py:386
  5.0 5.7 %collective-permute-done.1.far_pos_ref = s32[2,4]{1,0:T(2,128)S(1)} collective-permute-done((s32[2,4]{1,0:T(2,128)S(1)}, s32[2,4]{1,0:T(2,128)S(1)}, u32[]{:S(2)}, u32[]{:S(2)}) %collective-permute-start.1) | collective-permute-done | bytes 64 | tf_op jit(solution)/shard_map/ppermute | solution.py:386
  10.7 0.1 broadcast_in_dim.6
  10.8 0.0 copy-start.5
  10.8 16.8 %all_to_all.15.ga_ref = bf16[8,80,640]{2,1,0:T(8,128)(2,1)S(1)} all-to-all(bf16[8,80,640]{2,1,0:T(8,128)(2,1)S(1)} %broadcast_in_dim.6), channel_id=1, replica_groups={{0,16,32,48,64,80,96,112},{8,24,40,56,72,88,104,120},{1,17,33,49,65,81,..., dimensions={0} | all-to-all | bytes 1638400 | tf_op jit(solution)/shard_map/all_to_all | solution.py:401
  27.6 0.0 copy-start
  27.6 0.0 copy-start.1
  27.6 0.0 copy-start.2
  27.6 0.0 copy-start.3
  27.6 2.0 %collective-permute-start.2 = (bf16[8,80,640]{2,1,0:T(8,128)(2,1)S(1)}, bf16[8,80,640]{2,1,0:T(8,128)(2,1)S(1)}, u32[]{:S(2)}, u32[]{:S(2)}) collective-permute-start(bf16[8,80,640]{2,1,0:T(8,128)(2,1)S(1)} %all_to_all.15.ga_ref), channel_id=1, source_target_pairs={{0,8},{8,0},{16,24},{24,16},{32,40},{40,32},{48,56},{56,48},{64,72... | collective-permute-start | bytes 2457608 | tf_op jit(solution)/shard_map/ppermute | solution.py:404
  29.6 2.0 %collective-permute-done.2.gb_ref = bf16[8,80,640]{2,1,0:T(8,128)(2,1)S(1)} collective-permute-done((bf16[8,80,640]{2,1,0:T(8,128)(2,1)S(1)}, bf16[8,80,640]{2,1,0:T(8,128)(2,1)S(1)}, u32[]{:S(2)}, u32[]{:S(2)}) %collective-permute-start.2) | collective-permute-done | bytes 819232 | tf_op jit(solution)/shard_map/ppermute | solution.py:404
  31.5 0.0 copy-done.5
  31.5 0.0 copy-start.4
  31.5 3.3 %pick.1 = (bf16[2,288,80]{2,1,0:T(8,128)(2,1)S(1)}, bf16[8,48,80]{2,1,0:T(8,128)(2,1)S(1)}, bf16[2,288,80]{2,1,0:T(8,128)(2,1)S(1)}) custom-call(s32[1,4]{1,0:T(1,128)S(1)} %copy-done.6, s32[2,4]{1,0:T(2,128)S(1)} %collective-permute-done.1.far_pos_ref, bf16[8,80,640]{2,1,0:T(8,128)(2,1)S(1)} %all_to_all.15.ga_ref, ...), custom_call_target="tpu_custom_call" | custom-call | tf_op jit(solution)/shard_map/pick/pallas_call | solution.py:405
  34.9 3.2 %collective-permute-start.3 = (bf16[2,288,80]{2,1,0:T(8,128)(2,1)S(1)}, bf16[2,288,80]{2,1,0:T(8,128)(2,1)S(1)}, u32[]{:S(2)}, u32[]{:S(2)}) collective-permute-start(bf16[2,288,80]{2,1,0:T(8,128)(2,1)S(1)} %get-tuple-element.24), channel_id=1, source_target_pairs={{0,1},{1,2},{2,3},{3,4},{4,5},{5,6},{6,7},{7,0},{8,15},{9,8},{10,9... | collective-permute-start | bytes 276488 | tf_op jit(solution)/shard_map/ppermute | solution.py:425
  38.1 2.1 %collective-permute-done.3.near_ref = bf16[2,288,80]{2,1,0:T(8,128)(2,1)S(1)} collective-permute-done((bf16[2,288,80]{2,1,0:T(8,128)(2,1)S(1)}, bf16[2,288,80]{2,1,0:T(8,128)(2,1)S(1)}, u32[]{:S(2)}, u32[]{:S(2)}) %collective-permute-start.3) | collective-permute-done | bytes 92192 | tf_op jit(solution)/shard_map/ppermute | solution.py:425
  40.2 3.9 %collective-permute-start.4 = (bf16[2,288,80]{2,1,0:T(8,128)(2,1)S(1)}, bf16[2,288,80]{2,1,0:T(8,128)(2,1)S(1)}, u32[]{:S(2)}, u32[]{:S(2)}) collective-permute-start(bf16[2,288,80]{2,1,0:T(8,128)(2,1)S(1)} %collective-permute-done.3.near_ref), channel_id=1, source_target_pairs={{0,8},{8,0},{16,24},{24,16},{32,40},{40,32},{48,56},{56,48},{64,72... | collective-permute-start | bytes 276488 | tf_op jit(solution)/shard_map/ppermute | solution.py:426
  44.1 1.0 %collective-permute-done.4.swap_ref = bf16[2,288,80]{2,1,0:T(8,128)(2,1)S(1)} collective-permute-done((bf16[2,288,80]{2,1,0:T(8,128)(2,1)S(1)}, bf16[2,288,80]{2,1,0:T(8,128)(2,1)S(1)}, u32[]{:S(2)}, u32[]{:S(2)}) %collective-permute-start.4) | collective-permute-done | bytes 92192 | tf_op jit(solution)/shard_map/ppermute | solution.py:426
  45.1 0.0 copy-done
  45.1 0.0 copy-done.1
  45.1 0.0 copy-done.2
  45.1 0.0 copy-done.3
  45.1 0.0 copy-done.4
  45.1 15.4 %block.1 = (bf16[4,200,256]{2,1,0:T(8,128)(2,1)}, f32[64,24,128]{2,1,0:T(8,128)S(1)}, bf16[64,24,128]{2,1,0:T(8,128)(2,1)S(1)}) custom-call(s32[1,4]{1,0:T(1,128)} %rows_ref.3, bf16[2,288,80]{2,1,0:T(8,128)(2,1)S(1)} %get-tuple-element.22.side_ref, bf16[8,48,80]{2,1,0:T(8,128)(2,1)S(1)} %get-tuple-element.23.band_ref, ...), custom_call_target="tpu_custom_call" | custom-call | tf_op jit(solution)/shard_map/block/pallas_call | solution.py:429
  60.5 0.4 collective-permute-start.5
  60.8 1.4 %collective-permute-done.5 = bf16[64,24,128]{2,1,0:T(8,128)(2,1)S(1)} collective-permute-done((bf16[64,24,128]{2,1,0:T(8,128)(2,1)S(1)}, bf16[64,24,128]{2,1,0:T(8,128)(2,1)S(1)}, u32[]{:S(2)}, u32[]{:S(2)}) %collective-permute-start.5) | collective-permute-done | bytes 393248 | tf_op jit(solution)/shard_map/ppermute | solution.py:462
  62.2 0.1 add_convert_fusion
  62.3 15.9 %all_to_all.16 = bf16[64,24,128]{2,1,0:T(8,128)(2,1)S(1)} all-to-all(bf16[64,24,128]{2,1,0:T(8,128)(2,1)S(1)} %add_convert_fusion), channel_id=1, replica_groups={{0,1,2,3,4,5,6,7,16,17,18,19,20,21,22,23,32,33,34,35,36,37,38,39,48,49,..., dimensions={0} | all-to-all | bytes 786432 | tf_op jit(solution)/shard_map/all_to_all | solution.py:465
  78.2 0.1 reduce_sum.12
  78.3 0.1 broadcast_in_dim.8
  78.3 14.6 %all_to_all.17.own_ref = bf16[64,24,128]{2,1,0:T(8,128)(2,1)S(1)} all-to-all(bf16[64,24,128]{2,1,0:T(8,128)(2,1)S(1)} %broadcast_in_dim.8), channel_id=1, replica_groups={{0,1,2,3,4,5,6,7,16,17,18,19,20,21,22,23,32,33,34,35,36,37,38,39,48,49,..., dimensions={0} | all-to-all | bytes 786432 | tf_op jit(solution)/shard_map/all_to_all | solution.py:469
  92.9 2.7 %collective-permute-start.6 = (bf16[64,24,128]{2,1,0:T(8,128)(2,1)S(1)}, bf16[64,24,128]{2,1,0:T(8,128)(2,1)S(1)}, u32[]{:S(2)}, u32[]{:S(2)}) collective-permute-start(bf16[64,24,128]{2,1,0:T(8,128)(2,1)S(1)} %all_to_all.17.own_ref), channel_id=1, source_target_pairs={{0,8},{8,0},{16,24},{24,16},{32,40},{40,32},{48,56},{56,48},{64,72... | collective-permute-start | bytes 1179656 | tf_op jit(solution)/shard_map/ppermute | solution.py:470
  95.6 1.3 %collective-permute-done.6.other_ref = bf16[64,24,128]{2,1,0:T(8,128)(2,1)S(1)} collective-permute-done((bf16[64,24,128]{2,1,0:T(8,128)(2,1)S(1)}, bf16[64,24,128]{2,1,0:T(8,128)(2,1)S(1)}, u32[]{:S(2)}, u32[]{:S(2)}) %collective-permute-start.6) | collective-permute-done | bytes 393248 | tf_op jit(solution)/shard_map/ppermute | solution.py:470
  96.9 1.3 %finish.1 = (f32[200,800]{1,0:T(8,128)}, f32[200,800]{1,0:T(8,128)}, f32[49,200]{1,0:T(8,128)}, f32[1,200]{1,0:T(1,128)}) custom-call(bf16[64,24,128]{2,1,0:T(8,128)(2,1)S(1)} %all_to_all.17.own_ref, bf16[64,24,128]{2,1,0:T(8,128)(2,1)S(1)} %collective-permute-done.6.other_ref), custom_call_target="tpu_custom_call" | custom-call | tf_op jit(solution)/shard_map/finish/pallas_call | solution.py:471
  (1 shorter events, 0.0 us)
Async XLA Ops:
  0.6 2.9 %collective-permute-start = (s32[1,4]{1,0:T(1,128)}, s32[1,4]{1,0:T(1,128)S(1)}, u32[]{:S(2)}, u32[]{:S(2)}) collective-permute-start(s32[1,4]{1,0:T(1,128)} %pos_ref.3), channel_id=1, source_target_pairs={{0,8},{8,0},{16,24},{24,16},{32,40},{40,32},{48,56},{56,48},{64,72... | collective-permute-start | bytes 56 | tf_op jit(solution)/shard_map/ppermute | solution.py:385
  2.1 1.4 %copy-start.6 = (s32[1,4]{1,0:T(1,128)S(1)}, s32[1,4]{1,0:T(1,128)}, u32[]{:S(2)}) copy-start(s32[1,4]{1,0:T(1,128)} %pos_ref.3) | copy-start | bytes 52
  3.5 7.2 %collective-permute-start.1 = (s32[2,4]{1,0:T(2,128)S(1)}, s32[2,4]{1,0:T(2,128)S(1)}, u32[]{:S(2)}, u32[]{:S(2)}) collective-permute-start(s32[2,4]{1,0:T(2,128)S(1)} %pad_add_fusion), channel_id=1, source_target_pairs={{1,0},{2,1},{3,2},{4,3},{5,4},{6,5},{7,6},{0,7},{15,8},{8,9},{9,10... | collective-permute-start | bytes 104 | tf_op jit(solution)/shard_map/ppermute | solution.py:386
  10.8 20.7 %copy-start.5 = (s32[72,128]{1,0:T(8,128)S(1)}, s32[72,128]{1,0:T(8,128)}, u32[]{:S(2)}) copy-start(s32[72,128]{1,0:T(8,128)} %constant.8.clone.src_ref) | copy-start | bytes 110596
  27.6 17.5 %copy-start = (bf16[1,4,200,256]{3,2,1,0:T(8,128)(2,1)S(1)}, bf16[1,4,200,256]{3,2,1,0:T(8,128)(2,1)}, u32[]{:S(2)}) copy-start(bf16[1,4,200,256]{3,2,1,0:T(8,128)(2,1)} %param.19) | copy-start | bytes 1228804
  27.6 17.5 %copy-start.1 = (bf16[200,800]{1,0:T(8,128)(2,1)S(1)}, bf16[200,800]{1,0:T(8,128)(2,1)}, u32[]{:S(2)}) copy-start(bf16[200,800]{1,0:T(8,128)(2,1)} %wi_ref.1) | copy-start | bytes 960004
  27.6 17.5 %copy-start.2 = (bf16[800,200]{0,1:T(8,128)(2,1)S(1)}, bf16[800,200]{0,1:T(8,128)(2,1)}, u32[]{:S(2)}) copy-start(bf16[800,200]{0,1:T(8,128)(2,1)} %param.18) | copy-start | bytes 960004
  27.6 17.5 %copy-start.3 = (f32[200,49]{0,1:T(8,128)S(1)}, f32[200,49]{0,1:T(8,128)}, u32[]{:S(2)}) copy-start(f32[200,49]{0,1:T(8,128)} %param.15) | copy-start | bytes 117604
  27.6 3.9 %collective-permute-start.2 = (bf16[8,80,640]{2,1,0:T(8,128)(2,1)S(1)}, bf16[8,80,640]{2,1,0:T(8,128)(2,1)S(1)}, u32[]{:S(2)}, u32[]{:S(2)}) collective-permute-start(bf16[8,80,640]{2,1,0:T(8,128)(2,1)S(1)} %all_to_all.15.ga_ref), channel_id=1, source_target_pairs={{0,8},{8,0},{16,24},{24,16},{32,40},{40,32},{48,56},{56,48},{64,72... | collective-permute-start | bytes 2457608 | tf_op jit(solution)/shard_map/ppermute | solution.py:404
  31.5 13.6 %copy-start.4 = (bf16[77,200]{1,0:T(8,128)(2,1)S(1)}, bf16[77,200]{1,0:T(8,128)(2,1)}, u32[]{:S(2)}) copy-start(bf16[77,200]{1,0:T(8,128)(2,1)} %sw_ref.1) | copy-start | bytes 92404
  34.9 5.3 %collective-permute-start.3 = (bf16[2,288,80]{2,1,0:T(8,128)(2,1)S(1)}, bf16[2,288,80]{2,1,0:T(8,128)(2,1)S(1)}, u32[]{:S(2)}, u32[]{:S(2)}) collective-permute-start(bf16[2,288,80]{2,1,0:T(8,128)(2,1)S(1)} %get-tuple-element.24), channel_id=1, source_target_pairs={{0,1},{1,2},{2,3},{3,4},{4,5},{5,6},{6,7},{7,0},{8,15},{9,8},{10,9... | collective-permute-start | bytes 276488 | tf_op jit(solution)/shard_map/ppermute | solution.py:425
  40.2 4.9 %collective-permute-start.4 = (bf16[2,288,80]{2,1,0:T(8,128)(2,1)S(1)}, bf16[2,288,80]{2,1,0:T(8,128)(2,1)S(1)}, u32[]{:S(2)}, u32[]{:S(2)}) collective-permute-start(bf16[2,288,80]{2,1,0:T(8,128)(2,1)S(1)} %collective-permute-done.3.near_ref), channel_id=1, source_target_pairs={{0,8},{8,0},{16,24},{24,16},{32,40},{40,32},{48,56},{56,48},{64,72... | collective-permute-start | bytes 276488 | tf_op jit(solution)/shard_map/ppermute | solution.py:426
  60.5 1.7 %collective-permute-start.5 = (bf16[64,24,128]{2,1,0:T(8,128)(2,1)S(1)}, bf16[64,24,128]{2,1,0:T(8,128)(2,1)S(1)}, u32[]{:S(2)}, u32[]{:S(2)}) collective-permute-start(bf16[64,24,128]{2,1,0:T(8,128)(2,1)S(1)} %get-tuple-element.28), channel_id=1, source_target_pairs={{0,8},{8,0},{16,24},{24,16},{32,40},{40,32},{48,56},{56,48},{64,72... | collective-permute-start | bytes 1179656 | tf_op jit(solution)/shard_map/ppermute | solution.py:462
  92.9 4.0 %collective-permute-start.6 = (bf16[64,24,128]{2,1,0:T(8,128)(2,1)S(1)}, bf16[64,24,128]{2,1,0:T(8,128)(2,1)S(1)}, u32[]{:S(2)}, u32[]{:S(2)}) collective-permute-start(bf16[64,24,128]{2,1,0:T(8,128)(2,1)S(1)} %all_to_all.17.own_ref), channel_id=1, source_target_pairs={{0,8},{8,0},{16,24},{24,16},{32,40},{40,32},{48,56},{56,48},{64,72... | collective-permute-start | bytes 1179656 | tf_op jit(solution)/shard_map/ppermute | solution.py:470

commit v6 on v5

--- a/solution.py
+++ b/solution.py
@@ -226,12 +226,13 @@
         h = step // (2 * A_DEV)
         part = step % (2 * A_DEV)
         at = pl.multiple_of((part // 2) * (PROWS * PITCH) + (part % 2) * (8 * PITCH), 8)
-        acc = [jnp.zeros((TS, HALF), F32) for _ in range(8)]
+        acc = [None] * 8
         for r in range(KW):
             for k in range(KW):
                 w = jnp.broadcast_to(dwt[h, r * KW + k : r * KW + k + 1, :], (TS, HALF))
                 for y in range(8):
-                    acc[y] = acc[y] + w * pt[h, pl.ds(at + (y + r) * PITCH + k, TS), :]
+                    term = w * pt[h, pl.ds(at + (y + r) * PITCH + k, TS), :]
+                    acc[y] = term if acc[y] is None else acc[y] + term
         for y in range(8):
             cv[h, pl.ds(pl.multiple_of(part * HALF, 8) + y * TS, TS), :] = acc[y]
         return carry

time: 98.5 us -> 98.5 us (level)
  no operation moved by 1% of the time
where the time goes in v6:
time: 98.5 us; the launch traced here: 98.2 us
  blocking collectives  47.2 us (48%)
  Pallas kernels  21.4 us (22%)
  starting transfers between devices  15.1 us (15%)
  waiting for transfers between devices  13.5 us (14%)
    all_to_all x1, blocking collectives, body(): lax.all_to_all(jnp.broadcast_to(shell[None], (GROUP, KPAD, PAY)), 'lat',...  16.8 us
    all_to_all x1, blocking collectives, body(): lax.all_to_all(chip_sum, ('lat', 'lon'), 0, 0, axis_index_groups=every, t...  15.9 us
    pallas_call x1, Pallas kernels, body(): pl.pallas_call(main_kernel, out_shape=(jax.ShapeDtypeStruct((A_DEV, C, TT...  15.4 us
    all_to_all x1, blocking collectives, body(): lax.all_to_all(spread, ('lat', 'lon'), 0, 0, axis_index_groups=every, til...  14.6 us
    ppermute x1, waiting for transfers between devices, body(): pos_far = lax.ppermute(pos_pair, ('lat', 'lon'), back)  5.72 us
    ppermute x1, starting transfers between devices, body(): swap = lax.ppermute(near, 'lat', siblings)  3.89 us
    pallas_call x1, Pallas kernels, body(): pl.pallas_call(pick_kernel, out_shape=(pltpu.VMEM((2, A_DEV * STRIP, KPAD...  3.33 us
    ppermute x1, starting transfers between devices, body(): near = lax.ppermute(give, ('lat', 'lon'), hop)  3.21 us
  transfers between devices with their start and end apart: 7, of which 6 were waited for; matrix products, arithmetic and copies ran while one was open for 0% of the time, Pallas kernels for 1%

profile of v6, /device:TPU:1, one launch (start us, length us, event | category | flops | bytes accessed | tf_op | source)
XLA Modules:
  0.0 98.2 jit_solution(17293655670318595012)
XLA Ops:
  0.6 1.5 %collective-permute-start = (s32[1,4]{1,0:T(1,128)}, s32[1,4]{1,0:T(1,128)S(1)}, u32[]{:S(2)}, u32[]{:S(2)}) collective-permute-start(s32[1,4]{1,0:T(1,128)} %pos_ref.3), channel_id=1, source_target_pairs={{0,8},{8,0},{16,24},{24,16},{32,40},{40,32},{48,56},{56,48},{64,72... | collective-permute-start | bytes 56 | tf_op jit(solution)/shard_map/ppermute | solution.py:386
  2.1 0.0 copy-start.6
  2.1 1.4 %shell.1 = (bf16[80,640]{1,0:T(8,128)(2,1)S(1)}, bf16[4,80,256]{2,1,0:T(8,128)(2,1)S(1)}) custom-call(s32[1,4]{1,0:T(1,128)} %pos_ref.3, s32[1,4]{1,0:T(1,128)} %rows_ref.3, bf16[77,4,256]{2,1,0:T(4,128)(2,1)} %bitcast.14, s32[1,256]{1,0:T(1,128)} %constant.7.clone.map_ref), custom_call_target="tpu_custom_call" | custom-call | tf_op jit(solution)/shard_map/shell/pallas_call | solution.py:388
  3.5 0.0 collective-permute-done
  3.5 0.0 copy-done.6
  3.5 1.5 %collective-permute-start.1 = (s32[2,4]{1,0:T(2,128)S(1)}, s32[2,4]{1,0:T(2,128)S(1)}, u32[]{:S(2)}, u32[]{:S(2)}) collective-permute-start(s32[2,4]{1,0:T(2,128)S(1)} %pad_add_fusion), channel_id=1, source_target_pairs={{1,0},{2,1},{3,2},{4,3},{5,4},{6,5},{7,6},{0,7},{15,8},{8,9},{9,10... | collective-permute-start | bytes 104 | tf_op jit(solution)/shard_map/ppermute | solution.py:387
  5.0 5.7 %collective-permute-done.1.far_pos_ref = s32[2,4]{1,0:T(2,128)S(1)} collective-permute-done((s32[2,4]{1,0:T(2,128)S(1)}, s32[2,4]{1,0:T(2,128)S(1)}, u32[]{:S(2)}, u32[]{:S(2)}) %collective-permute-start.1) | collective-permute-done | bytes 64 | tf_op jit(solution)/shard_map/ppermute | solution.py:387
  10.7 0.1 broadcast_in_dim.6
  10.8 0.0 copy-start.5
  10.8 16.8 %all_to_all.15.ga_ref = bf16[8,80,640]{2,1,0:T(8,128)(2,1)S(1)} all-to-all(bf16[8,80,640]{2,1,0:T(8,128)(2,1)S(1)} %broadcast_in_dim.6), channel_id=1, replica_groups={{0,16,32,48,64,80,96,112},{8,24,40,56,72,88,104,120},{1,17,33,49,65,81,..., dimensions={0} | all-to-all | bytes 1638400 | tf_op jit(solution)/shard_map/all_to_all | solution.py:402
  27.6 0.0 copy-start
  27.6 0.0 copy-start.1
  27.6 0.0 copy-start.2
  27.6 0.0 copy-start.3
  27.6 2.0 %collective-permute-start.2 = (bf16[8,80,640]{2,1,0:T(8,128)(2,1)S(1)}, bf16[8,80,640]{2,1,0:T(8,128)(2,1)S(1)}, u32[]{:S(2)}, u32[]{:S(2)}) collective-permute-start(bf16[8,80,640]{2,1,0:T(8,128)(2,1)S(1)} %all_to_all.15.ga_ref), channel_id=1, source_target_pairs={{0,8},{8,0},{16,24},{24,16},{32,40},{40,32},{48,56},{56,48},{64,72... | collective-permute-start | bytes 2457608 | tf_op jit(solution)/shard_map/ppermute | solution.py:405
  29.6 2.0 %collective-permute-done.2.gb_ref = bf16[8,80,640]{2,1,0:T(8,128)(2,1)S(1)} collective-permute-done((bf16[8,80,640]{2,1,0:T(8,128)(2,1)S(1)}, bf16[8,80,640]{2,1,0:T(8,128)(2,1)S(1)}, u32[]{:S(2)}, u32[]{:S(2)}) %collective-permute-start.2) | collective-permute-done | bytes 819232 | tf_op jit(solution)/shard_map/ppermute | solution.py:405
  31.5 0.0 copy-done.5
  31.5 0.0 copy-start.4
  31.5 3.3 %pick.1 = (bf16[2,288,80]{2,1,0:T(8,128)(2,1)S(1)}, bf16[8,48,80]{2,1,0:T(8,128)(2,1)S(1)}, bf16[2,288,80]{2,1,0:T(8,128)(2,1)S(1)}) custom-call(s32[1,4]{1,0:T(1,128)S(1)} %copy-done.6, s32[2,4]{1,0:T(2,128)S(1)} %collective-permute-done.1.far_pos_ref, bf16[8,80,640]{2,1,0:T(8,128)(2,1)S(1)} %all_to_all.15.ga_ref, ...), custom_call_target="tpu_custom_call" | custom-call | tf_op jit(solution)/shard_map/pick/pallas_call | solution.py:406
  34.9 3.2 %collective-permute-start.3 = (bf16[2,288,80]{2,1,0:T(8,128)(2,1)S(1)}, bf16[2,288,80]{2,1,0:T(8,128)(2,1)S(1)}, u32[]{:S(2)}, u32[]{:S(2)}) collective-permute-start(bf16[2,288,80]{2,1,0:T(8,128)(2,1)S(1)} %get-tuple-element.24), channel_id=1, source_target_pairs={{0,1},{1,2},{2,3},{3,4},{4,5},{5,6},{6,7},{7,0},{8,15},{9,8},{10,9... | collective-permute-start | bytes 276488 | tf_op jit(solution)/shard_map/ppermute | solution.py:426
  38.1 2.1 %collective-permute-done.3.near_ref = bf16[2,288,80]{2,1,0:T(8,128)(2,1)S(1)} collective-permute-done((bf16[2,288,80]{2,1,0:T(8,128)(2,1)S(1)}, bf16[2,288,80]{2,1,0:T(8,128)(2,1)S(1)}, u32[]{:S(2)}, u32[]{:S(2)}) %collective-permute-start.3) | collective-permute-done | bytes 92192 | tf_op jit(solution)/shard_map/ppermute | solution.py:426
  40.2 3.9 %collective-permute-start.4 = (bf16[2,288,80]{2,1,0:T(8,128)(2,1)S(1)}, bf16[2,288,80]{2,1,0:T(8,128)(2,1)S(1)}, u32[]{:S(2)}, u32[]{:S(2)}) collective-permute-start(bf16[2,288,80]{2,1,0:T(8,128)(2,1)S(1)} %collective-permute-done.3.near_ref), channel_id=1, source_target_pairs={{0,8},{8,0},{16,24},{24,16},{32,40},{40,32},{48,56},{56,48},{64,72... | collective-permute-start | bytes 276488 | tf_op jit(solution)/shard_map/ppermute | solution.py:427
  44.1 1.0 %collective-permute-done.4.swap_ref = bf16[2,288,80]{2,1,0:T(8,128)(2,1)S(1)} collective-permute-done((bf16[2,288,80]{2,1,0:T(8,128)(2,1)S(1)}, bf16[2,288,80]{2,1,0:T(8,128)(2,1)S(1)}, u32[]{:S(2)}, u32[]{:S(2)}) %collective-permute-start.4) | collective-permute-done | bytes 92192 | tf_op jit(solution)/shard_map/ppermute | solution.py:427
  45.1 0.0 copy-done
  45.1 0.0 copy-done.1
  45.1 0.0 copy-done.2
  45.1 0.0 copy-done.3
  45.1 0.0 copy-done.4
  45.1 15.4 %block.1 = (bf16[4,200,256]{2,1,0:T(8,128)(2,1)}, f32[64,24,128]{2,1,0:T(8,128)S(1)}, bf16[64,24,128]{2,1,0:T(8,128)(2,1)S(1)}) custom-call(s32[1,4]{1,0:T(1,128)} %rows_ref.3, bf16[2,288,80]{2,1,0:T(8,128)(2,1)S(1)} %get-tuple-element.22.side_ref, bf16[8,48,80]{2,1,0:T(8,128)(2,1)S(1)} %get-tuple-element.23.band_ref, ...), custom_call_target="tpu_custom_call" | custom-call | tf_op jit(solution)/shard_map/block/pallas_call | solution.py:430
  60.5 0.4 collective-permute-start.5
  60.9 1.4 %collective-permute-done.5 = bf16[64,24,128]{2,1,0:T(8,128)(2,1)S(1)} collective-permute-done((bf16[64,24,128]{2,1,0:T(8,128)(2,1)S(1)}, bf16[64,24,128]{2,1,0:T(8,128)(2,1)S(1)}, u32[]{:S(2)}, u32[]{:S(2)}) %collective-permute-start.5) | collective-permute-done | bytes 393248 | tf_op jit(solution)/shard_map/ppermute | solution.py:463
  62.2 0.1 add_convert_fusion
  62.3 15.9 %all_to_all.16 = bf16[64,24,128]{2,1,0:T(8,128)(2,1)S(1)} all-to-all(bf16[64,24,128]{2,1,0:T(8,128)(2,1)S(1)} %add_convert_fusion), channel_id=1, replica_groups={{0,1,2,3,4,5,6,7,16,17,18,19,20,21,22,23,32,33,34,35,36,37,38,39,48,49,..., dimensions={0} | all-to-all | bytes 786432 | tf_op jit(solution)/shard_map/all_to_all | solution.py:466
  78.2 0.1 reduce_sum.12
  78.3 0.1 broadcast_in_dim.8
  78.3 14.6 %all_to_all.17.own_ref = bf16[64,24,128]{2,1,0:T(8,128)(2,1)S(1)} all-to-all(bf16[64,24,128]{2,1,0:T(8,128)(2,1)S(1)} %broadcast_in_dim.8), channel_id=1, replica_groups={{0,1,2,3,4,5,6,7,16,17,18,19,20,21,22,23,32,33,34,35,36,37,38,39,48,49,..., dimensions={0} | all-to-all | bytes 786432 | tf_op jit(solution)/shard_map/all_to_all | solution.py:470
  92.9 2.7 %collective-permute-start.6 = (bf16[64,24,128]{2,1,0:T(8,128)(2,1)S(1)}, bf16[64,24,128]{2,1,0:T(8,128)(2,1)S(1)}, u32[]{:S(2)}, u32[]{:S(2)}) collective-permute-start(bf16[64,24,128]{2,1,0:T(8,128)(2,1)S(1)} %all_to_all.17.own_ref), channel_id=1, source_target_pairs={{0,8},{8,0},{16,24},{24,16},{32,40},{40,32},{48,56},{56,48},{64,72... | collective-permute-start | bytes 1179656 | tf_op jit(solution)/shard_map/ppermute | solution.py:471
  95.6 1.3 %collective-permute-done.6.other_ref = bf16[64,24,128]{2,1,0:T(8,128)(2,1)S(1)} collective-permute-done((bf16[64,24,128]{2,1,0:T(8,128)(2,1)S(1)}, bf16[64,24,128]{2,1,0:T(8,128)(2,1)S(1)}, u32[]{:S(2)}, u32[]{:S(2)}) %collective-permute-start.6) | collective-permute-done | bytes 393248 | tf_op jit(solution)/shard_map/ppermute | solution.py:471
  96.9 1.3 %finish.1 = (f32[200,800]{1,0:T(8,128)}, f32[200,800]{1,0:T(8,128)}, f32[49,200]{1,0:T(8,128)}, f32[1,200]{1,0:T(1,128)}) custom-call(bf16[64,24,128]{2,1,0:T(8,128)(2,1)S(1)} %all_to_all.17.own_ref, bf16[64,24,128]{2,1,0:T(8,128)(2,1)S(1)} %collective-permute-done.6.other_ref), custom_call_target="tpu_custom_call" | custom-call | tf_op jit(solution)/shard_map/finish/pallas_call | solution.py:472
  (1 shorter events, 0.0 us)
Async XLA Ops:
  0.6 2.9 %collective-permute-start = (s32[1,4]{1,0:T(1,128)}, s32[1,4]{1,0:T(1,128)S(1)}, u32[]{:S(2)}, u32[]{:S(2)}) collective-permute-start(s32[1,4]{1,0:T(1,128)} %pos_ref.3), channel_id=1, source_target_pairs={{0,8},{8,0},{16,24},{24,16},{32,40},{40,32},{48,56},{56,48},{64,72... | collective-permute-start | bytes 56 | tf_op jit(solution)/shard_map/ppermute | solution.py:386
  2.1 1.4 %copy-start.6 = (s32[1,4]{1,0:T(1,128)S(1)}, s32[1,4]{1,0:T(1,128)}, u32[]{:S(2)}) copy-start(s32[1,4]{1,0:T(1,128)} %pos_ref.3) | copy-start | bytes 52
  3.5 7.2 %collective-permute-start.1 = (s32[2,4]{1,0:T(2,128)S(1)}, s32[2,4]{1,0:T(2,128)S(1)}, u32[]{:S(2)}, u32[]{:S(2)}) collective-permute-start(s32[2,4]{1,0:T(2,128)S(1)} %pad_add_fusion), channel_id=1, source_target_pairs={{1,0},{2,1},{3,2},{4,3},{5,4},{6,5},{7,6},{0,7},{15,8},{8,9},{9,10... | collective-permute-start | bytes 104 | tf_op jit(solution)/shard_map/ppermute | solution.py:387
  10.8 20.7 %copy-start.5 = (s32[72,128]{1,0:T(8,128)S(1)}, s32[72,128]{1,0:T(8,128)}, u32[]{:S(2)}) copy-start(s32[72,128]{1,0:T(8,128)} %constant.8.clone.src_ref) | copy-start | bytes 110596
  27.6 17.5 %copy-start = (bf16[1,4,200,256]{3,2,1,0:T(8,128)(2,1)S(1)}, bf16[1,4,200,256]{3,2,1,0:T(8,128)(2,1)}, u32[]{:S(2)}) copy-start(bf16[1,4,200,256]{3,2,1,0:T(8,128)(2,1)} %param.19) | copy-start | bytes 1228804
  27.6 17.5 %copy-start.1 = (bf16[200,800]{1,0:T(8,128)(2,1)S(1)}, bf16[200,800]{1,0:T(8,128)(2,1)}, u32[]{:S(2)}) copy-start(bf16[200,800]{1,0:T(8,128)(2,1)} %wi_ref.1) | copy-start | bytes 960004
  27.6 17.5 %copy-start.2 = (bf16[800,200]{0,1:T(8,128)(2,1)S(1)}, bf16[800,200]{0,1:T(8,128)(2,1)}, u32[]{:S(2)}) copy-start(bf16[800,200]{0,1:T(8,128)(2,1)} %param.18) | copy-start | bytes 960004
  27.6 17.5 %copy-start.3 = (f32[200,49]{0,1:T(8,128)S(1)}, f32[200,49]{0,1:T(8,128)}, u32[]{:S(2)}) copy-start(f32[200,49]{0,1:T(8,128)} %param.15) | copy-start | bytes 117604
  27.6 3.9 %collective-permute-start.2 = (bf16[8,80,640]{2,1,0:T(8,128)(2,1)S(1)}, bf16[8,80,640]{2,1,0:T(8,128)(2,1)S(1)}, u32[]{:S(2)}, u32[]{:S(2)}) collective-permute-start(bf16[8,80,640]{2,1,0:T(8,128)(2,1)S(1)} %all_to_all.15.ga_ref), channel_id=1, source_target_pairs={{0,8},{8,0},{16,24},{24,16},{32,40},{40,32},{48,56},{56,48},{64,72... | collective-permute-start | bytes 2457608 | tf_op jit(solution)/shard_map/ppermute | solution.py:405
  31.5 13.6 %copy-start.4 = (bf16[77,200]{1,0:T(8,128)(2,1)S(1)}, bf16[77,200]{1,0:T(8,128)(2,1)}, u32[]{:S(2)}) copy-start(bf16[77,200]{1,0:T(8,128)(2,1)} %sw_ref.1) | copy-start | bytes 92404
  34.9 5.3 %collective-permute-start.3 = (bf16[2,288,80]{2,1,0:T(8,128)(2,1)S(1)}, bf16[2,288,80]{2,1,0:T(8,128)(2,1)S(1)}, u32[]{:S(2)}, u32[]{:S(2)}) collective-permute-start(bf16[2,288,80]{2,1,0:T(8,128)(2,1)S(1)} %get-tuple-element.24), channel_id=1, source_target_pairs={{0,1},{1,2},{2,3},{3,4},{4,5},{5,6},{6,7},{7,0},{8,15},{9,8},{10,9... | collective-permute-start | bytes 276488 | tf_op jit(solution)/shard_map/ppermute | solution.py:426
  40.2 4.9 %collective-permute-start.4 = (bf16[2,288,80]{2,1,0:T(8,128)(2,1)S(1)}, bf16[2,288,80]{2,1,0:T(8,128)(2,1)S(1)}, u32[]{:S(2)}, u32[]{:S(2)}) collective-permute-start(bf16[2,288,80]{2,1,0:T(8,128)(2,1)S(1)} %collective-permute-done.3.near_ref), channel_id=1, source_target_pairs={{0,8},{8,0},{16,24},{24,16},{32,40},{40,32},{48,56},{56,48},{64,72... | collective-permute-start | bytes 276488 | tf_op jit(solution)/shard_map/ppermute | solution.py:427
  60.5 1.7 %collective-permute-start.5 = (bf16[64,24,128]{2,1,0:T(8,128)(2,1)S(1)}, bf16[64,24,128]{2,1,0:T(8,128)(2,1)S(1)}, u32[]{:S(2)}, u32[]{:S(2)}) collective-permute-start(bf16[64,24,128]{2,1,0:T(8,128)(2,1)S(1)} %get-tuple-element.28), channel_id=1, source_target_pairs={{0,8},{8,0},{16,24},{24,16},{32,40},{40,32},{48,56},{56,48},{64,72... | collective-permute-start | bytes 1179656 | tf_op jit(solution)/shard_map/ppermute | solution.py:463
  92.9 4.0 %collective-permute-start.6 = (bf16[64,24,128]{2,1,0:T(8,128)(2,1)S(1)}, bf16[64,24,128]{2,1,0:T(8,128)(2,1)S(1)}, u32[]{:S(2)}, u32[]{:S(2)}) collective-permute-start(bf16[64,24,128]{2,1,0:T(8,128)(2,1)S(1)} %all_to_all.17.own_ref), channel_id=1, source_target_pairs={{0,8},{8,0},{16,24},{24,16},{32,40},{40,32},{48,56},{56,48},{64,72... | collective-permute-start | bytes 1179656 | tf_op jit(solution)/shard_map/ppermute | solution.py:471
